TPU v7x, 32 devices: a whole 2x2x4 slice. The times are simulated.
32 devices in a mesh: user: 8 (over y, x, core), item: 4 (over z).
Axes of the slice: x: 2, y: 2, z: 4, core: 2. Of those that a mesh axis runs over, the one named last changes fastest.
Arguments:
- user_comps: bfloat16 [1024, 512], P(('user', 'item')), may hold values from -6 to 6
- item_text: bfloat16 [1024, 1024], P(('user', 'item')), may hold values from -6 to 6
- item_proj: bfloat16 [1024, 512], replicated, may hold values from -0.1875 to 0.1875
- w_in: float32 [64, 128], replicated, may hold values from -0.75 to 0.75
- b_in: float32 [128], replicated, may hold values from -4 to 4
- w_out: float32 [128, 64], replicated, may hold values from -1.5 to 1.5
- b_out: float32 [64], replicated, may hold values from -4 to 4
- pair_user: int32 [32768], P(('user', 'item')), may hold values from 0 to 127
- pair_item: int32 [32768], P(('user', 'item')), may hold values from 0 to 255
- teacher: float32 [32768], P(('user', 'item')), may hold values from -12 to 12
Outputs:
- user_grad: float32 [1024, 512], P(('user', 'item'))
- item_grad: float32 [1024, 512], P(('user', 'item'))
Inputs may be any that keep to these rules, and one draw needn't show every extreme that they name: `pair_user`: index of a user among the 128 users of the pair's tile. `pair_item`: index of an item among the 256 items of the pair's tile.
All inputs are finite; a program needn't handle non-finite values.
Results may differ from a plain program's by a relative error of at most 0.0058.
Values may be sent and summed in bfloat16 or wider, within the bound.
No kernel may reach another device: no remote copies, remote signals or barrier semaphores. Data moves between devices by JAX's collectives and lax.ppermute only.
A program may use at most 64 MiB of HBM per device.

v0:
```python
import math

import jax
import jax.numpy as jnp
from jax import lax
from jax.sharding import PartitionSpec as P

COMPS = 8
CDIM = 64


gate_cap = 8.0


def component_norm(values):
    mean_square = jnp.mean(values * values, axis=-1, keepdims=True)
    return values * lax.rsqrt(mean_square + 1e-06)


def project_rows(text_rows, projection):
    mixed = jnp.dot(text_rows, projection, preferred_element_type=jnp.float32)
    shaped = mixed.reshape(text_rows.shape[0], COMPS, CDIM)
    return component_norm(shaped).astype(jnp.bfloat16).reshape(text_rows.shape[0], COMPS * CDIM)


def spread_rows(onehot, values):
    upper = values.astype(jnp.bfloat16)
    lower = (values - upper.astype(jnp.float32)).astype(jnp.bfloat16)
    first = jnp.einsum("pr,pd->rd", onehot, upper, preferred_element_type=jnp.float32)
    return first + jnp.einsum("pr,pd->rd", onehot, lower, preferred_element_type=jnp.float32)


def item_terms(logit_gradient, user_portion):
    item_gradient = jnp.einsum(
        "uwx,uwz->uxz", logit_gradient, user_portion, preferred_element_type=jnp.float32
    )
    return item_gradient.reshape(item_gradient.shape[0], COMPS * CDIM)


def pair_grads(user_portion, item_portion, target, w_in, b_in, w_out, b_out, loss_scale):
    width = user_portion.shape[-1]
    reciprocal_norm = 1.0 / math.sqrt(width)
    mixture_logits = (
        jnp.einsum("xvw,xzw->xvz", user_portion, item_portion, preferred_element_type=jnp.float32)
        * reciprocal_norm
    )
    pair_count = mixture_logits.shape[0]
    flat_logits = mixture_logits.reshape(pair_count, -1)
    hidden_in = jnp.dot(flat_logits, w_in, precision=lax.Precision.HIGHEST) + b_in
    sig_pre = jax.nn.sigmoid(hidden_in)
    hidden = hidden_in * sig_pre
    gate_raw = jnp.dot(hidden, w_out, precision=lax.Precision.HIGHEST) + b_out
    capped = jnp.tanh(gate_raw / gate_cap)
    exp_gate = jnp.exp(gate_cap * capped)
    weights = exp_gate / jnp.sum(exp_gate, axis=-1, keepdims=True)
    student = jnp.sum(weights * flat_logits, axis=-1)
    residual_w = (student - target) * loss_scale
    d_gate = weights * (flat_logits - student[:, None]) * (1.0 - capped * capped)
    d_hidden = jnp.dot(d_gate, w_out.T, precision=lax.Precision.HIGHEST)
    d_pre = d_hidden * sig_pre * (1.0 + hidden_in * (1.0 - sig_pre))
    d_flat = residual_w[:, None] * (
        weights + jnp.dot(d_pre, w_in.T, precision=lax.Precision.HIGHEST)
    )
    logit_gradient = (d_flat * reciprocal_norm).astype(jnp.bfloat16).reshape(mixture_logits.shape)
    user_gradient = jnp.einsum(
        "ftz,fzr->ftr", logit_gradient, item_portion, preferred_element_type=jnp.float32
    )
    return (logit_gradient, user_gradient.reshape(pair_count, COMPS * CDIM))


def local(
    user_comps, item_text, item_proj, w_in, b_in, w_out, b_out, pair_user, pair_item, teacher
):
    user_tile = lax.all_gather(user_comps, "item", axis=0, tiled=True)
    item_tile = lax.all_gather(project_rows(item_text, item_proj), "user", axis=0, tiled=True)
    user_count = user_tile.shape[0]
    item_count = item_tile.shape[0]
    user_three = user_tile.reshape(user_count, COMPS, CDIM)
    item_three = item_tile.reshape(item_count, COMPS, CDIM)
    pair_total = pair_user.shape[0]
    block_rows = min(pair_total, 1024)
    block_total = pair_total // block_rows
    loss_scale = 2.0 * math.sqrt(user_count / (pair_total * lax.axis_size("item")))
    user_range = lax.iota(jnp.int32, user_count)
    item_range = lax.iota(jnp.int32, item_count)

    def one_block(step, carry):
        user_sum, item_sum, d_store = carry
        user_portion = jnp.take(user_three, pair_user, axis=0)
        item_portion = jnp.take(item_three, pair_item, axis=0)
        logit_gradient, user_gradient = pair_grads(
            user_portion, item_portion, teacher, w_in, b_in, w_out, b_out, loss_scale
        )
        user_onehot = (pair_user[:, None] == user_range[None, :]).astype(jnp.bfloat16)
        user_sum = user_sum + spread_rows(user_onehot, user_gradient)
        item_onehot = (pair_item[:, None] == item_range[None, :]).astype(jnp.bfloat16)
        item_sum = item_sum + spread_rows(item_onehot, item_terms(logit_gradient, user_portion))
        return (user_sum, item_sum, d_store)

    item_start = jnp.zeros((item_count, COMPS * CDIM), jnp.float32)
    store_start = jnp.zeros((1, COMPS, COMPS), jnp.bfloat16)
    start_carry = (jnp.zeros((user_count, COMPS * CDIM), jnp.float32), item_start, store_start)
    grad_users, grad_items, d_store = lax.fori_loop(0, block_total, one_block, start_carry)
    user_grad = lax.psum_scatter(grad_users, "item", scatter_dimension=0, tiled=True)
    item_grad = lax.psum_scatter(grad_items, "user", scatter_dimension=0, tiled=True)
    return (user_grad, item_grad)


def solution(mesh):
    in_specs = (
        P(("user", "item"), None),
        P(("user", "item"), None),
        P(),
        P(),
        P(),
        P(),
        P(),
        P(("user", "item")),
        P(("user", "item")),
        P(("user", "item")),
    )
    out_specs = (P(("user", "item"), None), P(("user", "item"), None))
    return jax.shard_map(local, mesh=mesh, in_specs=in_specs, out_specs=out_specs, check_vma=False)
```

profile of v0, /device:TPU:0, one launch (start us, length us, event | category | flops | bytes accessed | tf_op | source)
XLA Modules:
  0.0 142.5 jit_solution(17847967467742728318)
XLA Ops:
  7.2 0.0 copy-start
  7.2 0.0 reduce-scatter.3.cloned.1.call-start
  7.2 0.8 fusion.37
  8.0 0.7 compare_and_fusion
  8.7 0.7 fusion.38
  9.4 15.3 %all_gather.6 = bf16[128,512]{1,0:T(8,128)(2,1)S(1)} all-gather(bf16[32,512]{1,0:T(8,128)(2,1)} %param.10), channel_id=1, replica_groups=mesh['user'=8,'item'=4] {'item'}, dimensions={0}, use_global_device_ids=true | all-gather | bytes 163840 | tf_op jit(solution)/shard_map/all_gather | solution.py:74
  24.7 0.1 copy.36
  24.8 0.2 copy.37
  25.0 0.0 copy-done
  25.0 1.1 fusion.45
  26.1 0.1 mul.78
  26.2 0.1 reduce_sum.29
  26.4 0.1 mul.79
  26.5 0.1 mul.80
  26.6 9.3 %all_gather.7 = bf16[256,512]{1,0:T(8,128)(2,1)S(1)} all-gather(bf16[32,512]{1,0:T(8,128)(2,1)S(1)} %multiply_convert_fusion), channel_id=1, replica_groups=mesh['user'=8,'item'=4] {'user'}, dimensions={0}, use_global_device_ids=true | all-gather | bytes 294912 | tf_op jit(solution)/shard_map/all_gather | solution.py:75
  35.9 0.1 copy.38
  36.0 0.3 copy.39
  36.4 7.6 %gather_fusion.1 = bf16[1024,8,64]{2,1,0:T(8,128)(2,1)} fusion(bf16[256,8,64]{2,1,0:T(8,128)(2,1)S(1)} %copy.39, s32[1024]{0:T(1024)S(1)} %fusion.38), kind=kCustom, calls=%fused_computation.1 | custom fusion | bytes 2101248 | tf_op jit(solution)/shard_map/while/body/eval_jaxpr/jit(_take)/gather | solution.py:90
  44.0 3.3 %gather_fusion = bf16[1024,8,64]{2,1,0:T(8,128)(2,1)S(1)} fusion(bf16[128,8,64]{2,1,0:T(8,128)(2,1)S(1)} %copy.37, s32[1024]{0:T(1024)S(1)} %fusion.37), kind=kCustom, calls=%fused_computation | custom fusion | bytes 2101248 | tf_op jit(solution)/shard_map/while/body/eval_jaxpr/jit(_take)/gather | solution.py:89
  47.3 7.7 %convolution_multiply_fusion = f32[1024,8,8]{2,1,0:T(8,128)} fusion(bf16[1024,8,64]{2,1,0:T(8,128)(2,1)S(1)} %gather_fusion, pred[1024]{0:T(1024)(128)(4,1)S(1)} %get-tuple-element.39, bf16[1024,8,64]{2,1,0:T(8,128)(2,1)} %gather_fusion.1, pred[1024]{0:T(1024)(128)(4,1)S(1)} %get-tuple-element.38), kind=kOutput, calls=%fused_computation.2 | convolution fusion | flops 9502720 | bytes 2361344 | tf_op jit(solution)/shard_map/while/body/eval_jaxpr/xvw,xzw->xvz/dot_general | solution.py:44
  55.0 2.8 %copy.40 = f32[1024,8,8]{0,2,1:T(8,128)S(1)} copy(f32[1024,8,8]{2,1,0:T(8,128)} %convolution_multiply_fusion) | data formatting | bytes 524288 | tf_op jit(solution)/shard_map/while/body/eval_jaxpr/mul | solution.py:44
  57.8 0.0 copy-done.3
  57.9 0.0 copy-done.5
  57.9 1.0 convolution_add_fusion.1
  58.9 0.0 copy-done.6
  58.9 0.9 fusion.33
  59.8 0.1 fusion.23
  59.8 0.0 copy-start.4
  59.8 1.0 fusion.2
  60.9 0.7 fusion.8
  61.6 2.4 %copy.43 = bf16[1024,8,8]{1,2,0:T(8,128)(2,1)} copy(bf16[1024,8,8]{0,2,1:T(8,128)(2,1)S(1)} %fusion.8) | data formatting | bytes 262144 | tf_op jit(solution)/shard_map/while/body/eval_jaxpr/reshape | solution.py:64
  64.0 7.0 %fusion.11 = f32[1024,8,64]{2,1,0:T(8,128)} fusion(bf16[1024,8,8]{1,2,0:T(8,128)(2,1)} %copy.43, bf16[1024,8,64]{2,1,0:T(8,128)(2,1)} %gather_fusion.1, pred[1024]{0:T(1024)(128)(4,1)S(1)} %get-tuple-element.38), kind=kOutput, calls=%fused_computation.27 | convolution fusion | flops 8912896 | bytes 3277824 | tf_op jit(solution)/shard_map/while/body/eval_jaxpr/ftz,fzr->ftr/dot_general | solution.py:65
  71.0 3.8 %copy.42 = f32[1024,8,64]{0,2,1:T(8,128)} copy(f32[1024,8,64]{2,1,0:T(8,128)} %fusion.11) | data formatting | bytes 4194304 | tf_op jit(solution)/shard_map/while/body/eval_jaxpr/ftz,fzr->ftr/dot_general | solution.py:65
  74.9 2.0 %fusion.1 = (bf16[1024,512]{0,1:T(8,128)(2,1)S(1)}, bf16[1024,512]{0,1:T(8,128)(2,1)S(1)}) fusion(f32[1024,8,64]{0,2,1:T(8,128)} %copy.42), kind=kLoop, calls=%fused_computation.8 | loop fusion | flops 2097152 | bytes 4194304 | tf_op jit(solution)/shard_map/while/body/eval_jaxpr/convert_element_type | solution.py:28
  76.9 0.7 fusion.20
  77.6 1.4 %convolution_add_fusion.4 = f32[128,512]{1,0:T(8,128)} fusion(f32[128,512]{1,0:T(8,128)S(1)} %fusion.20, bf16[1024,512]{0,1:T(8,128)(2,1)S(1)} %get-tuple-element.32, s32[1024]{0:T(1024)S(1)} %copy-done.1), kind=kOutput, calls=%fused_computation.21 | convolution fusion | flops 134545408 | bytes 1576960 | tf_op jit(solution)/shard_map/while/body/eval_jaxpr/pr,pd->rd/dot_general | solution.py:30
  79.0 0.0 reduce-scatter.3.cloned.1.call-update
  79.1 0.2 reduce-scatter.5.cloned.1.call-start
  79.3 6.4 %fusion.10 = f32[1024,8,64]{2,1,0:T(8,128)} fusion(bf16[1024,8,8]{1,2,0:T(8,128)(2,1)} %copy.43, bf16[1024,8,64]{2,1,0:T(8,128)(2,1)S(1)} %gather_fusion, pred[1024]{0:T(1024)(128)(4,1)S(1)} %get-tuple-element.39), kind=kOutput, calls=%fused_computation.26 | convolution fusion | flops 8912896 | bytes 3277824 | tf_op jit(solution)/shard_map/while/body/eval_jaxpr/uwx,uwz->uxz/dot_general | solution.py:34
  85.7 2.8 %copy.44 = f32[1024,8,64]{0,2,1:T(8,128)S(1)} copy(f32[1024,8,64]{2,1,0:T(8,128)} %fusion.10) | data formatting | bytes 4194304 | tf_op jit(solution)/shard_map/while/body/eval_jaxpr/uwx,uwz->uxz/dot_general | solution.py:34
  88.5 0.0 copy-start.2
  88.5 0.3 fusion
  88.9 0.4 copy-done.2
  89.2 0.7 fusion.13
  90.0 1.5 %convolution_add_fusion = f32[256,512]{1,0:T(8,128)} fusion(f32[256,512]{1,0:T(8,128)S(1)} %fusion.13, bf16[1024,512]{0,1:T(8,128)(2,1)S(1)} %get-tuple-element.30, s32[1024]{0:T(1024)S(1)} %copy-done.2), kind=kOutput, calls=%fused_computation.11 | convolution fusion | flops 269090816 | bytes 2101248 | tf_op jit(solution)/shard_map/while/body/eval_jaxpr/pr,pd->rd/dot_general | solution.py:30
  91.5 0.0 reduce-scatter.5.cloned.1.call-update
  91.5 8.1 %reduce-scatter.3.cloned.1.call-done = f32[32,512]{1,0:T(8,128)} async-done(((f32[128,512]{1,0:T(8,128)}), f32[32,512]{1,0:T(8,128)}) %reduce-scatter.3.cloned.1.call-update) | async-done | bytes 65552 | tf_op jit(solution)/shard_map/reduce_scatter | solution.py:104
  99.6 36.0 %reduce-scatter.5.cloned.1.call-done = f32[32,512]{1,0:T(8,128)} async-done(((f32[256,512]{1,0:T(8,128)}), f32[32,512]{1,0:T(8,128)}) %reduce-scatter.5.cloned.1.call-update) | async-done | bytes 65552 | tf_op jit(solution)/shard_map/reduce_scatter | solution.py:105
  (11 shorter events, 0.0 us)
Async XLA Ops:
  7.2 17.9 %copy-start = (bf16[1024,512]{1,0:T(8,128)(2,1)S(1)}, bf16[1024,512]{1,0:T(8,128)(2,1)}, u32[]{:S(2)}) copy-start(bf16[1024,512]{1,0:T(8,128)(2,1)} %param.12) | copy-start | bytes 3145732
  7.2 92.4 %reduce-scatter.3.cloned.1.call-start = ((), (), s32[]{:S(2)}) async-start(), calls=%async_computation.2 | async-start | bytes 327680 | tf_op jit(solution)/shard_map/reduce_scatter | solution.py:104
  55.0 2.9 %copy-start.3 = (f32[64,128]{1,0:T(8,128)S(1)}, f32[64,128]{1,0:T(8,128)}, u32[]{:S(2)}) copy-start(f32[64,128]{1,0:T(8,128)} %param.13) | copy-start | bytes 98308
  55.0 2.9 %copy-start.5 = (f32[128]{0:T(128)S(1)}, f32[128]{0:T(128)}, u32[]{:S(2)}) copy-start(f32[128]{0:T(128)} %param.14) | copy-start | bytes 1540
  55.0 3.9 %copy-start.6 = (f32[128,64]{0,1:T(8,128)S(1)}, f32[128,64]{0,1:T(8,128)}, u32[]{:S(2)}) copy-start(f32[128,64]{0,1:T(8,128)} %param.15) | copy-start | bytes 98308
  55.0 3.9 %copy-start.7 = (f32[64]{0:T(128)S(1)}, f32[64]{0:T(128)}, u32[]{:S(2)}) copy-start(f32[64]{0:T(128)} %param.16) | copy-start | bytes 772
  59.8 1.0 copy-start.4
  74.9 2.0 %copy-start.1 = (s32[1024]{0:T(1024)S(1)}, s32[1024]{0:T(1024)}, u32[]{:S(2)}) copy-start(s32[1024]{0:T(1024)} %param.17) | copy-start | bytes 12292
  79.1 56.6 %reduce-scatter.5.cloned.1.call-start = ((), (), s32[]{:S(2)}) async-start(), calls=%async_computation.3 | async-start | bytes 589824 | tf_op jit(solution)/shard_map/reduce_scatter | solution.py:105
  88.5 0.7 copy-start.2
Sparse Core Ops, SparseCore 0:
  79.2 20.3 reduce-scatter.2
  103.3 32.3 reduce-scatter.4
where the time goes:
time: 143 us; the launch traced here: 142 us
  waiting for transfers between devices  44.2 us (31%)
  matrix products  30.2 us (21%)
  blocking collectives  24.6 us (17%)
  local copies, waits for them, and re-layouts  24.3 us (17%)
  between operations  14.3 us (10%)
  other arithmetic  4.67 us (3%)
    reduce_scatter x1, waiting for transfers between devices, local(): lax.psum_scatter(grad_items, 'user', scatter_dimension=0, tiled=True)  36 us
    all_gather x1, blocking collectives, local(): user_tile = lax.all_gather(user_comps, 'item', axis=0, tiled=True)  15.3 us
    all_gather x1, blocking collectives, local(): lax.all_gather(project_rows(item_text, item_proj), 'user', axis=0, tiled=...  9.31 us
    reduce_scatter x1, waiting for transfers between devices, local(): lax.psum_scatter(grad_users, 'item', scatter_dimension=0, tiled=True)  8.1 us
    dot_general x1, matrix products, pair_grads(): jnp.einsum('xvw,xzw->xvz', user_portion, item_portion, preferred_element_...  7.69 us
    gather x1, local copies, waits for them, and re-layouts, one_block(): item_portion = jnp.take(item_three, pair_item, axis=0)  7.63 us
    dot_general x1, matrix products, pair_grads(): jnp.einsum('ftz,fzr->ftr', logit_gradient, item_portion, preferred_elemen...  7.01 us
    dot_general x1, matrix products, item_terms(): jnp.einsum('uwx,uwz->uxz', logit_gradient, user_portion, preferred_elemen...  6.39 us
  transfers between devices with their start and end apart: 2, of which 2 were waited for; matrix products, arithmetic and copies ran while one was open for 8% of the time, Pallas kernels for 0%

commit v1 on v0

v1 whole, which is shorter than its diff:
```python
import functools
import math

import jax
import jax.numpy as jnp
from jax import lax
from jax.experimental import pallas as pl
from jax.experimental.pallas import tpu as pltpu
from jax.sharding import PartitionSpec as P

COMPS = 8
CDIM = 64
gate_cap = 8.0
F32 = jnp.float32
BF16 = jnp.bfloat16
VMEM = pl.BlockSpec(memory_space=pltpu.VMEM)


def bits_of(size):
    return size.bit_length() - 1


def exchange(value, axis, step):
    size = lax.axis_size(axis)
    return lax.ppermute(value, axis, [(i, i ^ step) for i in range(size)])


def round_steps(size):
    steps = [1 << bit for bit in range(1, bits_of(size))]
    return steps + ([1] if size > 1 else [])


def place_of(block, me, size):
    apart = block ^ me
    if size < 4:
        return apart
    return (apart >> 1) | ((apart & 1) << (bits_of(size) - 1))


def gather_rows(value, axis):
    for step in round_steps(lax.axis_size(axis)):
        value = jnp.concatenate([value, exchange(value, axis, step)], axis=0)
    return value


def scatter_rows(keep, send, axis):
    steps = round_steps(lax.axis_size(axis))[::-1]
    for at, step in enumerate(steps):
        total = keep + exchange(send, axis, step).astype(F32)
        if at + 1 < len(steps):
            half = total.shape[0] // 2
            keep, send = total[:half], total[half:].astype(BF16)
    return total


def project_kernel(text_ref, proj_ref, out_ref):
    mixed = jnp.dot(text_ref[...], proj_ref[...], preferred_element_type=F32)
    parts = []
    for at in range(COMPS):
        part = mixed[:, at * CDIM : (at + 1) * CDIM]
        square = jnp.mean(part * part, axis=-1, keepdims=True)
        parts.append(part * lax.rsqrt(square + 1e-06))
    out_ref[...] = jnp.concatenate(parts, axis=1).astype(BF16)


def project_rows(text, proj):
    return pl.pallas_call(
        project_kernel,
        out_shape=jax.ShapeDtypeStruct((text.shape[0], proj.shape[1]), BF16),
        in_specs=[VMEM, VMEM],
        out_specs=VMEM,
        compiler_params=pltpu.CompilerParams(vmem_limit_bytes=8 << 20),
        name="project",
    )(text, proj)


def halves(value):
    upper = value.astype(BF16)
    return upper, (value - upper.astype(F32)).astype(BF16)


def weight_stack(weight, axis):
    upper, lower = halves(weight)
    return jnp.concatenate([upper, lower, upper], axis=axis)


def value_stack(value, bias):
    upper, lower = halves(value)
    pieces = [upper, upper, lower]
    if bias:
        pieces.append(jnp.ones((16, value.shape[1]), BF16))
    return jnp.concatenate(pieces, axis=0)


def bias_rows(bias):
    upper, rest = bias.astype(BF16), bias
    rows = [upper]
    for _ in range(2):
        rest = rest - upper.astype(F32)
        upper = rest.astype(BF16)
        rows.append(upper)
    rows.append(jnp.zeros((13, bias.shape[1]), BF16))
    return jnp.concatenate([r.astype(F32) for r in rows], axis=0).astype(BF16)


def fold_rows(parts):
    place = lax.broadcasted_iota(jnp.int32, parts[0].shape, 0)
    width = 4
    while len(parts) > 1:
        low = (place & width) == 0
        half = len(parts) // 2
        merged = []
        for at in range(half):
            one, two = parts[at], parts[at + half]
            stay = jnp.where(low, one, two)
            move = jnp.where(low, two, one)
            merged.append(stay + pltpu.roll(move, width, 0) if width == 4 else stay + shift_rows(move, width, low))
        parts = merged
        width //= 2
    return parts[0]


def shift_rows(value, width, low):
    return jnp.where(low, pltpu.roll(value, 8 - width, 0), pltpu.roll(value, width, 0))


def pair_kernel(
    sizes,
    loss_scale,
    users_ref,
    items_ref,
    w_in_ref,
    b_in_ref,
    w_out_ref,
    b_out_ref,
    pair_user_ref,
    pair_item_ref,
    teacher_ref,
    user_keep_ref,
    user_send_ref,
    item_keep_ref,
    item_send_ref,
    user_hot,
    item_hot,
    user_pairs,
    item_pairs,
    logits_ref,
    grad_ref,
    user_terms,
    item_terms,
):
    n_user, n_item = sizes
    user_rows, item_rows = users_ref.shape[0], items_ref.shape[0]
    pairs = pair_user_ref.shape[1]
    me_user, me_item = lax.axis_index("user"), lax.axis_index("item")
    gates = COMPS * COMPS
    wide = 256
    tile = 128
    scale = 1.0 / math.sqrt(CDIM)

    def spots(index, rows, size, me):
        each = rows // size
        return place_of(index // each, me, size) * each + index % each

    users_t = users_ref[...].T
    items_t = items_ref[...].T
    w_in, w_out = w_in_ref[...], w_out_ref[...]
    w_in_fwd = jnp.concatenate([weight_stack(w_in, 0), bias_rows(b_in_ref[...])], axis=0).T
    w_out_fwd = jnp.concatenate([weight_stack(w_out, 0), bias_rows(b_out_ref[...])], axis=0).T
    w_in_bwd = weight_stack(w_in, 1)
    w_out_bwd = weight_stack(w_out, 1)

    def dot(one, two):
        return jnp.dot(one, two, preferred_element_type=F32)

    for block in range(pairs // wide):
        lanes = slice(block * wide, (block + 1) * wide)
        user_at = spots(pair_user_ref[:, lanes], user_rows, n_item, me_item)
        item_at = spots(pair_item_ref[:, lanes], item_rows, n_user, me_user)
        hot = lax.broadcasted_iota(jnp.int32, (user_rows, wide), 0) == user_at
        user_hot[:, lanes] = jnp.where(hot, 1.0, 0.0).astype(BF16)
        hot = lax.broadcasted_iota(jnp.int32, (item_rows, wide), 0) == item_at
        item_hot[:, lanes] = jnp.where(hot, 1.0, 0.0).astype(BF16)
        user_pairs[:, lanes] = dot(users_t, user_hot[:, lanes])
        item_pairs[:, lanes] = dot(items_t, item_hot[:, lanes])

        for sub in range(wide // tile):
            span = slice(block * wide + sub * tile, block * wide + (sub + 1) * tile)
            for c in range(COMPS):
                parts = []
                for k in range(COMPS):
                    total = None
                    for j in range(CDIM // 8):
                        u = user_pairs[c * CDIM + j * 8 : c * CDIM + (j + 1) * 8, span]
                        v = item_pairs[k * CDIM + j * 8 : k * CDIM + (j + 1) * 8, span]
                        total = u * v if total is None else total + u * v
                    parts.append(total)
                logits_ref[c * COMPS : (c + 1) * COMPS, span] = fold_rows(parts) * scale

        logits = logits_ref[:, lanes]
        pre = dot(w_in_fwd, value_stack(logits, True))
        sig = jax.nn.sigmoid(pre)
        hidden = pre * sig
        raw = dot(w_out_fwd, value_stack(hidden, True))
        capped = jnp.tanh(raw * (1.0 / gate_cap))
        powers = jnp.exp(gate_cap * capped)
        weights = powers * (1.0 / jnp.sum(powers, axis=0, keepdims=True))
        student = jnp.sum(weights * logits, axis=0, keepdims=True)
        residual = (student - teacher_ref[:, lanes]) * loss_scale
        d_gate = weights * (logits - student) * (1.0 - capped * capped)
        d_hidden = dot(w_out_bwd, value_stack(d_gate, False))
        d_pre = d_hidden * sig * (1.0 + pre * (1.0 - sig))
        d_flat = residual * (weights + dot(w_in_bwd, value_stack(d_pre, False)))
        grad_ref[:, lanes] = (d_flat * scale).astype(BF16).astype(F32)

        for sub in range(wide // tile):
            span = slice(block * wide + sub * tile, block * wide + (sub + 1) * tile)
            for terms, pairs_ref, row in (
                (user_terms, item_pairs, lambda c, k: c * COMPS + k),
                (item_terms, user_pairs, lambda k, c: c * COMPS + k),
            ):
                for one in range(COMPS):
                    spread = [
                        jnp.broadcast_to(grad_ref[row(one, two) : row(one, two) + 1, span], (16, tile))
                        for two in range(COMPS)
                    ]
                    for j in range(CDIM // 16):
                        total = None
                        for two in range(COMPS):
                            at = two * CDIM + j * 16
                            term = spread[two] * pairs_ref[at : at + 16, span]
                            total = term if total is None else total + term
                        at = one * CDIM + j * 16
                        terms[at : at + 16, span] = total.astype(BF16)

    def collect(hot, terms, keep_ref, send_ref):
        total = lax.dot_general(
            hot[...], terms[...], (((1,), (1,)), ((), ())), preferred_element_type=F32
        )
        half = total.shape[0] // 2
        keep_ref[...] = total[:half]
        send_ref[...] = total[half:].astype(BF16)

    collect(user_hot, user_terms, user_keep_ref, user_send_ref)
    collect(item_hot, item_terms, item_keep_ref, item_send_ref)


def pair_terms(users, items, w_in, b_in, w_out, b_out, pair_user, pair_item, teacher, sizes, loss_scale):
    pairs = pair_user.shape[0]
    user_rows, item_rows = users.shape[0], items.shape[0]
    width = COMPS * CDIM

    def out(rows):
        return [
            jax.ShapeDtypeStruct((rows // 2, width), F32),
            jax.ShapeDtypeStruct((rows // 2, width), BF16),
        ]

    return pl.pallas_call(
        functools.partial(pair_kernel, sizes, loss_scale),
        out_shape=out(user_rows) + out(item_rows),
        in_specs=[VMEM] * 9,
        out_specs=[VMEM] * 4,
        scratch_shapes=[
            pltpu.VMEM((user_rows, pairs), BF16),
            pltpu.VMEM((item_rows, pairs), BF16),
            pltpu.VMEM((width, pairs), F32),
            pltpu.VMEM((width, pairs), F32),
            pltpu.VMEM((COMPS * COMPS, pairs), F32),
            pltpu.VMEM((COMPS * COMPS, pairs), F32),
            pltpu.VMEM((width, pairs), BF16),
            pltpu.VMEM((width, pairs), BF16),
        ],
        compiler_params=pltpu.CompilerParams(vmem_limit_bytes=24 << 20),
        name="pairs",
    )(
        users,
        items,
        w_in,
        b_in.reshape(1, -1),
        w_out,
        b_out.reshape(1, -1),
        pair_user.reshape(1, -1),
        pair_item.reshape(1, -1),
        teacher.reshape(1, -1),
    )


def local(user_comps, item_text, item_proj, w_in, b_in, w_out, b_out, pair_user, pair_item, teacher):
    n_user, n_item = lax.axis_size("user"), lax.axis_size("item")
    users = gather_rows(user_comps, "item")
    items = gather_rows(project_rows(item_text, item_proj), "user")
    loss_scale = 2.0 * math.sqrt(users.shape[0] / (pair_user.shape[0] * n_item))
    user_keep, user_send, item_keep, item_send = pair_terms(
        users, items, w_in, b_in, w_out, b_out, pair_user, pair_item, teacher, (n_user, n_item), loss_scale
    )
    return scatter_rows(user_keep, user_send, "item"), scatter_rows(item_keep, item_send, "user")


def solution(mesh):
    split = P(("user", "item"))
    rows = P(("user", "item"), None)
    in_specs = (rows, rows, P(), P(), P(), P(), P(), split, split, split)
    return jax.shard_map(local, mesh=mesh, in_specs=in_specs, out_specs=(rows, rows), check_vma=False)
```

time: 143 us -> 35 us (0.24)
  waiting for transfers between devices: 44.2 us -> 7.06 us
  matrix products: 30.2 us -> 0 us
  blocking collectives: 24.6 us -> 0 us
  local copies, waits for them, and re-layouts: 24.3 us -> 2.87 us
  starting transfers between devices: 0.26 us -> 15.6 us
  between operations: 14.3 us -> 0.81 us
  Pallas kernels: 0 us -> 7.06 us
  other arithmetic: 4.67 us -> 1.38 us
    reduce_scatter x2 -> x0, waiting for transfers between devices: 44.1 us -> none  [the longest x1 36 us: local(): lax.psum_scatter(grad_items, 'user', scatter_dimension=0, tiled=True)]
    dot_general x12 -> x0, matrix products: 30.2 us -> none  [the longest x1 7.69 us: pair_grads(): jnp.einsum('xvw,xzw->xvz', user_portion, item_portion, preferred_element_...]
    all_gather x2 -> x0, blocking collectives: 24.6 us -> none  [the longest x1 15.3 us: local(): user_tile = lax.all_gather(user_comps, 'item', axis=0, tiled=True)]
    ppermute x0 -> x10, starting transfers between devices: none -> 15.6 us  [exchange(): return lax.ppermute(value, axis, [(i, i ^ step) for i in range(size)])]
    gather x2 -> x0, local copies, waits for them, and re-layouts: 10.9 us -> none  [the longest x1 7.63 us: one_block(): item_portion = jnp.take(item_three, pair_item, axis=0)]
    pallas_call x0 -> x2, Pallas kernels: none -> 7.06 us  [the longest x1 6.55 us: pair_terms(): pl.pallas_call(functools.partial(pair_kernel, sizes, loss_scale), out_sha...]
    ppermute x0 -> x10, waiting for transfers between devices: none -> 7.06 us  [exchange(): return lax.ppermute(value, axis, [(i, i ^ step) for i in range(size)])]
    dot_general x2 -> x0, local copies, waits for them, and re-layouts: 6.68 us -> none  [the longest x1 3.85 us: pair_grads(): jnp.einsum('ftz,fzr->ftr', logit_gradient, item_portion, preferred_elemen...]
  transfers between devices with their start and end apart: 2 -> 10, of which waited for: 2 -> 6; matrix products, arithmetic and copies ran while one was open for 8% -> 2% of each run, Pallas kernels for 0% -> 0%
where the time goes in v1:
time: 35 us; the launch traced here: 34.7 us
  starting transfers between devices  15.6 us (45%)
  Pallas kernels  7.06 us (20%)
  waiting for transfers between devices  7.06 us (20%)
  local copies, waits for them, and re-layouts  2.87 us (8%)
  other arithmetic  1.38 us (4%)
  between operations  0.81 us (2%)
    ppermute x10, starting transfers between devices, exchange(): return lax.ppermute(value, axis, [(i, i ^ step) for i in range(size)])  15.6 us
    ppermute x10, waiting for transfers between devices, exchange(): return lax.ppermute(value, axis, [(i, i ^ step) for i in range(size)])  7.06 us
    pallas_call x1, Pallas kernels, pair_terms(): pl.pallas_call(functools.partial(pair_kernel, sizes, loss_scale), out_sha...  6.55 us
    unnamed x21, local copies, waits for them, and re-layouts  2.84 us
    add x5, other arithmetic, scatter_rows(): total = keep + exchange(send, axis, step).astype(F32)  1.33 us
  transfers between devices with their start and end apart: 10, of which 6 were waited for; matrix products, arithmetic and copies ran while one was open for 2% of the time, Pallas kernels for 0%

profile of v1, /device:TPU:0, one launch (start us, length us, event | category | flops | bytes accessed | tf_op | source)
XLA Modules:
  0.0 34.7 jit_solution(3596075447815141842)
XLA Ops:
  0.6 0.0 copy-start
  0.6 1.2 %copy-done = bf16[1024,512]{1,0:T(8,128)(2,1)S(1)} copy-done((bf16[1024,512]{1,0:T(8,128)(2,1)S(1)}, bf16[1024,512]{1,0:T(8,128)(2,1)}, u32[]{:S(2)}) %copy-start) | copy-done | bytes 1048600
  1.9 0.0 copy-start.1
  1.9 0.8 %copy-done.1 = bf16[32,1024]{1,0:T(8,128)(2,1)S(1)} copy-done((bf16[32,1024]{1,0:T(8,128)(2,1)S(1)}, bf16[32,1024]{1,0:T(8,128)(2,1)}, u32[]{:S(2)}) %copy-start.1) | copy-done | bytes 65560
  2.7 0.0 copy-start.8
  2.7 0.5 %project.1 = bf16[32,512]{1,0:T(8,128)(2,1)S(1)} custom-call(bf16[32,1024]{1,0:T(8,128)(2,1)S(1)} %copy-done.1, bf16[1024,512]{1,0:T(8,128)(2,1)S(1)} %copy-done), custom_call_target="tpu_custom_call" | custom-call | tf_op jit(solution)/shard_map/project/pallas_call | solution.py:67
  3.2 3.0 %collective-permute-start.2 = (bf16[32,512]{1,0:T(8,128)(2,1)S(1)}, bf16[32,512]{1,0:T(8,128)(2,1)S(1)}, u32[]{:S(2)}, u32[]{:S(2)}) collective-permute-start(bf16[32,512]{1,0:T(8,128)(2,1)S(1)} %project.1), channel_id=1, source_target_pairs={{0,8},{4,12},{8,0},{12,4},{16,24},{20,28},{24,16},{28,20},{1,9},{5... | collective-permute-start | bytes 98312 | tf_op jit(solution)/shard_map/ppermute | solution.py:25
  6.2 0.0 copy-done.8
  6.2 2.6 %collective-permute-start = (bf16[32,512]{1,0:T(8,128)(2,1)S(1)}, bf16[32,512]{1,0:T(8,128)(2,1)S(1)}, u32[]{:S(2)}, u32[]{:S(2)}) collective-permute-start(bf16[32,512]{1,0:T(8,128)(2,1)S(1)} %copy-done.8), channel_id=1, source_target_pairs={{0,2},{1,3},{2,0},{3,1},{4,6},{5,7},{6,4},{7,5},{8,10},{9,11},{10,... | collective-permute-start | bytes 98312 | tf_op jit(solution)/shard_map/ppermute | solution.py:25
  8.8 0.0 collective-permute-done.2
  8.8 1.6 %collective-permute-start.3 = (bf16[64,512]{1,0:T(8,128)(2,1)S(1)}, bf16[64,512]{1,0:T(8,128)(2,1)S(1)}, u32[]{:S(2)}, u32[]{:S(2)}) collective-permute-start(bf16[64,512]{1,0:T(8,128)(2,1)S(1)} %pad_maximum_fusion.4), channel_id=1, source_target_pairs={{0,16},{4,20},{8,24},{12,28},{16,0},{20,4},{24,8},{28,12},{1,17},{... | collective-permute-start | bytes 196616 | tf_op jit(solution)/shard_map/ppermute | solution.py:25
  10.4 0.6 %collective-permute-done = bf16[32,512]{1,0:T(8,128)(2,1)S(1)} collective-permute-done((bf16[32,512]{1,0:T(8,128)(2,1)S(1)}, bf16[32,512]{1,0:T(8,128)(2,1)S(1)}, u32[]{:S(2)}, u32[]{:S(2)}) %collective-permute-start) | collective-permute-done | bytes 32800 | tf_op jit(solution)/shard_map/ppermute | solution.py:25
  11.1 0.0 copy-start.9
  11.1 1.6 %collective-permute-start.1 = (bf16[64,512]{1,0:T(8,128)(2,1)S(1)}, bf16[64,512]{1,0:T(8,128)(2,1)S(1)}, u32[]{:S(2)}, u32[]{:S(2)}) collective-permute-start(bf16[64,512]{1,0:T(8,128)(2,1)S(1)} %pad_maximum_fusion.3), channel_id=1, source_target_pairs={{0,1},{1,0},{2,3},{3,2},{4,5},{5,4},{6,7},{7,6},{8,9},{9,8},{10,11... | collective-permute-start | bytes 196616 | tf_op jit(solution)/shard_map/ppermute | solution.py:25
  12.7 0.5 %collective-permute-done.3 = bf16[64,512]{1,0:T(8,128)(2,1)S(1)} collective-permute-done((bf16[64,512]{1,0:T(8,128)(2,1)S(1)}, bf16[64,512]{1,0:T(8,128)(2,1)S(1)}, u32[]{:S(2)}, u32[]{:S(2)}) %collective-permute-start.3) | collective-permute-done | bytes 65568 | tf_op jit(solution)/shard_map/ppermute | solution.py:25
  13.2 0.1 collective-permute-start.4
  13.3 0.0 copy-done.9
  13.3 0.1 copy.12.w_out_ref
  13.4 2.0 %collective-permute-done.1 = bf16[64,512]{1,0:T(8,128)(2,1)S(1)} collective-permute-done((bf16[64,512]{1,0:T(8,128)(2,1)S(1)}, bf16[64,512]{1,0:T(8,128)(2,1)S(1)}, u32[]{:S(2)}, u32[]{:S(2)}) %collective-permute-start.1) | collective-permute-done | bytes 65568 | tf_op jit(solution)/shard_map/ppermute | solution.py:25
  15.4 0.0 copy-start.2
  15.4 0.0 collective-permute-done.4
  15.4 0.0 copy-start.5
  15.5 0.0 copy-start.4
  15.5 0.0 copy-start.3
  15.5 0.0 copy-start.6
  15.5 0.0 copy-start.7
  15.5 0.7 %copy-done.2 = f32[64,128]{1,0:T(8,128)S(1)} copy-done((f32[64,128]{1,0:T(8,128)S(1)}, f32[64,128]{1,0:T(8,128)}, u32[]{:S(2)}) %copy-start.2) | copy-done | bytes 32792
  16.2 0.0 copy-done.5
  16.2 0.0 copy-done.4
  16.2 0.0 copy-done.3
  16.2 0.0 copy-done.6
  16.2 0.0 copy-done.7
  16.2 6.5 %pairs.1 = (f32[64,512]{1,0:T(8,128)S(1)}, bf16[64,512]{1,0:T(8,128)(2,1)S(1)}, f32[128,512]{1,0:T(8,128)S(1)}, bf16[128,512]{1,0:T(8,128)(2,1)S(1)}) custom-call(bf16[128,512]{1,0:T(8,128)(2,1)S(1)} %pad_maximum_fusion.1.users_ref, bf16[256,512]{1,0:T(8,128)(2,1)S(1)} %pad_maximum_fusion.items_ref, f32[64,128]{1,0:T(8,128)S(1)} %copy-done.2, ...), custom_call_target="tpu_custom_call" | custom-call | tf_op jit(solution)/shard_map/pairs/pallas_call | solution.py:259
  22.7 0.1 collective-permute-start.7
  22.8 1.6 %collective-permute-start.5 = (bf16[64,512]{1,0:T(8,128)(2,1)S(1)}, bf16[64,512]{1,0:T(8,128)(2,1)S(1)}, u32[]{:S(2)}, u32[]{:S(2)}) collective-permute-start(bf16[64,512]{1,0:T(8,128)(2,1)S(1)} %get-tuple-element.7), channel_id=1, source_target_pairs={{0,1},{1,0},{2,3},{3,2},{4,5},{5,4},{6,7},{7,6},{8,9},{9,8},{10,11... | collective-permute-start | bytes 196616 | tf_op jit(solution)/shard_map/ppermute | solution.py:25
  24.5 0.0 collective-permute-done.7
  24.5 1.6 %collective-permute-start.8 = (bf16[64,512]{1,0:T(8,128)(2,1)S(1)}, bf16[64,512]{1,0:T(8,128)(2,1)S(1)}, u32[]{:S(2)}, u32[]{:S(2)}) collective-permute-start(bf16[64,512]{1,0:T(8,128)(2,1)S(1)} %slice.39), channel_id=1, source_target_pairs={{0,16},{4,20},{8,24},{12,28},{16,0},{20,4},{24,8},{28,12},{1,17},{... | collective-permute-start | bytes 196616 | tf_op jit(solution)/shard_map/ppermute | solution.py:25
  26.1 1.2 %collective-permute-done.5 = bf16[64,512]{1,0:T(8,128)(2,1)S(1)} collective-permute-done((bf16[64,512]{1,0:T(8,128)(2,1)S(1)}, bf16[64,512]{1,0:T(8,128)(2,1)S(1)}, u32[]{:S(2)}, u32[]{:S(2)}) %collective-permute-start.5) | collective-permute-done | bytes 65568 | tf_op jit(solution)/shard_map/ppermute | solution.py:25
  27.4 2.7 %collective-permute-start.6 = (bf16[32,512]{1,0:T(8,128)(2,1)S(1)}, bf16[32,512]{1,0:T(8,128)(2,1)S(1)}, u32[]{:S(2)}, u32[]{:S(2)}) collective-permute-start(bf16[32,512]{1,0:T(8,128)(2,1)S(1)} %slice.41), channel_id=1, source_target_pairs={{0,2},{1,3},{2,0},{3,1},{4,6},{5,7},{6,4},{7,5},{8,10},{9,11},{10,... | collective-permute-start | bytes 98312 | tf_op jit(solution)/shard_map/ppermute | solution.py:25
  30.1 0.0 collective-permute-done.8
  30.1 0.6 %collective-permute-start.9 = (bf16[32,512]{1,0:T(8,128)(2,1)S(1)}, bf16[32,512]{1,0:T(8,128)(2,1)S(1)}, u32[]{:S(2)}, u32[]{:S(2)}) collective-permute-start(bf16[32,512]{1,0:T(8,128)(2,1)S(1)} %slice.40), channel_id=1, source_target_pairs={{0,8},{4,12},{8,0},{12,4},{16,24},{20,28},{24,16},{28,20},{1,9},{5... | collective-permute-start | bytes 98312 | tf_op jit(solution)/shard_map/ppermute | solution.py:25
  30.7 1.6 %collective-permute-done.6 = bf16[32,512]{1,0:T(8,128)(2,1)S(1)} collective-permute-done((bf16[32,512]{1,0:T(8,128)(2,1)S(1)}, bf16[32,512]{1,0:T(8,128)(2,1)S(1)}, u32[]{:S(2)}, u32[]{:S(2)}) %collective-permute-start.6) | collective-permute-done | bytes 32800 | tf_op jit(solution)/shard_map/ppermute | solution.py:25
  32.4 0.6 %slice_add_fusion.2 = f32[32,512]{1,0:T(8,128)} fusion(f32[64,512]{1,0:T(8,128)S(1)} %convert_add_fusion.1, bf16[32,512]{1,0:T(8,128)(2,1)S(1)} %collective-permute-done.6), kind=kLoop, calls=%fused_computation.10 | loop fusion | flops 32768 | bytes 163840 | tf_op jit(solution)/shard_map/add | solution.py:49
  33.0 1.1 %collective-permute-done.9 = bf16[32,512]{1,0:T(8,128)(2,1)S(1)} collective-permute-done((bf16[32,512]{1,0:T(8,128)(2,1)S(1)}, bf16[32,512]{1,0:T(8,128)(2,1)S(1)}, u32[]{:S(2)}, u32[]{:S(2)}) %collective-permute-start.9) | collective-permute-done | bytes 32800 | tf_op jit(solution)/shard_map/ppermute | solution.py:25
  34.1 0.6 %slice_add_fusion.1 = f32[32,512]{1,0:T(8,128)} fusion(f32[64,512]{1,0:T(8,128)S(1)} %slice_add_fusion, bf16[32,512]{1,0:T(8,128)(2,1)S(1)} %collective-permute-done.9), kind=kLoop, calls=%fused_computation.8 | loop fusion | flops 32768 | bytes 163840 | tf_op jit(solution)/shard_map/add | solution.py:49
  (11 shorter events, 0.1 us)
Async XLA Ops:
  0.6 1.2 %copy-start = (bf16[1024,512]{1,0:T(8,128)(2,1)S(1)}, bf16[1024,512]{1,0:T(8,128)(2,1)}, u32[]{:S(2)}) copy-start(bf16[1024,512]{1,0:T(8,128)(2,1)} %proj_ref.1) | copy-start | bytes 3145732
  1.9 0.8 %copy-start.1 = (bf16[32,1024]{1,0:T(8,128)(2,1)S(1)}, bf16[32,1024]{1,0:T(8,128)(2,1)}, u32[]{:S(2)}) copy-start(bf16[32,1024]{1,0:T(8,128)(2,1)} %text_ref.1) | copy-start | bytes 196612
  2.7 3.5 %copy-start.8 = (bf16[32,512]{1,0:T(8,128)(2,1)S(1)}, bf16[32,512]{1,0:T(8,128)(2,1)}, u32[]{:S(2)}) copy-start(bf16[32,512]{1,0:T(8,128)(2,1)} %param.10) | copy-start | bytes 98308
  3.2 5.6 %collective-permute-start.2 = (bf16[32,512]{1,0:T(8,128)(2,1)S(1)}, bf16[32,512]{1,0:T(8,128)(2,1)S(1)}, u32[]{:S(2)}, u32[]{:S(2)}) collective-permute-start(bf16[32,512]{1,0:T(8,128)(2,1)S(1)} %project.1), channel_id=1, source_target_pairs={{0,8},{4,12},{8,0},{12,4},{16,24},{20,28},{24,16},{28,20},{1,9},{5... | collective-permute-start | bytes 98312 | tf_op jit(solution)/shard_map/ppermute | solution.py:25
  6.2 4.8 %collective-permute-start = (bf16[32,512]{1,0:T(8,128)(2,1)S(1)}, bf16[32,512]{1,0:T(8,128)(2,1)S(1)}, u32[]{:S(2)}, u32[]{:S(2)}) collective-permute-start(bf16[32,512]{1,0:T(8,128)(2,1)S(1)} %copy-done.8), channel_id=1, source_target_pairs={{0,2},{1,3},{2,0},{3,1},{4,6},{5,7},{6,4},{7,5},{8,10},{9,11},{10,... | collective-permute-start | bytes 98312 | tf_op jit(solution)/shard_map/ppermute | solution.py:25
  8.8 4.3 %collective-permute-start.3 = (bf16[64,512]{1,0:T(8,128)(2,1)S(1)}, bf16[64,512]{1,0:T(8,128)(2,1)S(1)}, u32[]{:S(2)}, u32[]{:S(2)}) collective-permute-start(bf16[64,512]{1,0:T(8,128)(2,1)S(1)} %pad_maximum_fusion.4), channel_id=1, source_target_pairs={{0,16},{4,20},{8,24},{12,28},{16,0},{20,4},{24,8},{28,12},{1,17},{... | collective-permute-start | bytes 196616 | tf_op jit(solution)/shard_map/ppermute | solution.py:25
  11.1 2.2 %copy-start.9 = (f32[128,64]{0,1:T(8,128)S(1)}, f32[128,64]{0,1:T(8,128)}, u32[]{:S(2)}) copy-start(f32[128,64]{0,1:T(8,128)} %param.15) | copy-start | bytes 98308
  11.1 4.3 %collective-permute-start.1 = (bf16[64,512]{1,0:T(8,128)(2,1)S(1)}, bf16[64,512]{1,0:T(8,128)(2,1)S(1)}, u32[]{:S(2)}, u32[]{:S(2)}) collective-permute-start(bf16[64,512]{1,0:T(8,128)(2,1)S(1)} %pad_maximum_fusion.3), channel_id=1, source_target_pairs={{0,1},{1,0},{2,3},{3,2},{4,5},{5,4},{6,7},{7,6},{8,9},{9,8},{10,11... | collective-permute-start | bytes 196616 | tf_op jit(solution)/shard_map/ppermute | solution.py:25
  13.2 2.2 %collective-permute-start.4 = (bf16[128,512]{1,0:T(8,128)(2,1)S(1)}, bf16[128,512]{1,0:T(8,128)(2,1)S(1)}, u32[]{:S(2)}, u32[]{:S(2)}) collective-permute-start(bf16[128,512]{1,0:T(8,128)(2,1)S(1)} %pad_maximum_fusion.2), channel_id=1, source_target_pairs={{0,4},{4,0},{8,12},{12,8},{16,20},{20,16},{24,28},{28,24},{1,5},{5... | collective-permute-start | bytes 393224 | tf_op jit(solution)/shard_map/ppermute | solution.py:25
  15.4 0.8 %copy-start.2 = (f32[64,128]{1,0:T(8,128)S(1)}, f32[64,128]{1,0:T(8,128)}, u32[]{:S(2)}) copy-start(f32[64,128]{1,0:T(8,128)} %w_in_ref.1) | copy-start | bytes 98308
  15.4 0.7 %copy-start.5 = (f32[1024]{0:T(1024)S(1)}, f32[1024]{0:T(1024)}, u32[]{:S(2)}) copy-start(f32[1024]{0:T(1024)} %param.19) | copy-start | bytes 12292
  15.5 0.7 %copy-start.4 = (s32[1024]{0:T(1024)S(1)}, s32[1024]{0:T(1024)}, u32[]{:S(2)}) copy-start(s32[1024]{0:T(1024)} %param.18) | copy-start | bytes 12292
  15.5 0.7 %copy-start.3 = (s32[1024]{0:T(1024)S(1)}, s32[1024]{0:T(1024)}, u32[]{:S(2)}) copy-start(s32[1024]{0:T(1024)} %param.17) | copy-start | bytes 12292
  15.5 0.7 %copy-start.6 = (f32[128]{0:T(128)S(1)}, f32[128]{0:T(128)}, u32[]{:S(2)}) copy-start(f32[128]{0:T(128)} %param.14) | copy-start | bytes 1540
  15.5 0.7 %copy-start.7 = (f32[64]{0:T(128)S(1)}, f32[64]{0:T(128)}, u32[]{:S(2)}) copy-start(f32[64]{0:T(128)} %param.16) | copy-start | bytes 772
  22.7 1.7 %collective-permute-start.7 = (bf16[128,512]{1,0:T(8,128)(2,1)S(1)}, bf16[128,512]{1,0:T(8,128)(2,1)S(1)}, u32[]{:S(2)}, u32[]{:S(2)}) collective-permute-start(bf16[128,512]{1,0:T(8,128)(2,1)S(1)} %get-tuple-element.9), channel_id=1, source_target_pairs={{0,4},{4,0},{8,12},{12,8},{16,20},{20,16},{24,28},{28,24},{1,5},{5... | collective-permute-start | bytes 393224 | tf_op jit(solution)/shard_map/ppermute | solution.py:25
  22.8 4.5 %collective-permute-start.5 = (bf16[64,512]{1,0:T(8,128)(2,1)S(1)}, bf16[64,512]{1,0:T(8,128)(2,1)S(1)}, u32[]{:S(2)}, u32[]{:S(2)}) collective-permute-start(bf16[64,512]{1,0:T(8,128)(2,1)S(1)} %get-tuple-element.7), channel_id=1, source_target_pairs={{0,1},{1,0},{2,3},{3,2},{4,5},{5,4},{6,7},{7,6},{8,9},{9,8},{10,11... | collective-permute-start | bytes 196616 | tf_op jit(solution)/shard_map/ppermute | solution.py:25
  24.5 5.6 %collective-permute-start.8 = (bf16[64,512]{1,0:T(8,128)(2,1)S(1)}, bf16[64,512]{1,0:T(8,128)(2,1)S(1)}, u32[]{:S(2)}, u32[]{:S(2)}) collective-permute-start(bf16[64,512]{1,0:T(8,128)(2,1)S(1)} %slice.39), channel_id=1, source_target_pairs={{0,16},{4,20},{8,24},{12,28},{16,0},{20,4},{24,8},{28,12},{1,17},{... | collective-permute-start | bytes 196616 | tf_op jit(solution)/shard_map/ppermute | solution.py:25
  27.4 5.0 %collective-permute-start.6 = (bf16[32,512]{1,0:T(8,128)(2,1)S(1)}, bf16[32,512]{1,0:T(8,128)(2,1)S(1)}, u32[]{:S(2)}, u32[]{:S(2)}) collective-permute-start(bf16[32,512]{1,0:T(8,128)(2,1)S(1)} %slice.41), channel_id=1, source_target_pairs={{0,2},{1,3},{2,0},{3,1},{4,6},{5,7},{6,4},{7,5},{8,10},{9,11},{10,... | collective-permute-start | bytes 98312 | tf_op jit(solution)/shard_map/ppermute | solution.py:25
  30.1 4.0 %collective-permute-start.9 = (bf16[32,512]{1,0:T(8,128)(2,1)S(1)}, bf16[32,512]{1,0:T(8,128)(2,1)S(1)}, u32[]{:S(2)}, u32[]{:S(2)}) collective-permute-start(bf16[32,512]{1,0:T(8,128)(2,1)S(1)} %slice.40), channel_id=1, source_target_pairs={{0,8},{4,12},{8,0},{12,4},{16,24},{20,28},{24,16},{28,20},{1,9},{5... | collective-permute-start | bytes 98312 | tf_op jit(solution)/shard_map/ppermute | solution.py:25

commit v2 on v1

v2 whole, which is shorter than its diff:
```python
import functools
import math

import jax
import jax.numpy as jnp
from jax import lax
from jax.experimental import pallas as pl
from jax.experimental.pallas import tpu as pltpu
from jax.sharding import PartitionSpec as P


COMPS = 8
CDIM = 64
gate_cap = 8.0
F32 = jnp.float32
BF16 = jnp.bfloat16
VMEM = pl.BlockSpec(memory_space=pltpu.VMEM)
WIDE = 256
TILE = 128


def bits_of(size):
    return size.bit_length() - 1


def exchange(value, axis, step):
    size = lax.axis_size(axis)
    return lax.ppermute(value, axis, [(i, i ^ step) for i in range(size)])


def round_steps(size):
    steps = [1 << bit for bit in range(1, bits_of(size))]
    return steps + ([1] if size > 1 else [])


def place_of(block, me, size):
    apart = block ^ me
    if size < 4:
        return apart
    return (apart >> 1) | ((apart & 1) << (bits_of(size) - 1))


def ready_kernel(out_ref):
    out_ref[...] = jnp.zeros_like(out_ref)


def project_kernel(text_ref, proj_ref, ready_ref, out_ref):
    mixed = jnp.dot(text_ref[...], proj_ref[...], preferred_element_type=F32)
    parts = []
    for at in range(COMPS):
        part = mixed[:, at * CDIM : (at + 1) * CDIM]
        square = jnp.mean(part * part, axis=-1, keepdims=True)
        parts.append(part * lax.rsqrt(square + 1e-06))
    out_ref[...] = jnp.concatenate(parts, axis=1).astype(BF16)


def halves(value):
    upper = value.astype(BF16)
    return upper, (value - upper.astype(F32)).astype(BF16)


def weight_stack(weight, axis):
    upper, lower = halves(weight)
    return jnp.concatenate([upper, lower, upper], axis=axis)


def value_stack(value, bias):
    upper, lower = halves(value)
    pieces = [upper, upper, lower]
    if bias:
        pieces.append(jnp.ones((16, value.shape[1]), BF16))
    return jnp.concatenate(pieces, axis=0)


def bias_rows(bias):
    upper, rest = bias.astype(BF16), bias
    rows = [upper]
    for _ in range(2):
        rest = rest - upper.astype(F32)
        upper = rest.astype(BF16)
        rows.append(upper)
    rows.append(jnp.zeros((13, bias.shape[1]), BF16))
    return jnp.concatenate([r.astype(F32) for r in rows], axis=0).astype(BF16)


def fold_rows(parts):
    place = lax.broadcasted_iota(jnp.int32, parts[0].shape, 0)
    width = 4
    while len(parts) > 1:
        low = (place & width) == 0
        half = len(parts) // 2
        merged = []
        for at in range(half):
            one, two = parts[at], parts[at + half]
            stay = jnp.where(low, one, two)
            move = jnp.where(low, two, one)
            merged.append(stay + pltpu.roll(move, width, 0) if width == 4 else stay + shift_rows(move, width, low))
        parts = merged
        width //= 2
    return parts[0]


def shift_rows(value, width, low):
    return jnp.where(low, pltpu.roll(value, 8 - width, 0), pltpu.roll(value, width, 0))


def dot(one, two):
    return jnp.dot(one, two, preferred_element_type=F32)


def hot_rows(index, rows, size, me):
    each = rows // size
    spot = place_of(index // each, me, size) * each + index % each
    hot = lax.broadcasted_iota(jnp.int32, (rows, index.shape[1]), 0) == spot
    return jnp.where(hot, 1.0, 0.0).astype(BF16)


def user_kernel(
    sizes,
    users_ref,
    w_in_ref,
    b_in_ref,
    w_out_ref,
    b_out_ref,
    pair_user_ref,
    pair_item_ref,
    teacher_ref,
    user_pairs,
    user_hot,
    item_hot,
    w_in_fwd,
    w_out_fwd,
    w_in_bwd,
    w_out_bwd,
    target,
):
    n_user, n_item = sizes
    user_rows, item_rows = user_hot.shape[0], item_hot.shape[0]
    me_user, me_item = lax.axis_index("user"), lax.axis_index("item")
    w_in, w_out = w_in_ref[...], w_out_ref[...]
    w_in_fwd[...] = jnp.concatenate([weight_stack(w_in, 0), bias_rows(b_in_ref[...])], axis=0).T
    w_out_fwd[...] = jnp.concatenate([weight_stack(w_out, 0), bias_rows(b_out_ref[...])], axis=0).T
    w_in_bwd[...] = weight_stack(w_in, 1)
    w_out_bwd[...] = weight_stack(w_out, 1)
    target[...] = teacher_ref[...]
    users_t = users_ref[...].T
    for block in range(user_hot.shape[1] // WIDE):
        lanes = slice(block * WIDE, (block + 1) * WIDE)
        hot = hot_rows(pair_user_ref[:, lanes], user_rows, n_item, me_item)
        user_hot[:, lanes] = hot
        user_pairs[:, lanes] = dot(users_t, hot)
        item_hot[:, lanes] = hot_rows(pair_item_ref[:, lanes], item_rows, n_user, me_user)


def pair_gradients(grad_ref, pairs_ref, terms, span, row):
    for one in range(COMPS):
        spread = [
            jnp.broadcast_to(grad_ref[row(one, two) : row(one, two) + 1, span], (16, TILE)) for two in range(COMPS)
        ]
        for j in range(CDIM // 16):
            total = None
            for two in range(COMPS):
                at = two * CDIM + j * 16
                term = spread[two] * pairs_ref[at : at + 16, span]
                total = term if total is None else total + term
            at = one * CDIM + j * 16
            terms[at : at + 16, span] = total.astype(BF16)


def collect(hot, terms, keep_ref, send_ref):
    total = lax.dot_general(hot[...], terms[...], (((1,), (1,)), ((), ())), preferred_element_type=F32)
    half = total.shape[0] // 2
    keep_ref[...] = total[:half]
    send_ref[...] = total[half:].astype(BF16)


def pair_kernel(
    loss_scale,
    items_ref,
    user_pairs,
    user_hot,
    item_hot,
    w_in_fwd,
    w_out_fwd,
    w_in_bwd,
    w_out_bwd,
    target,
    user_keep_ref,
    user_send_ref,
    grad_ref,
    item_pairs,
    logits_ref,
    user_terms,
):
    pairs = user_hot.shape[1]
    blocks = pairs // WIDE
    scale = 1.0 / math.sqrt(CDIM)
    items_t = items_ref[...].T

    def gather(block):
        lanes = slice(block * WIDE, (block + 1) * WIDE)
        item_pairs[:, lanes] = dot(items_t, item_hot[:, lanes])

    def spans(block):
        return [slice(block * WIDE + at, block * WIDE + at + TILE) for at in range(0, WIDE, TILE)]

    def make_logits(block):
        for span in spans(block):
            for c in range(COMPS):
                parts = []
                for k in range(COMPS):
                    total = None
                    for j in range(CDIM // 8):
                        u = user_pairs[c * CDIM + j * 8 : c * CDIM + (j + 1) * 8, span]
                        v = item_pairs[k * CDIM + j * 8 : k * CDIM + (j + 1) * 8, span]
                        total = u * v if total is None else total + u * v
                    parts.append(total)
                logits_ref[c * COMPS : (c + 1) * COMPS, span] = fold_rows(parts) * scale

    def gate(block):
        lanes = slice(block * WIDE, (block + 1) * WIDE)
        logits = logits_ref[:, lanes]
        pre = dot(w_in_fwd[...], value_stack(logits, True))
        sig = 0.5 * jnp.tanh(0.5 * pre) + 0.5
        hidden = pre * sig
        raw = dot(w_out_fwd[...], value_stack(hidden, True))
        capped = jnp.tanh(raw * (1.0 / gate_cap))
        powers = jnp.exp(gate_cap * capped)
        weights = powers * (1.0 / jnp.sum(powers, axis=0, keepdims=True))
        student = jnp.sum(weights * logits, axis=0, keepdims=True)
        residual = (student - target[:, lanes]) * (loss_scale * scale)
        d_gate = weights * (logits - student) * (1.0 - capped * capped)
        d_hidden = dot(w_out_bwd[...], value_stack(d_gate, False))
        d_pre = d_hidden * (sig + hidden * (1.0 - sig))
        d_flat = residual * (weights + dot(w_in_bwd[...], value_stack(d_pre, False)))
        grad_ref[:, lanes] = d_flat.astype(BF16).astype(F32)

    def gradients(block):
        for span in spans(block):
            pair_gradients(grad_ref, item_pairs, user_terms, span, lambda c, k: c * COMPS + k)

    stages = (gather, make_logits, gate, gradients)
    for step in range(blocks + len(stages) - 1):
        for at, stage in enumerate(stages):
            if 0 <= step - at < blocks:
                stage(step - at)
    collect(user_hot, user_terms, user_keep_ref, user_send_ref)


def item_kernel(user_pairs, item_hot, grad_ref, item_keep_ref, item_send_ref, item_terms):
    for at in range(0, item_hot.shape[1], TILE):
        pair_gradients(grad_ref, user_pairs, item_terms, slice(at, at + TILE), lambda k, c: c * COMPS + k)
    collect(item_hot, item_terms, item_keep_ref, item_send_ref)


def shape(rows, columns, kind):
    return jax.ShapeDtypeStruct((rows, columns), kind)


def call(kernel, outputs, scratch, arguments, grant, micros):
    return pl.pallas_call(
        kernel,
        out_shape=outputs,
        in_specs=[VMEM] * len(arguments),
        out_specs=[VMEM] * len(outputs),
        scratch_shapes=[pltpu.VMEM(s.shape, s.dtype) for s in scratch],
        compiler_params=pltpu.CompilerParams(vmem_limit_bytes=grant << 20),
        cost_estimate=pl.CostEstimate(flops=int(micros*5e8), bytes_accessed=int(micros * 3e6), transcendentals=0),
    )(*arguments)


def gather_round(value, axis, step):
    return jnp.concatenate([value, exchange(value, axis, step)], axis=0)


def local(user_comps, item_text, item_proj, w_in, b_in, w_out, b_out, pair_user, pair_item, teacher):
    n_user, n_item = lax.axis_size("user"), lax.axis_size("item")
    pairs, width = pair_user.shape[0], COMPS * CDIM
    hidden, gates = b_in.shape[0], b_out.shape[0]
    user_rows, item_rows = user_comps.shape[0] * n_item, item_text.shape[0] * n_user
    loss_scale = 2.0 * math.sqrt(user_rows / (pairs * n_item))

    (ready,) = call(ready_kernel, [shape(8, 128, F32)], [], [], 1, 8.0)
    users = user_comps
    for step in round_steps(n_item):
        users = gather_round(users, "item", step)
    (items,) = call(project_kernel, [shape(item_text.shape[0], width, BF16)], [], [item_text, item_proj, ready], 8, 2.0)
    for step in round_steps(n_user):
        items = gather_round(items, "user", step)

    user_pairs, user_hot, item_hot, w_in_fwd, w_out_fwd, w_in_bwd, w_out_bwd, target = call(
        functools.partial(user_kernel, (n_user, n_item)),
        [
            shape(width, pairs, F32),
            shape(user_rows, pairs, BF16),
            shape(item_rows, pairs, BF16),
            shape(hidden, 3 * gates + 16, BF16),
            shape(gates, 3 * hidden + 16, BF16),
            shape(gates, 3 * hidden, BF16),
            shape(hidden, 3 * gates, BF16),
            shape(1, pairs, F32),
        ],
        [],
        [
            users,
            w_in,
            b_in.reshape(1, -1),
            w_out,
            b_out.reshape(1, -1),
            pair_user.reshape(1, -1),
            pair_item.reshape(1, -1),
            teacher.reshape(1, -1),
        ],
        12,
        1.5,
    )
    user_keep, user_send, grads = call(
        functools.partial(pair_kernel, loss_scale),
        [shape(user_rows // 2, width, F32), shape(user_rows // 2, width, BF16), shape(gates, pairs, F32)],
        [shape(width, pairs, F32), shape(gates, pairs, F32), shape(width, pairs, BF16)],
        [items, user_pairs, user_hot, item_hot, w_in_fwd, w_out_fwd, w_in_bwd, w_out_bwd, target],
        20,
        4.5,
    )
    item_keep, item_send = call(
        item_kernel,
        [shape(item_rows // 2, width, F32), shape(item_rows // 2, width, BF16)],
        [shape(width, pairs, BF16)],
        [user_pairs, item_hot, grads],
        12,
        2.0,
    )

    def scatter(keep, send, axis):
        steps = round_steps(lax.axis_size(axis))[::-1]
        for at, step in enumerate(steps):
            total = keep + exchange(send, axis, step).astype(F32)
            if at + 1 < len(steps):
                half = total.shape[0] // 2
                keep, send = total[:half], total[half:].astype(BF16)
        return total

    return scatter(user_keep, user_send, "item"), scatter(item_keep, item_send, "user")


def solution(mesh):
    split = P(("user", "item"))
    rows = P(("user", "item"), None)
    in_specs = (rows, rows, P(), P(), P(), P(), P(), split, split, split)

    return jax.shard_map(local, mesh=mesh, in_specs=in_specs, out_specs=(rows, rows), check_vma=False)
```

time: 35 us -> 33.3 us (0.951)
  local copies, waits for them, and re-layouts: 2.87 us -> 1.36 us
    unnamed x21, local copies, waits for them, and re-layouts: 2.84 us -> 1.33 us
    pallas_call x2 -> x5, Pallas kernels: 7.06 us -> 7 us  [call(): pl.pallas_call(kernel, out_shape=outputs, in_specs=[VMEM] * len(arguments...]
  transfers between devices with their start and end apart: 10 -> 10, of which waited for: 6 -> 6; matrix products, arithmetic and copies ran while one was open for 2% -> 3% of each run, Pallas kernels for 0% -> 2%
where the time goes in v2:
time: 33.3 us; the launch traced here: 33.2 us
  starting transfers between devices  15.6 us (47%)
  Pallas kernels  7 us (21%)
  waiting for transfers between devices  6.98 us (21%)
  other arithmetic  1.39 us (4%)
  local copies, waits for them, and re-layouts  1.36 us (4%)
  between operations  0.87 us (3%)
    ppermute x10, starting transfers between devices, exchange(): return lax.ppermute(value, axis, [(i, i ^ step) for i in range(size)])  15.6 us
    pallas_call x5, Pallas kernels, call(): pl.pallas_call(kernel, out_shape=outputs, in_specs=[VMEM] * len(arguments...  7 us
    ppermute x10, waiting for transfers between devices, exchange(): return lax.ppermute(value, axis, [(i, i ^ step) for i in range(size)])  6.98 us
    add x5, other arithmetic, scatter(): total = keep + exchange(send, axis, step).astype(F32)  1.34 us
    unnamed x21, local copies, waits for them, and re-layouts  1.33 us
  transfers between devices with their start and end apart: 10, of which 6 were waited for; matrix products, arithmetic and copies ran while one was open for 3% of the time, Pallas kernels for 2%

profile of v2, /device:TPU:0, one launch (start us, length us, event | category | flops | bytes accessed | tf_op | source)
XLA Modules:
  0.0 33.2 jit_solution(17597433601462439048)
XLA Ops:
  0.6 0.0 copy-start
  0.6 0.0 copy-start.1
  0.7 1.2 %copy-done = bf16[1024,512]{1,0:T(8,128)(2,1)S(1)} copy-done((bf16[1024,512]{1,0:T(8,128)(2,1)S(1)}, bf16[1024,512]{1,0:T(8,128)(2,1)}, u32[]{:S(2)}) %copy-start) | copy-done | bytes 1048600
  1.9 0.0 copy-done.1
  1.9 0.0 copy-start.8
  1.9 0.0 copy-start.9
  1.9 0.0 copy-start.2
  1.9 0.0 copy-start.3
  1.9 0.0 copy-start.4
  1.9 0.0 copy-start.5
  1.9 0.0 copy-start.6
  1.9 0.0 copy-start.7
  1.9 0.5 %shard_map.114 = bf16[32,512]{1,0:T(8,128)(2,1)S(1)} custom-call(bf16[32,1024]{1,0:T(8,128)(2,1)S(1)} %copy-done.1, bf16[1024,512]{1,0:T(8,128)(2,1)S(1)} %copy-done, f32[8,128]{1,0:T(8,128)S(1)} %shard_map.113.ready_ref), custom_call_target="tpu_custom_call" | custom-call | flops 1000000000 | bytes 6000000 | tf_op jit(solution)/shard_map/pallas_call | solution.py:261
  2.4 3.0 %collective-permute-start = (bf16[32,512]{1,0:T(8,128)(2,1)S(1)}, bf16[32,512]{1,0:T(8,128)(2,1)S(1)}, u32[]{:S(2)}, u32[]{:S(2)}) collective-permute-start(bf16[32,512]{1,0:T(8,128)(2,1)S(1)} %shard_map.114), channel_id=1, source_target_pairs={{0,8},{4,12},{8,0},{12,4},{16,24},{20,28},{24,16},{28,20},{1,9},{5... | collective-permute-start | bytes 98312 | tf_op jit(solution)/shard_map/ppermute | solution.py:28
  5.5 0.0 copy-done.8
  5.5 2.6 %collective-permute-start.3 = (bf16[32,512]{1,0:T(8,128)(2,1)S(1)}, bf16[32,512]{1,0:T(8,128)(2,1)S(1)}, u32[]{:S(2)}, u32[]{:S(2)}) collective-permute-start(bf16[32,512]{1,0:T(8,128)(2,1)S(1)} %copy-done.8), channel_id=1, source_target_pairs={{0,2},{1,3},{2,0},{3,1},{4,6},{5,7},{6,4},{7,5},{8,10},{9,11},{10,... | collective-permute-start | bytes 98312 | tf_op jit(solution)/shard_map/ppermute | solution.py:28
  8.1 0.0 copy-done.9
  8.1 0.1 copy.12.w_out_ref
  8.2 0.0 collective-permute-done
  8.2 1.6 %collective-permute-start.1 = (bf16[64,512]{1,0:T(8,128)(2,1)S(1)}, bf16[64,512]{1,0:T(8,128)(2,1)S(1)}, u32[]{:S(2)}, u32[]{:S(2)}) collective-permute-start(bf16[64,512]{1,0:T(8,128)(2,1)S(1)} %pad_maximum_fusion.3), channel_id=1, source_target_pairs={{0,16},{4,20},{8,24},{12,28},{16,0},{20,4},{24,8},{28,12},{1,17},{... | collective-permute-start | bytes 196616 | tf_op jit(solution)/shard_map/ppermute | solution.py:28
  9.8 0.5 %collective-permute-done.3 = bf16[32,512]{1,0:T(8,128)(2,1)S(1)} collective-permute-done((bf16[32,512]{1,0:T(8,128)(2,1)S(1)}, bf16[32,512]{1,0:T(8,128)(2,1)S(1)}, u32[]{:S(2)}, u32[]{:S(2)}) %collective-permute-start.3) | collective-permute-done | bytes 32800 | tf_op jit(solution)/shard_map/ppermute | solution.py:28
  10.3 1.6 %collective-permute-start.4 = (bf16[64,512]{1,0:T(8,128)(2,1)S(1)}, bf16[64,512]{1,0:T(8,128)(2,1)S(1)}, u32[]{:S(2)}, u32[]{:S(2)}) collective-permute-start(bf16[64,512]{1,0:T(8,128)(2,1)S(1)} %pad_maximum_fusion.4), channel_id=1, source_target_pairs={{0,1},{1,0},{2,3},{3,2},{4,5},{5,4},{6,7},{7,6},{8,9},{9,8},{10,11... | collective-permute-start | bytes 196616 | tf_op jit(solution)/shard_map/ppermute | solution.py:28
  11.9 0.6 %collective-permute-done.1 = bf16[64,512]{1,0:T(8,128)(2,1)S(1)} collective-permute-done((bf16[64,512]{1,0:T(8,128)(2,1)S(1)}, bf16[64,512]{1,0:T(8,128)(2,1)S(1)}, u32[]{:S(2)}, u32[]{:S(2)}) %collective-permute-start.1) | collective-permute-done | bytes 65568 | tf_op jit(solution)/shard_map/ppermute | solution.py:28
  12.5 0.1 collective-permute-start.2
  12.6 1.9 %collective-permute-done.4 = bf16[64,512]{1,0:T(8,128)(2,1)S(1)} collective-permute-done((bf16[64,512]{1,0:T(8,128)(2,1)S(1)}, bf16[64,512]{1,0:T(8,128)(2,1)S(1)}, u32[]{:S(2)}, u32[]{:S(2)}) %collective-permute-start.4) | collective-permute-done | bytes 65568 | tf_op jit(solution)/shard_map/ppermute | solution.py:28
  14.6 0.0 copy-done.2
  14.6 0.0 copy-done.3
  14.6 0.0 copy-done.4
  14.6 0.0 copy-done.5
  14.6 0.0 copy-done.6
  14.6 0.0 copy-done.7
  14.6 0.6 %shard_map.115 = (f32[512,1024]{1,0:T(8,128)S(1)}, bf16[128,1024]{1,0:T(8,128)(2,1)S(1)}, bf16[256,1024]{1,0:T(8,128)(2,1)S(1)}, bf16[128,208]{1,0:T(8,128)(2,1)...) custom-call(bf16[128,512]{1,0:T(8,128)(2,1)S(1)} %pad_maximum_fusion, ...), custom_call_target="tpu_custom_call" | custom-call | flops 750000000 | bytes 4500000 | tf_op jit(solution)/shard_map/pallas_call | solution.py:261
  15.2 0.0 collective-permute-done.2
  15.3 4.2 %shard_map.116 = (f32[64,512]{1,0:T(8,128)S(1)}, bf16[64,512]{1,0:T(8,128)(2,1)S(1)}, f32[64,1024]{1,0:T(8,128)S(1)}) custom-call(bf16[256,512]{1,0:T(8,128)(2,1)S(1)} %pad_maximum_fusion.items_ref, f32[512,1024]{1,0:T(8,128)S(1)} %get-tuple-element.15.user_pairs, bf16[128,1024]{1,0:T(8,128)(2,1)S(1)} %get-tuple-element.16.user_hot, ...), custom_call_target="tpu_custom_call" | custom-call | flops 2249999872 | bytes 13500000 | tf_op jit(solution)/shard_map/pallas_call | solution.py:261
  19.4 1.7 %shard_map.117 = (f32[128,512]{1,0:T(8,128)S(1)}, bf16[128,512]{1,0:T(8,128)(2,1)S(1)}) custom-call(f32[512,1024]{1,0:T(8,128)S(1)} %get-tuple-element.15.user_pairs, bf16[256,1024]{1,0:T(8,128)(2,1)S(1)} %get-tuple-element.17.item_hot, f32[64,1024]{1,0:T(8,128)S(1)} %get-tuple-element.25.grad_ref), custom_call_target="tpu_custom_call" | custom-call | flops 1000000000 | bytes 6000000 | tf_op jit(solution)/shard_map/pallas_call | solution.py:261
  21.2 0.1 collective-permute-start.7
  21.3 1.6 %collective-permute-start.5 = (bf16[64,512]{1,0:T(8,128)(2,1)S(1)}, bf16[64,512]{1,0:T(8,128)(2,1)S(1)}, u32[]{:S(2)}, u32[]{:S(2)}) collective-permute-start(bf16[64,512]{1,0:T(8,128)(2,1)S(1)} %get-tuple-element.24), channel_id=1, source_target_pairs={{0,1},{1,0},{2,3},{3,2},{4,5},{5,4},{6,7},{7,6},{8,9},{9,8},{10,11... | collective-permute-start | bytes 196616 | tf_op jit(solution)/shard_map/ppermute | solution.py:28
  22.9 0.0 collective-permute-done.7
  23.0 1.6 %collective-permute-start.8 = (bf16[64,512]{1,0:T(8,128)(2,1)S(1)}, bf16[64,512]{1,0:T(8,128)(2,1)S(1)}, u32[]{:S(2)}, u32[]{:S(2)}) collective-permute-start(bf16[64,512]{1,0:T(8,128)(2,1)S(1)} %slice.39), channel_id=1, source_target_pairs={{0,16},{4,20},{8,24},{12,28},{16,0},{20,4},{24,8},{28,12},{1,17},{... | collective-permute-start | bytes 196616 | tf_op jit(solution)/shard_map/ppermute | solution.py:28
  24.5 1.2 %collective-permute-done.5 = bf16[64,512]{1,0:T(8,128)(2,1)S(1)} collective-permute-done((bf16[64,512]{1,0:T(8,128)(2,1)S(1)}, bf16[64,512]{1,0:T(8,128)(2,1)S(1)}, u32[]{:S(2)}, u32[]{:S(2)}) %collective-permute-start.5) | collective-permute-done | bytes 65568 | tf_op jit(solution)/shard_map/ppermute | solution.py:28
  25.8 2.7 %collective-permute-start.6 = (bf16[32,512]{1,0:T(8,128)(2,1)S(1)}, bf16[32,512]{1,0:T(8,128)(2,1)S(1)}, u32[]{:S(2)}, u32[]{:S(2)}) collective-permute-start(bf16[32,512]{1,0:T(8,128)(2,1)S(1)} %slice.41), channel_id=1, source_target_pairs={{0,2},{1,3},{2,0},{3,1},{4,6},{5,7},{6,4},{7,5},{8,10},{9,11},{10,... | collective-permute-start | bytes 98312 | tf_op jit(solution)/shard_map/ppermute | solution.py:28
  28.5 0.0 collective-permute-done.8
  28.5 0.7 %collective-permute-start.9 = (bf16[32,512]{1,0:T(8,128)(2,1)S(1)}, bf16[32,512]{1,0:T(8,128)(2,1)S(1)}, u32[]{:S(2)}, u32[]{:S(2)}) collective-permute-start(bf16[32,512]{1,0:T(8,128)(2,1)S(1)} %slice.40), channel_id=1, source_target_pairs={{0,8},{4,12},{8,0},{12,4},{16,24},{20,28},{24,16},{28,20},{1,9},{5... | collective-permute-start | bytes 98312 | tf_op jit(solution)/shard_map/ppermute | solution.py:28
  29.2 1.6 %collective-permute-done.6 = bf16[32,512]{1,0:T(8,128)(2,1)S(1)} collective-permute-done((bf16[32,512]{1,0:T(8,128)(2,1)S(1)}, bf16[32,512]{1,0:T(8,128)(2,1)S(1)}, u32[]{:S(2)}, u32[]{:S(2)}) %collective-permute-start.6) | collective-permute-done | bytes 32800 | tf_op jit(solution)/shard_map/ppermute | solution.py:28
  30.8 0.6 %slice_add_fusion.2 = f32[32,512]{1,0:T(8,128)} fusion(f32[64,512]{1,0:T(8,128)S(1)} %convert_add_fusion.1, bf16[32,512]{1,0:T(8,128)(2,1)S(1)} %collective-permute-done.6), kind=kLoop, calls=%fused_computation.10 | loop fusion | flops 32768 | bytes 163840 | tf_op jit(solution)/shard_map/add | solution.py:337
  31.4 1.1 %collective-permute-done.9 = bf16[32,512]{1,0:T(8,128)(2,1)S(1)} collective-permute-done((bf16[32,512]{1,0:T(8,128)(2,1)S(1)}, bf16[32,512]{1,0:T(8,128)(2,1)S(1)}, u32[]{:S(2)}, u32[]{:S(2)}) %collective-permute-start.9) | collective-permute-done | bytes 32800 | tf_op jit(solution)/shard_map/ppermute | solution.py:28
  32.5 0.6 %slice_add_fusion.1 = f32[32,512]{1,0:T(8,128)} fusion(f32[64,512]{1,0:T(8,128)S(1)} %slice_add_fusion, bf16[32,512]{1,0:T(8,128)(2,1)S(1)} %collective-permute-done.9), kind=kLoop, calls=%fused_computation.8 | loop fusion | flops 32768 | bytes 163840 | tf_op jit(solution)/shard_map/add | solution.py:337
  (12 shorter events, 0.1 us)
Async XLA Ops:
  0.6 1.2 %copy-start = (bf16[1024,512]{1,0:T(8,128)(2,1)S(1)}, bf16[1024,512]{1,0:T(8,128)(2,1)}, u32[]{:S(2)}) copy-start(bf16[1024,512]{1,0:T(8,128)(2,1)} %proj_ref.1) | copy-start | bytes 3145732
  0.6 1.2 %copy-start.1 = (bf16[32,1024]{1,0:T(8,128)(2,1)S(1)}, bf16[32,1024]{1,0:T(8,128)(2,1)}, u32[]{:S(2)}) copy-start(bf16[32,1024]{1,0:T(8,128)(2,1)} %text_ref.1) | copy-start | bytes 196612
  1.9 3.6 %copy-start.8 = (bf16[32,512]{1,0:T(8,128)(2,1)S(1)}, bf16[32,512]{1,0:T(8,128)(2,1)}, u32[]{:S(2)}) copy-start(bf16[32,512]{1,0:T(8,128)(2,1)} %param.10) | copy-start | bytes 98308
  1.9 6.2 %copy-start.9 = (f32[128,64]{0,1:T(8,128)S(1)}, f32[128,64]{0,1:T(8,128)}, u32[]{:S(2)}) copy-start(f32[128,64]{0,1:T(8,128)} %param.15) | copy-start | bytes 98308
  1.9 12.7 %copy-start.2 = (f32[64,128]{1,0:T(8,128)S(1)}, f32[64,128]{1,0:T(8,128)}, u32[]{:S(2)}) copy-start(f32[64,128]{1,0:T(8,128)} %w_in_ref.1) | copy-start | bytes 98308
  1.9 12.7 %copy-start.3 = (s32[1024]{0:T(1024)S(1)}, s32[1024]{0:T(1024)}, u32[]{:S(2)}) copy-start(s32[1024]{0:T(1024)} %param.17) | copy-start | bytes 12292
  1.9 12.7 %copy-start.4 = (s32[1024]{0:T(1024)S(1)}, s32[1024]{0:T(1024)}, u32[]{:S(2)}) copy-start(s32[1024]{0:T(1024)} %param.18) | copy-start | bytes 12292
  1.9 12.7 %copy-start.5 = (f32[1024]{0:T(1024)S(1)}, f32[1024]{0:T(1024)}, u32[]{:S(2)}) copy-start(f32[1024]{0:T(1024)} %param.19) | copy-start | bytes 12292
  1.9 12.7 %copy-start.6 = (f32[128]{0:T(128)S(1)}, f32[128]{0:T(128)}, u32[]{:S(2)}) copy-start(f32[128]{0:T(128)} %param.14) | copy-start | bytes 1540
  1.9 12.7 %copy-start.7 = (f32[64]{0:T(128)S(1)}, f32[64]{0:T(128)}, u32[]{:S(2)}) copy-start(f32[64]{0:T(128)} %param.16) | copy-start | bytes 772
  2.4 5.7 %collective-permute-start = (bf16[32,512]{1,0:T(8,128)(2,1)S(1)}, bf16[32,512]{1,0:T(8,128)(2,1)S(1)}, u32[]{:S(2)}, u32[]{:S(2)}) collective-permute-start(bf16[32,512]{1,0:T(8,128)(2,1)S(1)} %shard_map.114), channel_id=1, source_target_pairs={{0,8},{4,12},{8,0},{12,4},{16,24},{20,28},{24,16},{28,20},{1,9},{5... | collective-permute-start | bytes 98312 | tf_op jit(solution)/shard_map/ppermute | solution.py:28
  5.5 4.8 %collective-permute-start.3 = (bf16[32,512]{1,0:T(8,128)(2,1)S(1)}, bf16[32,512]{1,0:T(8,128)(2,1)S(1)}, u32[]{:S(2)}, u32[]{:S(2)}) collective-permute-start(bf16[32,512]{1,0:T(8,128)(2,1)S(1)} %copy-done.8), channel_id=1, source_target_pairs={{0,2},{1,3},{2,0},{3,1},{4,6},{5,7},{6,4},{7,5},{8,10},{9,11},{10,... | collective-permute-start | bytes 98312 | tf_op jit(solution)/shard_map/ppermute | solution.py:28
  8.2 4.3 %collective-permute-start.1 = (bf16[64,512]{1,0:T(8,128)(2,1)S(1)}, bf16[64,512]{1,0:T(8,128)(2,1)S(1)}, u32[]{:S(2)}, u32[]{:S(2)}) collective-permute-start(bf16[64,512]{1,0:T(8,128)(2,1)S(1)} %pad_maximum_fusion.3), channel_id=1, source_target_pairs={{0,16},{4,20},{8,24},{12,28},{16,0},{20,4},{24,8},{28,12},{1,17},{... | collective-permute-start | bytes 196616 | tf_op jit(solution)/shard_map/ppermute | solution.py:28
  10.3 4.3 %collective-permute-start.4 = (bf16[64,512]{1,0:T(8,128)(2,1)S(1)}, bf16[64,512]{1,0:T(8,128)(2,1)S(1)}, u32[]{:S(2)}, u32[]{:S(2)}) collective-permute-start(bf16[64,512]{1,0:T(8,128)(2,1)S(1)} %pad_maximum_fusion.4), channel_id=1, source_target_pairs={{0,1},{1,0},{2,3},{3,2},{4,5},{5,4},{6,7},{7,6},{8,9},{9,8},{10,11... | collective-permute-start | bytes 196616 | tf_op jit(solution)/shard_map/ppermute | solution.py:28
  12.5 2.7 %collective-permute-start.2 = (bf16[128,512]{1,0:T(8,128)(2,1)S(1)}, bf16[128,512]{1,0:T(8,128)(2,1)S(1)}, u32[]{:S(2)}, u32[]{:S(2)}) collective-permute-start(bf16[128,512]{1,0:T(8,128)(2,1)S(1)} %pad_maximum_fusion.1), channel_id=1, source_target_pairs={{0,4},{4,0},{8,12},{12,8},{16,20},{20,16},{24,28},{28,24},{1,5},{5... | collective-permute-start | bytes 393224 | tf_op jit(solution)/shard_map/ppermute | solution.py:28
  21.2 1.7 %collective-permute-start.7 = (bf16[128,512]{1,0:T(8,128)(2,1)S(1)}, bf16[128,512]{1,0:T(8,128)(2,1)S(1)}, u32[]{:S(2)}, u32[]{:S(2)}) collective-permute-start(bf16[128,512]{1,0:T(8,128)(2,1)S(1)} %get-tuple-element.27), channel_id=1, source_target_pairs={{0,4},{4,0},{8,12},{12,8},{16,20},{20,16},{24,28},{28,24},{1,5},{5... | collective-permute-start | bytes 393224 | tf_op jit(solution)/shard_map/ppermute | solution.py:28
  21.3 4.5 %collective-permute-start.5 = (bf16[64,512]{1,0:T(8,128)(2,1)S(1)}, bf16[64,512]{1,0:T(8,128)(2,1)S(1)}, u32[]{:S(2)}, u32[]{:S(2)}) collective-permute-start(bf16[64,512]{1,0:T(8,128)(2,1)S(1)} %get-tuple-element.24), channel_id=1, source_target_pairs={{0,1},{1,0},{2,3},{3,2},{4,5},{5,4},{6,7},{7,6},{8,9},{9,8},{10,11... | collective-permute-start | bytes 196616 | tf_op jit(solution)/shard_map/ppermute | solution.py:28
  23.0 5.5 %collective-permute-start.8 = (bf16[64,512]{1,0:T(8,128)(2,1)S(1)}, bf16[64,512]{1,0:T(8,128)(2,1)S(1)}, u32[]{:S(2)}, u32[]{:S(2)}) collective-permute-start(bf16[64,512]{1,0:T(8,128)(2,1)S(1)} %slice.39), channel_id=1, source_target_pairs={{0,16},{4,20},{8,24},{12,28},{16,0},{20,4},{24,8},{28,12},{1,17},{... | collective-permute-start | bytes 196616 | tf_op jit(solution)/shard_map/ppermute | solution.py:28
  25.8 5.0 %collective-permute-start.6 = (bf16[32,512]{1,0:T(8,128)(2,1)S(1)}, bf16[32,512]{1,0:T(8,128)(2,1)S(1)}, u32[]{:S(2)}, u32[]{:S(2)}) collective-permute-start(bf16[32,512]{1,0:T(8,128)(2,1)S(1)} %slice.41), channel_id=1, source_target_pairs={{0,2},{1,3},{2,0},{3,1},{4,6},{5,7},{6,4},{7,5},{8,10},{9,11},{10,... | collective-permute-start | bytes 98312 | tf_op jit(solution)/shard_map/ppermute | solution.py:28
  28.5 4.0 %collective-permute-start.9 = (bf16[32,512]{1,0:T(8,128)(2,1)S(1)}, bf16[32,512]{1,0:T(8,128)(2,1)S(1)}, u32[]{:S(2)}, u32[]{:S(2)}) collective-permute-start(bf16[32,512]{1,0:T(8,128)(2,1)S(1)} %slice.40), channel_id=1, source_target_pairs={{0,8},{4,12},{8,0},{12,4},{16,24},{20,28},{24,16},{28,20},{1,9},{5... | collective-permute-start | bytes 98312 | tf_op jit(solution)/shard_map/ppermute | solution.py:28

commit v3 on v2

--- a/solution.py
+++ b/solution.py
@@ -28,16 +28,21 @@
     return lax.ppermute(value, axis, [(i, i ^ step) for i in range(size)])
 
 
-def round_steps(size):
-    steps = [1 << bit for bit in range(1, bits_of(size))]
+def round_steps(size, crossed):
+    steps = [(1 << bit) | crossed for bit in range(1, bits_of(size))]
     return steps + ([1] if size > 1 else [])
 
 
-def place_of(block, me, size):
+def place_of(block, me, size, crossed):
     apart = block ^ me
-    if size < 4:
+    bits = bits_of(size)
+    if bits < 2:
         return apart
-    return (apart >> 1) | ((apart & 1) << (bits_of(size) - 1))
+    last = apart & 1
+    if crossed:
+        for bit in range(1, bits):
+            last = last ^ ((apart >> bit) & 1)
+    return (apart >> 1) | (last << (bits - 1))
 
 
 def ready_kernel(out_ref):
@@ -108,16 +113,16 @@
     return jnp.dot(one, two, preferred_element_type=F32)
 
 
-def hot_rows(index, rows, size, me):
+def hot_rows(index, rows, size, me, crossed):
     each = rows // size
-    spot = place_of(index // each, me, size) * each + index % each
+    spot = place_of(index // each, me, size, crossed) * each + index % each
     hot = lax.broadcasted_iota(jnp.int32, (rows, index.shape[1]), 0) == spot
     return jnp.where(hot, 1.0, 0.0).astype(BF16)
 
 
-def user_kernel(
+def item_kernel(
     sizes,
-    users_ref,
+    items_ref,
     w_in_ref,
     b_in_ref,
     w_out_ref,
@@ -125,7 +130,7 @@
     pair_user_ref,
     pair_item_ref,
     teacher_ref,
-    user_pairs,
+    item_pairs,
     user_hot,
     item_hot,
     w_in_fwd,
@@ -143,13 +148,13 @@
     w_in_bwd[...] = weight_stack(w_in, 1)
     w_out_bwd[...] = weight_stack(w_out, 1)
     target[...] = teacher_ref[...]
-    users_t = users_ref[...].T
+    items_t = items_ref[...].T
     for block in range(user_hot.shape[1] // WIDE):
         lanes = slice(block * WIDE, (block + 1) * WIDE)
-        hot = hot_rows(pair_user_ref[:, lanes], user_rows, n_item, me_item)
-        user_hot[:, lanes] = hot
-        user_pairs[:, lanes] = dot(users_t, hot)
-        item_hot[:, lanes] = hot_rows(pair_item_ref[:, lanes], item_rows, n_user, me_user)
+        hot = hot_rows(pair_item_ref[:, lanes], item_rows, n_user, me_user, 1)
+        item_hot[:, lanes] = hot
+        item_pairs[:, lanes] = dot(items_t, hot)
+        user_hot[:, lanes] = hot_rows(pair_user_ref[:, lanes], user_rows, n_item, me_item, 0)
 
 
 def pair_gradients(grad_ref, pairs_ref, terms, span, row):
@@ -176,8 +181,8 @@
 
 def pair_kernel(
     loss_scale,
-    items_ref,
-    user_pairs,
+    users_ref,
+    item_pairs,
     user_hot,
     item_hot,
     w_in_fwd,
@@ -185,21 +190,21 @@
     w_in_bwd,
     w_out_bwd,
     target,
-    user_keep_ref,
-    user_send_ref,
+    item_keep_ref,
+    item_send_ref,
     grad_ref,
-    item_pairs,
+    user_pairs,
     logits_ref,
-    user_terms,
+    item_terms,
 ):
     pairs = user_hot.shape[1]
     blocks = pairs // WIDE
     scale = 1.0 / math.sqrt(CDIM)
-    items_t = items_ref[...].T
+    users_t = users_ref[...].T
 
     def gather(block):
         lanes = slice(block * WIDE, (block + 1) * WIDE)
-        item_pairs[:, lanes] = dot(items_t, item_hot[:, lanes])
+        user_pairs[:, lanes] = dot(users_t, user_hot[:, lanes])
 
     def spans(block):
         return [slice(block * WIDE + at, block * WIDE + at + TILE) for at in range(0, WIDE, TILE)]
@@ -237,20 +242,20 @@
 
     def gradients(block):
         for span in spans(block):
-            pair_gradients(grad_ref, item_pairs, user_terms, span, lambda c, k: c * COMPS + k)
+            pair_gradients(grad_ref, user_pairs, item_terms, span, lambda k, c: c * COMPS + k)
 
     stages = (gather, make_logits, gate, gradients)
     for step in range(blocks + len(stages) - 1):
         for at, stage in enumerate(stages):
             if 0 <= step - at < blocks:
                 stage(step - at)
+    collect(item_hot, item_terms, item_keep_ref, item_send_ref)
+
+
+def user_kernel(item_pairs, user_hot, grad_ref, user_keep_ref, user_send_ref, user_terms):
+    for at in range(0, user_hot.shape[1], TILE):
+        pair_gradients(grad_ref, item_pairs, user_terms, slice(at, at + TILE), lambda c, k: c * COMPS + k)
     collect(user_hot, user_terms, user_keep_ref, user_send_ref)
-
-
-def item_kernel(user_pairs, item_hot, grad_ref, item_keep_ref, item_send_ref, item_terms):
-    for at in range(0, item_hot.shape[1], TILE):
-        pair_gradients(grad_ref, user_pairs, item_terms, slice(at, at + TILE), lambda k, c: c * COMPS + k)
-    collect(item_hot, item_terms, item_keep_ref, item_send_ref)
 
 
 def shape(rows, columns, kind):
@@ -282,14 +287,14 @@
 
     (ready,) = call(ready_kernel, [shape(8, 128, F32)], [], [], 1, 8.0)
     users = user_comps
-    for step in round_steps(n_item):
+    for step in round_steps(n_item, 0):
         users = gather_round(users, "item", step)
     (items,) = call(project_kernel, [shape(item_text.shape[0], width, BF16)], [], [item_text, item_proj, ready], 8, 2.0)
-    for step in round_steps(n_user):
+    for step in round_steps(n_user, 1):
         items = gather_round(items, "user", step)
 
-    user_pairs, user_hot, item_hot, w_in_fwd, w_out_fwd, w_in_bwd, w_out_bwd, target = call(
-        functools.partial(user_kernel, (n_user, n_item)),
+    item_pairs, user_hot, item_hot, w_in_fwd, w_out_fwd, w_in_bwd, w_out_bwd, target = call(
+        functools.partial(item_kernel, (n_user, n_item)),
         [
             shape(width, pairs, F32),
             shape(user_rows, pairs, BF16),
@@ -302,7 +307,7 @@
         ],
         [],
         [
-            users,
+            items,
             w_in,
             b_in.reshape(1, -1),
             w_out,
@@ -314,33 +319,34 @@
         12,
         1.5,
     )
-    user_keep, user_send, grads = call(
+    item_keep, item_send, grads = call(
         functools.partial(pair_kernel, loss_scale),
-        [shape(user_rows // 2, width, F32), shape(user_rows // 2, width, BF16), shape(gates, pairs, F32)],
+        [shape(item_rows // 2, width, F32), shape(item_rows // 2, width, BF16), shape(gates, pairs, F32)],
         [shape(width, pairs, F32), shape(gates, pairs, F32), shape(width, pairs, BF16)],
-        [items, user_pairs, user_hot, item_hot, w_in_fwd, w_out_fwd, w_in_bwd, w_out_bwd, target],
+        [users, item_pairs, user_hot, item_hot, w_in_fwd, w_out_fwd, w_in_bwd, w_out_bwd, target],
         20,
         4.5,
     )
-    item_keep, item_send = call(
-        item_kernel,
-        [shape(item_rows // 2, width, F32), shape(item_rows // 2, width, BF16)],
+    user_keep, user_send = call(
+        user_kernel,
+        [shape(user_rows // 2, width, F32), shape(user_rows // 2, width, BF16)],
         [shape(width, pairs, BF16)],
-        [user_pairs, item_hot, grads],
+        [item_pairs, user_hot, grads],
         12,
         2.0,
     )
 
-    def scatter(keep, send, axis):
-        steps = round_steps(lax.axis_size(axis))[::-1]
+    def scatter(keep, send, axis, crossed):
+        steps = round_steps(lax.axis_size(axis), crossed)[::-1]
         for at, step in enumerate(steps):
-            total = keep + exchange(send, axis, step).astype(F32)
+            got = exchange(send, axis, step)
+            total = keep + got.astype(F32)
             if at + 1 < len(steps):
                 half = total.shape[0] // 2
                 keep, send = total[:half], total[half:].astype(BF16)
         return total
 
-    return scatter(user_keep, user_send, "item"), scatter(item_keep, item_send, "user")
+    return scatter(user_keep, user_send, "item", 0), scatter(item_keep, item_send, "user", 1)
 
 
 def solution(mesh):

time: 33.3 us -> 33 us (level)
  starting transfers between devices: 15.6 us -> 14.9 us
    ppermute x10, starting transfers between devices: 15.6 us -> 14.9 us  [exchange(): return lax.ppermute(value, axis, [(i, i ^ step) for i in range(size)])]
  transfers between devices with their start and end apart: 10 -> 10, of which waited for: 6 -> 5; matrix products, arithmetic and copies ran while one was open for 3% -> 3% of each run, Pallas kernels for 2% -> 5%
where the time goes in v3:
time: 33 us; the launch traced here: 32.8 us
  starting transfers between devices  14.9 us (45%)
  Pallas kernels  7.24 us (22%)
  waiting for transfers between devices  7.01 us (21%)
  other arithmetic  1.39 us (4%)
  local copies, waits for them, and re-layouts  1.36 us (4%)
  between operations  0.86 us (3%)
    ppermute x10, starting transfers between devices, exchange(): return lax.ppermute(value, axis, [(i, i ^ step) for i in range(size)])  14.9 us
    pallas_call x5, Pallas kernels, call(): pl.pallas_call(kernel, out_shape=outputs, in_specs=[VMEM] * len(arguments...  7.24 us
    ppermute x10, waiting for transfers between devices, exchange(): return lax.ppermute(value, axis, [(i, i ^ step) for i in range(size)])  7.01 us
    add x5, other arithmetic, scatter(): total = keep + got.astype(F32)  1.34 us
    unnamed x21, local copies, waits for them, and re-layouts  1.33 us
  transfers between devices with their start and end apart: 10, of which 5 were waited for; matrix products, arithmetic and copies ran while one was open for 3% of the time, Pallas kernels for 5%

profile of v3, /device:TPU:0, one launch (start us, length us, event | category | flops | bytes accessed | tf_op | source)
XLA Modules:
  0.0 32.8 jit_solution(880944311314419680)
XLA Ops:
  0.6 0.0 copy-start
  0.6 0.0 copy-start.1
  0.7 1.2 %copy-done = bf16[1024,512]{1,0:T(8,128)(2,1)S(1)} copy-done((bf16[1024,512]{1,0:T(8,128)(2,1)S(1)}, bf16[1024,512]{1,0:T(8,128)(2,1)}, u32[]{:S(2)}) %copy-start) | copy-done | bytes 1048600
  1.9 0.0 copy-done.1
  1.9 0.0 copy-start.8
  1.9 0.0 copy-start.9
  1.9 0.0 copy-start.2
  1.9 0.0 copy-start.3
  1.9 0.0 copy-start.4
  1.9 0.0 copy-start.5
  1.9 0.0 copy-start.6
  1.9 0.0 copy-start.7
  1.9 0.5 %shard_map.114 = bf16[32,512]{1,0:T(8,128)(2,1)S(1)} custom-call(bf16[32,1024]{1,0:T(8,128)(2,1)S(1)} %copy-done.1, bf16[1024,512]{1,0:T(8,128)(2,1)S(1)} %copy-done, f32[8,128]{1,0:T(8,128)S(1)} %shard_map.113.ready_ref), custom_call_target="tpu_custom_call" | custom-call | flops 1000000000 | bytes 6000000 | tf_op jit(solution)/shard_map/pallas_call | solution.py:266
  2.4 2.5 %collective-permute-start = (bf16[32,512]{1,0:T(8,128)(2,1)S(1)}, bf16[32,512]{1,0:T(8,128)(2,1)S(1)}, u32[]{:S(2)}, u32[]{:S(2)}) collective-permute-start(bf16[32,512]{1,0:T(8,128)(2,1)S(1)} %shard_map.114), channel_id=1, source_target_pairs={{0,12},{4,8},{8,4},{12,0},{16,28},{20,24},{24,20},{28,16},{1,13},{... | collective-permute-start | bytes 98312 | tf_op jit(solution)/shard_map/ppermute | solution.py:28
  4.9 0.0 copy-done.8
  4.9 2.6 %collective-permute-start.3 = (bf16[32,512]{1,0:T(8,128)(2,1)S(1)}, bf16[32,512]{1,0:T(8,128)(2,1)S(1)}, u32[]{:S(2)}, u32[]{:S(2)}) collective-permute-start(bf16[32,512]{1,0:T(8,128)(2,1)S(1)} %copy-done.8), channel_id=1, source_target_pairs={{0,2},{1,3},{2,0},{3,1},{4,6},{5,7},{6,4},{7,5},{8,10},{9,11},{10,... | collective-permute-start | bytes 98312 | tf_op jit(solution)/shard_map/ppermute | solution.py:28
  7.5 0.0 collective-permute-done
  7.5 1.6 %collective-permute-start.1 = (bf16[64,512]{1,0:T(8,128)(2,1)S(1)}, bf16[64,512]{1,0:T(8,128)(2,1)S(1)}, u32[]{:S(2)}, u32[]{:S(2)}) collective-permute-start(bf16[64,512]{1,0:T(8,128)(2,1)S(1)} %pad_maximum_fusion.3), channel_id=1, source_target_pairs={{0,20},{4,16},{8,28},{12,24},{16,4},{20,0},{24,12},{28,8},{1,21},{... | collective-permute-start | bytes 196616 | tf_op jit(solution)/shard_map/ppermute | solution.py:28
  9.1 0.7 %collective-permute-done.3 = bf16[32,512]{1,0:T(8,128)(2,1)S(1)} collective-permute-done((bf16[32,512]{1,0:T(8,128)(2,1)S(1)}, bf16[32,512]{1,0:T(8,128)(2,1)S(1)}, u32[]{:S(2)}, u32[]{:S(2)}) %collective-permute-start.3) | collective-permute-done | bytes 32800 | tf_op jit(solution)/shard_map/ppermute | solution.py:28
  9.8 1.6 %collective-permute-start.4 = (bf16[64,512]{1,0:T(8,128)(2,1)S(1)}, bf16[64,512]{1,0:T(8,128)(2,1)S(1)}, u32[]{:S(2)}, u32[]{:S(2)}) collective-permute-start(bf16[64,512]{1,0:T(8,128)(2,1)S(1)} %pad_maximum_fusion.4), channel_id=1, source_target_pairs={{0,1},{1,0},{2,3},{3,2},{4,5},{5,4},{6,7},{7,6},{8,9},{9,8},{10,11... | collective-permute-start | bytes 196616 | tf_op jit(solution)/shard_map/ppermute | solution.py:28
  11.4 0.0 collective-permute-done.1
  11.4 0.5 %collective-permute-start.2 = (bf16[128,512]{1,0:T(8,128)(2,1)S(1)}, bf16[128,512]{1,0:T(8,128)(2,1)S(1)}, u32[]{:S(2)}, u32[]{:S(2)}) collective-permute-start(bf16[128,512]{1,0:T(8,128)(2,1)S(1)} %pad_maximum_fusion.1), channel_id=1, source_target_pairs={{0,4},{4,0},{8,12},{12,8},{16,20},{20,16},{24,28},{28,24},{1,5},{5... | collective-permute-start | bytes 393224 | tf_op jit(solution)/shard_map/ppermute | solution.py:28
  11.9 0.0 copy-done.9
  11.9 0.1 copy.12.w_out_ref
  12.0 2.1 %collective-permute-done.4 = bf16[64,512]{1,0:T(8,128)(2,1)S(1)} collective-permute-done((bf16[64,512]{1,0:T(8,128)(2,1)S(1)}, bf16[64,512]{1,0:T(8,128)(2,1)S(1)}, u32[]{:S(2)}, u32[]{:S(2)}) %collective-permute-start.4) | collective-permute-done | bytes 65568 | tf_op jit(solution)/shard_map/ppermute | solution.py:28
  14.1 0.0 collective-permute-done.2
  14.1 0.0 copy-done.2
  14.1 0.0 copy-done.3
  14.1 0.0 copy-done.4
  14.1 0.0 copy-done.5
  14.1 0.0 copy-done.6
  14.2 0.0 copy-done.7
  14.2 0.5 %shard_map.115 = (f32[512,1024]{1,0:T(8,128)S(1)}, bf16[128,1024]{1,0:T(8,128)(2,1)S(1)}, bf16[256,1024]{1,0:T(8,128)(2,1)S(1)}, bf16[128,208]{1,0:T(8,128)(2,1)...) custom-call(bf16[256,512]{1,0:T(8,128)(2,1)S(1)} %pad_maximum_fusion, ...), custom_call_target="tpu_custom_call" | custom-call | flops 750000000 | bytes 4500000 | tf_op jit(solution)/shard_map/pallas_call | solution.py:266
  14.7 4.5 %shard_map.116 = (f32[128,512]{1,0:T(8,128)S(1)}, bf16[128,512]{1,0:T(8,128)(2,1)S(1)}, f32[64,1024]{1,0:T(8,128)S(1)}) custom-call(bf16[128,512]{1,0:T(8,128)(2,1)S(1)} %pad_maximum_fusion.2.users_ref, f32[512,1024]{1,0:T(8,128)S(1)} %get-tuple-element.15.item_pairs, bf16[128,1024]{1,0:T(8,128)(2,1)S(1)} %get-tuple-element.16.user_hot, ...), custom_call_target="tpu_custom_call" | custom-call | flops 2249999872 | bytes 13500000 | tf_op jit(solution)/shard_map/pallas_call | solution.py:266
  19.3 0.1 collective-permute-start.7
  19.3 1.6 %shard_map.117 = (f32[64,512]{1,0:T(8,128)S(1)}, bf16[64,512]{1,0:T(8,128)(2,1)S(1)}) custom-call(f32[512,1024]{1,0:T(8,128)S(1)} %get-tuple-element.15.item_pairs, bf16[128,1024]{1,0:T(8,128)(2,1)S(1)} %get-tuple-element.16.user_hot, f32[64,1024]{1,0:T(8,128)S(1)} %get-tuple-element.23.grad_ref), custom_call_target="tpu_custom_call" | custom-call | flops 1000000000 | bytes 6000000 | tf_op jit(solution)/shard_map/pallas_call | solution.py:266
  21.0 1.6 %collective-permute-start.5 = (bf16[64,512]{1,0:T(8,128)(2,1)S(1)}, bf16[64,512]{1,0:T(8,128)(2,1)S(1)}, u32[]{:S(2)}, u32[]{:S(2)}) collective-permute-start(bf16[64,512]{1,0:T(8,128)(2,1)S(1)} %get-tuple-element.25), channel_id=1, source_target_pairs={{0,1},{1,0},{2,3},{3,2},{4,5},{5,4},{6,7},{7,6},{8,9},{9,8},{10,11... | collective-permute-start | bytes 196616 | tf_op jit(solution)/shard_map/ppermute | solution.py:28
  22.6 0.0 collective-permute-done.7
  22.7 1.4 %collective-permute-start.8 = (bf16[64,512]{1,0:T(8,128)(2,1)S(1)}, bf16[64,512]{1,0:T(8,128)(2,1)S(1)}, u32[]{:S(2)}, u32[]{:S(2)}) collective-permute-start(bf16[64,512]{1,0:T(8,128)(2,1)S(1)} %slice.39), channel_id=1, source_target_pairs={{0,20},{4,16},{8,28},{12,24},{16,4},{20,0},{24,12},{28,8},{1,21},{... | collective-permute-start | bytes 196616 | tf_op jit(solution)/shard_map/ppermute | solution.py:28
  24.1 1.4 %collective-permute-done.5 = bf16[64,512]{1,0:T(8,128)(2,1)S(1)} collective-permute-done((bf16[64,512]{1,0:T(8,128)(2,1)S(1)}, bf16[64,512]{1,0:T(8,128)(2,1)S(1)}, u32[]{:S(2)}, u32[]{:S(2)}) %collective-permute-start.5) | collective-permute-done | bytes 65568 | tf_op jit(solution)/shard_map/ppermute | solution.py:28
  25.6 3.1 %collective-permute-start.6 = (bf16[32,512]{1,0:T(8,128)(2,1)S(1)}, bf16[32,512]{1,0:T(8,128)(2,1)S(1)}, u32[]{:S(2)}, u32[]{:S(2)}) collective-permute-start(bf16[32,512]{1,0:T(8,128)(2,1)S(1)} %slice.41), channel_id=1, source_target_pairs={{0,2},{1,3},{2,0},{3,1},{4,6},{5,7},{6,4},{7,5},{8,10},{9,11},{10,... | collective-permute-start | bytes 98312 | tf_op jit(solution)/shard_map/ppermute | solution.py:28
  28.7 0.0 collective-permute-done.8
  28.7 0.1 collective-permute-start.9
  28.8 2.1 %collective-permute-done.6 = bf16[32,512]{1,0:T(8,128)(2,1)S(1)} collective-permute-done((bf16[32,512]{1,0:T(8,128)(2,1)S(1)}, bf16[32,512]{1,0:T(8,128)(2,1)S(1)}, u32[]{:S(2)}, u32[]{:S(2)}) %collective-permute-start.6) | collective-permute-done | bytes 32800 | tf_op jit(solution)/shard_map/ppermute | solution.py:28
  30.9 0.6 %slice_add_fusion.2 = f32[32,512]{1,0:T(8,128)} fusion(f32[64,512]{1,0:T(8,128)S(1)} %convert_add_fusion.1, bf16[32,512]{1,0:T(8,128)(2,1)S(1)} %collective-permute-done.6), kind=kLoop, calls=%fused_computation.10 | loop fusion | flops 32768 | bytes 163840 | tf_op jit(solution)/shard_map/add | solution.py:343
  31.5 0.6 %collective-permute-done.9 = bf16[32,512]{1,0:T(8,128)(2,1)S(1)} collective-permute-done((bf16[32,512]{1,0:T(8,128)(2,1)S(1)}, bf16[32,512]{1,0:T(8,128)(2,1)S(1)}, u32[]{:S(2)}, u32[]{:S(2)}) %collective-permute-start.9) | collective-permute-done | bytes 32800 | tf_op jit(solution)/shard_map/ppermute | solution.py:28
  32.2 0.6 %slice_add_fusion.1 = f32[32,512]{1,0:T(8,128)} fusion(f32[64,512]{1,0:T(8,128)S(1)} %slice_add_fusion, bf16[32,512]{1,0:T(8,128)(2,1)S(1)} %collective-permute-done.9), kind=kLoop, calls=%fused_computation.8 | loop fusion | flops 32768 | bytes 163840 | tf_op jit(solution)/shard_map/add | solution.py:343
  (12 shorter events, 0.1 us)
Async XLA Ops:
  0.6 1.2 %copy-start = (bf16[1024,512]{1,0:T(8,128)(2,1)S(1)}, bf16[1024,512]{1,0:T(8,128)(2,1)}, u32[]{:S(2)}) copy-start(bf16[1024,512]{1,0:T(8,128)(2,1)} %proj_ref.1) | copy-start | bytes 3145732
  0.6 1.2 %copy-start.1 = (bf16[32,1024]{1,0:T(8,128)(2,1)S(1)}, bf16[32,1024]{1,0:T(8,128)(2,1)}, u32[]{:S(2)}) copy-start(bf16[32,1024]{1,0:T(8,128)(2,1)} %text_ref.1) | copy-start | bytes 196612
  1.9 3.0 %copy-start.8 = (bf16[32,512]{1,0:T(8,128)(2,1)S(1)}, bf16[32,512]{1,0:T(8,128)(2,1)}, u32[]{:S(2)}) copy-start(bf16[32,512]{1,0:T(8,128)(2,1)} %param.10) | copy-start | bytes 98308
  1.9 10.0 %copy-start.9 = (f32[128,64]{0,1:T(8,128)S(1)}, f32[128,64]{0,1:T(8,128)}, u32[]{:S(2)}) copy-start(f32[128,64]{0,1:T(8,128)} %param.15) | copy-start | bytes 98308
  1.9 12.2 %copy-start.2 = (f32[64,128]{1,0:T(8,128)S(1)}, f32[64,128]{1,0:T(8,128)}, u32[]{:S(2)}) copy-start(f32[64,128]{1,0:T(8,128)} %w_in_ref.1) | copy-start | bytes 98308
  1.9 12.2 %copy-start.3 = (s32[1024]{0:T(1024)S(1)}, s32[1024]{0:T(1024)}, u32[]{:S(2)}) copy-start(s32[1024]{0:T(1024)} %param.17) | copy-start | bytes 12292
  1.9 12.2 %copy-start.4 = (s32[1024]{0:T(1024)S(1)}, s32[1024]{0:T(1024)}, u32[]{:S(2)}) copy-start(s32[1024]{0:T(1024)} %param.18) | copy-start | bytes 12292
  1.9 12.2 %copy-start.5 = (f32[1024]{0:T(1024)S(1)}, f32[1024]{0:T(1024)}, u32[]{:S(2)}) copy-start(f32[1024]{0:T(1024)} %param.19) | copy-start | bytes 12292
  1.9 12.2 %copy-start.6 = (f32[128]{0:T(128)S(1)}, f32[128]{0:T(128)}, u32[]{:S(2)}) copy-start(f32[128]{0:T(128)} %param.14) | copy-start | bytes 1540
  1.9 12.2 %copy-start.7 = (f32[64]{0:T(128)S(1)}, f32[64]{0:T(128)}, u32[]{:S(2)}) copy-start(f32[64]{0:T(128)} %param.16) | copy-start | bytes 772
  2.4 5.1 %collective-permute-start = (bf16[32,512]{1,0:T(8,128)(2,1)S(1)}, bf16[32,512]{1,0:T(8,128)(2,1)S(1)}, u32[]{:S(2)}, u32[]{:S(2)}) collective-permute-start(bf16[32,512]{1,0:T(8,128)(2,1)S(1)} %shard_map.114), channel_id=1, source_target_pairs={{0,12},{4,8},{8,4},{12,0},{16,28},{20,24},{24,20},{28,16},{1,13},{... | collective-permute-start | bytes 98312 | tf_op jit(solution)/shard_map/ppermute | solution.py:28
  4.9 4.9 %collective-permute-start.3 = (bf16[32,512]{1,0:T(8,128)(2,1)S(1)}, bf16[32,512]{1,0:T(8,128)(2,1)S(1)}, u32[]{:S(2)}, u32[]{:S(2)}) collective-permute-start(bf16[32,512]{1,0:T(8,128)(2,1)S(1)} %copy-done.8), channel_id=1, source_target_pairs={{0,2},{1,3},{2,0},{3,1},{4,6},{5,7},{6,4},{7,5},{8,10},{9,11},{10,... | collective-permute-start | bytes 98312 | tf_op jit(solution)/shard_map/ppermute | solution.py:28
  7.5 3.9 %collective-permute-start.1 = (bf16[64,512]{1,0:T(8,128)(2,1)S(1)}, bf16[64,512]{1,0:T(8,128)(2,1)S(1)}, u32[]{:S(2)}, u32[]{:S(2)}) collective-permute-start(bf16[64,512]{1,0:T(8,128)(2,1)S(1)} %pad_maximum_fusion.3), channel_id=1, source_target_pairs={{0,20},{4,16},{8,28},{12,24},{16,4},{20,0},{24,12},{28,8},{1,21},{... | collective-permute-start | bytes 196616 | tf_op jit(solution)/shard_map/ppermute | solution.py:28
  9.8 4.3 %collective-permute-start.4 = (bf16[64,512]{1,0:T(8,128)(2,1)S(1)}, bf16[64,512]{1,0:T(8,128)(2,1)S(1)}, u32[]{:S(2)}, u32[]{:S(2)}) collective-permute-start(bf16[64,512]{1,0:T(8,128)(2,1)S(1)} %pad_maximum_fusion.4), channel_id=1, source_target_pairs={{0,1},{1,0},{2,3},{3,2},{4,5},{5,4},{6,7},{7,6},{8,9},{9,8},{10,11... | collective-permute-start | bytes 196616 | tf_op jit(solution)/shard_map/ppermute | solution.py:28
  11.4 2.7 %collective-permute-start.2 = (bf16[128,512]{1,0:T(8,128)(2,1)S(1)}, bf16[128,512]{1,0:T(8,128)(2,1)S(1)}, u32[]{:S(2)}, u32[]{:S(2)}) collective-permute-start(bf16[128,512]{1,0:T(8,128)(2,1)S(1)} %pad_maximum_fusion.1), channel_id=1, source_target_pairs={{0,4},{4,0},{8,12},{12,8},{16,20},{20,16},{24,28},{28,24},{1,5},{5... | collective-permute-start | bytes 393224 | tf_op jit(solution)/shard_map/ppermute | solution.py:28
  19.3 3.4 %collective-permute-start.7 = (bf16[128,512]{1,0:T(8,128)(2,1)S(1)}, bf16[128,512]{1,0:T(8,128)(2,1)S(1)}, u32[]{:S(2)}, u32[]{:S(2)}) collective-permute-start(bf16[128,512]{1,0:T(8,128)(2,1)S(1)} %get-tuple-element.27), channel_id=1, source_target_pairs={{0,4},{4,0},{8,12},{12,8},{16,20},{20,16},{24,28},{28,24},{1,5},{5... | collective-permute-start | bytes 393224 | tf_op jit(solution)/shard_map/ppermute | solution.py:28
  21.0 4.6 %collective-permute-start.5 = (bf16[64,512]{1,0:T(8,128)(2,1)S(1)}, bf16[64,512]{1,0:T(8,128)(2,1)S(1)}, u32[]{:S(2)}, u32[]{:S(2)}) collective-permute-start(bf16[64,512]{1,0:T(8,128)(2,1)S(1)} %get-tuple-element.25), channel_id=1, source_target_pairs={{0,1},{1,0},{2,3},{3,2},{4,5},{5,4},{6,7},{7,6},{8,9},{9,8},{10,11... | collective-permute-start | bytes 196616 | tf_op jit(solution)/shard_map/ppermute | solution.py:28
  22.7 6.0 %collective-permute-start.8 = (bf16[64,512]{1,0:T(8,128)(2,1)S(1)}, bf16[64,512]{1,0:T(8,128)(2,1)S(1)}, u32[]{:S(2)}, u32[]{:S(2)}) collective-permute-start(bf16[64,512]{1,0:T(8,128)(2,1)S(1)} %slice.39), channel_id=1, source_target_pairs={{0,20},{4,16},{8,28},{12,24},{16,4},{20,0},{24,12},{28,8},{1,21},{... | collective-permute-start | bytes 196616 | tf_op jit(solution)/shard_map/ppermute | solution.py:28
  25.6 5.3 %collective-permute-start.6 = (bf16[32,512]{1,0:T(8,128)(2,1)S(1)}, bf16[32,512]{1,0:T(8,128)(2,1)S(1)}, u32[]{:S(2)}, u32[]{:S(2)}) collective-permute-start(bf16[32,512]{1,0:T(8,128)(2,1)S(1)} %slice.41), channel_id=1, source_target_pairs={{0,2},{1,3},{2,0},{3,1},{4,6},{5,7},{6,4},{7,5},{8,10},{9,11},{10,... | collective-permute-start | bytes 98312 | tf_op jit(solution)/shard_map/ppermute | solution.py:28
  28.7 3.5 %collective-permute-start.9 = (bf16[32,512]{1,0:T(8,128)(2,1)S(1)}, bf16[32,512]{1,0:T(8,128)(2,1)S(1)}, u32[]{:S(2)}, u32[]{:S(2)}) collective-permute-start(bf16[32,512]{1,0:T(8,128)(2,1)S(1)} %slice.40), channel_id=1, source_target_pairs={{0,12},{4,8},{8,4},{12,0},{16,28},{20,24},{24,20},{28,16},{1,13},{... | collective-permute-start | bytes 98312 | tf_op jit(solution)/shard_map/ppermute | solution.py:28

commit v4 on v3

--- a/solution.py
+++ b/solution.py
@@ -90,23 +90,19 @@
 
 def fold_rows(parts):
     place = lax.broadcasted_iota(jnp.int32, parts[0].shape, 0)
-    width = 4
-    while len(parts) > 1:
-        low = (place & width) == 0
-        half = len(parts) // 2
-        merged = []
-        for at in range(half):
-            one, two = parts[at], parts[at + half]
-            stay = jnp.where(low, one, two)
-            move = jnp.where(low, two, one)
-            merged.append(stay + pltpu.roll(move, width, 0) if width == 4 else stay + shift_rows(move, width, low))
-        parts = merged
-        width //= 2
-    return parts[0]
-
-
-def shift_rows(value, width, low):
-    return jnp.where(low, pltpu.roll(value, 8 - width, 0), pltpu.roll(value, width, 0))
+
+    def merge(one, two, start, width):
+        mine = ((place - start) & (2 * width - 1)) < width
+        stay = jnp.where(mine, two, one)
+        move = jnp.where(mine, one, two)
+        return stay + pltpu.roll(move, width, 0)
+
+    def quad(shift):
+        first = merge(parts[(7 + shift) % 8], parts[(3 + shift) % 8], shift, 4)
+        second = merge(parts[(1 + shift) % 8], parts[(5 + shift) % 8], 2 + shift, 4)
+        return merge(first, second, 4 + shift, 2)
+
+    return merge(quad(0), quad(1), 0, 1)
 
 
 def dot(one, two):
@@ -211,16 +207,21 @@
 
     def make_logits(block):
         for span in spans(block):
-            for c in range(COMPS):
-                parts = []
+            for c in range(0, COMPS, 2):
+                parts = [[], []]
                 for k in range(COMPS):
-                    total = None
+                    total = [None, None]
                     for j in range(CDIM // 8):
-                        u = user_pairs[c * CDIM + j * 8 : c * CDIM + (j + 1) * 8, span]
                         v = item_pairs[k * CDIM + j * 8 : k * CDIM + (j + 1) * 8, span]
-                        total = u * v if total is None else total + u * v
-                    parts.append(total)
-                logits_ref[c * COMPS : (c + 1) * COMPS, span] = fold_rows(parts) * scale
+                        for at in range(2):
+                            row = (c + at) * CDIM + j * 8
+                            term = user_pairs[row : row + 8, span] * v
+                            total[at] = term if total[at] is None else total[at] + term
+                    for at in range(2):
+                        parts[at].append(total[at])
+                for at in range(2):
+                    row = (c + at) * COMPS
+                    logits_ref[row : row + COMPS, span] = fold_rows(parts[at]) * scale
 
     def gate(block):
         lanes = slice(block * WIDE, (block + 1) * WIDE)
@@ -244,7 +245,9 @@
         for span in spans(block):
             pair_gradients(grad_ref, user_pairs, item_terms, span, lambda k, c: c * COMPS + k)
 
-    stages = (gather, make_logits, gate, gradients)
+    for block in range(blocks):
+        gather(block)
+    stages = (make_logits, gate, gradients)
     for step in range(blocks + len(stages) - 1):
         for at, stage in enumerate(stages):
             if 0 <= step - at < blocks:

time: 33 us -> 32.5 us (0.985)
  Pallas kernels: 7.24 us -> 6.76 us
    pallas_call x5, Pallas kernels: 7.24 us -> 6.76 us  [call(): pl.pallas_call(kernel, out_shape=outputs, in_specs=[VMEM] * len(arguments...]
where the time goes in v4:
time: 32.5 us; the launch traced here: 32.3 us
  starting transfers between devices  14.9 us (46%)
  waiting for transfers between devices  7.02 us (22%)
  Pallas kernels  6.76 us (21%)
  other arithmetic  1.39 us (4%)
  local copies, waits for them, and re-layouts  1.36 us (4%)
  between operations  0.86 us (3%)
    ppermute x10, starting transfers between devices, exchange(): return lax.ppermute(value, axis, [(i, i ^ step) for i in range(size)])  14.9 us
    ppermute x10, waiting for transfers between devices, exchange(): return lax.ppermute(value, axis, [(i, i ^ step) for i in range(size)])  7.02 us
    pallas_call x5, Pallas kernels, call(): pl.pallas_call(kernel, out_shape=outputs, in_specs=[VMEM] * len(arguments...  6.76 us
    add x5, other arithmetic, scatter(): total = keep + got.astype(F32)  1.34 us
    unnamed x21, local copies, waits for them, and re-layouts  1.33 us
  transfers between devices with their start and end apart: 10, of which 5 were waited for; matrix products, arithmetic and copies ran while one was open for 3% of the time, Pallas kernels for 5%

profile of v4, /device:TPU:0, one launch (start us, length us, event | category | flops | bytes accessed | tf_op | source)
XLA Modules:
  0.0 32.3 jit_solution(11615085477110032349)
XLA Ops:
  0.6 0.0 copy-start
  0.6 0.0 copy-start.1
  0.7 1.2 %copy-done = bf16[1024,512]{1,0:T(8,128)(2,1)S(1)} copy-done((bf16[1024,512]{1,0:T(8,128)(2,1)S(1)}, bf16[1024,512]{1,0:T(8,128)(2,1)}, u32[]{:S(2)}) %copy-start) | copy-done | bytes 1048600
  1.9 0.0 copy-done.1
  1.9 0.0 copy-start.8
  1.9 0.0 copy-start.9
  1.9 0.0 copy-start.2
  1.9 0.0 copy-start.3
  1.9 0.0 copy-start.4
  1.9 0.0 copy-start.5
  1.9 0.0 copy-start.6
  1.9 0.0 copy-start.7
  1.9 0.5 %shard_map.114 = bf16[32,512]{1,0:T(8,128)(2,1)S(1)} custom-call(bf16[32,1024]{1,0:T(8,128)(2,1)S(1)} %copy-done.1, bf16[1024,512]{1,0:T(8,128)(2,1)S(1)} %copy-done, f32[8,128]{1,0:T(8,128)S(1)} %shard_map.113.ready_ref), custom_call_target="tpu_custom_call" | custom-call | flops 1000000000 | bytes 6000000 | tf_op jit(solution)/shard_map/pallas_call | solution.py:269
  2.4 2.5 %collective-permute-start = (bf16[32,512]{1,0:T(8,128)(2,1)S(1)}, bf16[32,512]{1,0:T(8,128)(2,1)S(1)}, u32[]{:S(2)}, u32[]{:S(2)}) collective-permute-start(bf16[32,512]{1,0:T(8,128)(2,1)S(1)} %shard_map.114), channel_id=1, source_target_pairs={{0,12},{4,8},{8,4},{12,0},{16,28},{20,24},{24,20},{28,16},{1,13},{... | collective-permute-start | bytes 98312 | tf_op jit(solution)/shard_map/ppermute | solution.py:28
  4.9 0.0 copy-done.8
  4.9 2.6 %collective-permute-start.3 = (bf16[32,512]{1,0:T(8,128)(2,1)S(1)}, bf16[32,512]{1,0:T(8,128)(2,1)S(1)}, u32[]{:S(2)}, u32[]{:S(2)}) collective-permute-start(bf16[32,512]{1,0:T(8,128)(2,1)S(1)} %copy-done.8), channel_id=1, source_target_pairs={{0,2},{1,3},{2,0},{3,1},{4,6},{5,7},{6,4},{7,5},{8,10},{9,11},{10,... | collective-permute-start | bytes 98312 | tf_op jit(solution)/shard_map/ppermute | solution.py:28
  7.5 0.0 collective-permute-done
  7.5 1.6 %collective-permute-start.1 = (bf16[64,512]{1,0:T(8,128)(2,1)S(1)}, bf16[64,512]{1,0:T(8,128)(2,1)S(1)}, u32[]{:S(2)}, u32[]{:S(2)}) collective-permute-start(bf16[64,512]{1,0:T(8,128)(2,1)S(1)} %pad_maximum_fusion.3), channel_id=1, source_target_pairs={{0,20},{4,16},{8,28},{12,24},{16,4},{20,0},{24,12},{28,8},{1,21},{... | collective-permute-start | bytes 196616 | tf_op jit(solution)/shard_map/ppermute | solution.py:28
  9.1 0.7 %collective-permute-done.3 = bf16[32,512]{1,0:T(8,128)(2,1)S(1)} collective-permute-done((bf16[32,512]{1,0:T(8,128)(2,1)S(1)}, bf16[32,512]{1,0:T(8,128)(2,1)S(1)}, u32[]{:S(2)}, u32[]{:S(2)}) %collective-permute-start.3) | collective-permute-done | bytes 32800 | tf_op jit(solution)/shard_map/ppermute | solution.py:28
  9.8 1.6 %collective-permute-start.4 = (bf16[64,512]{1,0:T(8,128)(2,1)S(1)}, bf16[64,512]{1,0:T(8,128)(2,1)S(1)}, u32[]{:S(2)}, u32[]{:S(2)}) collective-permute-start(bf16[64,512]{1,0:T(8,128)(2,1)S(1)} %pad_maximum_fusion.4), channel_id=1, source_target_pairs={{0,1},{1,0},{2,3},{3,2},{4,5},{5,4},{6,7},{7,6},{8,9},{9,8},{10,11... | collective-permute-start | bytes 196616 | tf_op jit(solution)/shard_map/ppermute | solution.py:28
  11.4 0.0 collective-permute-done.1
  11.4 0.5 %collective-permute-start.2 = (bf16[128,512]{1,0:T(8,128)(2,1)S(1)}, bf16[128,512]{1,0:T(8,128)(2,1)S(1)}, u32[]{:S(2)}, u32[]{:S(2)}) collective-permute-start(bf16[128,512]{1,0:T(8,128)(2,1)S(1)} %pad_maximum_fusion.1), channel_id=1, source_target_pairs={{0,4},{4,0},{8,12},{12,8},{16,20},{20,16},{24,28},{28,24},{1,5},{5... | collective-permute-start | bytes 393224 | tf_op jit(solution)/shard_map/ppermute | solution.py:28
  11.9 0.0 copy-done.9
  11.9 0.1 copy.12.w_out_ref
  12.0 2.1 %collective-permute-done.4 = bf16[64,512]{1,0:T(8,128)(2,1)S(1)} collective-permute-done((bf16[64,512]{1,0:T(8,128)(2,1)S(1)}, bf16[64,512]{1,0:T(8,128)(2,1)S(1)}, u32[]{:S(2)}, u32[]{:S(2)}) %collective-permute-start.4) | collective-permute-done | bytes 65568 | tf_op jit(solution)/shard_map/ppermute | solution.py:28
  14.1 0.0 collective-permute-done.2
  14.1 0.0 copy-done.2
  14.1 0.0 copy-done.3
  14.1 0.0 copy-done.4
  14.1 0.0 copy-done.5
  14.1 0.0 copy-done.6
  14.2 0.0 copy-done.7
  14.2 0.5 %shard_map.115 = (f32[512,1024]{1,0:T(8,128)S(1)}, bf16[128,1024]{1,0:T(8,128)(2,1)S(1)}, bf16[256,1024]{1,0:T(8,128)(2,1)S(1)}, bf16[128,208]{1,0:T(8,128)(2,1)...) custom-call(bf16[256,512]{1,0:T(8,128)(2,1)S(1)} %pad_maximum_fusion, ...), custom_call_target="tpu_custom_call" | custom-call | flops 750000000 | bytes 4500000 | tf_op jit(solution)/shard_map/pallas_call | solution.py:269
  14.7 4.1 %shard_map.116 = (f32[128,512]{1,0:T(8,128)S(1)}, bf16[128,512]{1,0:T(8,128)(2,1)S(1)}, f32[64,1024]{1,0:T(8,128)S(1)}) custom-call(bf16[128,512]{1,0:T(8,128)(2,1)S(1)} %pad_maximum_fusion.2.users_ref, f32[512,1024]{1,0:T(8,128)S(1)} %get-tuple-element.15.item_pairs, bf16[128,1024]{1,0:T(8,128)(2,1)S(1)} %get-tuple-element.16.user_hot, ...), custom_call_target="tpu_custom_call" | custom-call | flops 2249999872 | bytes 13500000 | tf_op jit(solution)/shard_map/pallas_call | solution.py:269
  18.8 0.1 collective-permute-start.7
  18.9 1.6 %shard_map.117 = (f32[64,512]{1,0:T(8,128)S(1)}, bf16[64,512]{1,0:T(8,128)(2,1)S(1)}) custom-call(f32[512,1024]{1,0:T(8,128)S(1)} %get-tuple-element.15.item_pairs, bf16[128,1024]{1,0:T(8,128)(2,1)S(1)} %get-tuple-element.16.user_hot, f32[64,1024]{1,0:T(8,128)S(1)} %get-tuple-element.23.grad_ref), custom_call_target="tpu_custom_call" | custom-call | flops 1000000000 | bytes 6000000 | tf_op jit(solution)/shard_map/pallas_call | solution.py:269
  20.5 1.6 %collective-permute-start.5 = (bf16[64,512]{1,0:T(8,128)(2,1)S(1)}, bf16[64,512]{1,0:T(8,128)(2,1)S(1)}, u32[]{:S(2)}, u32[]{:S(2)}) collective-permute-start(bf16[64,512]{1,0:T(8,128)(2,1)S(1)} %get-tuple-element.25), channel_id=1, source_target_pairs={{0,1},{1,0},{2,3},{3,2},{4,5},{5,4},{6,7},{7,6},{8,9},{9,8},{10,11... | collective-permute-start | bytes 196616 | tf_op jit(solution)/shard_map/ppermute | solution.py:28
  22.1 0.0 collective-permute-done.7
  22.2 1.4 %collective-permute-start.8 = (bf16[64,512]{1,0:T(8,128)(2,1)S(1)}, bf16[64,512]{1,0:T(8,128)(2,1)S(1)}, u32[]{:S(2)}, u32[]{:S(2)}) collective-permute-start(bf16[64,512]{1,0:T(8,128)(2,1)S(1)} %slice.39), channel_id=1, source_target_pairs={{0,20},{4,16},{8,28},{12,24},{16,4},{20,0},{24,12},{28,8},{1,21},{... | collective-permute-start | bytes 196616 | tf_op jit(solution)/shard_map/ppermute | solution.py:28
  23.6 1.4 %collective-permute-done.5 = bf16[64,512]{1,0:T(8,128)(2,1)S(1)} collective-permute-done((bf16[64,512]{1,0:T(8,128)(2,1)S(1)}, bf16[64,512]{1,0:T(8,128)(2,1)S(1)}, u32[]{:S(2)}, u32[]{:S(2)}) %collective-permute-start.5) | collective-permute-done | bytes 65568 | tf_op jit(solution)/shard_map/ppermute | solution.py:28
  25.1 3.1 %collective-permute-start.6 = (bf16[32,512]{1,0:T(8,128)(2,1)S(1)}, bf16[32,512]{1,0:T(8,128)(2,1)S(1)}, u32[]{:S(2)}, u32[]{:S(2)}) collective-permute-start(bf16[32,512]{1,0:T(8,128)(2,1)S(1)} %slice.41), channel_id=1, source_target_pairs={{0,2},{1,3},{2,0},{3,1},{4,6},{5,7},{6,4},{7,5},{8,10},{9,11},{10,... | collective-permute-start | bytes 98312 | tf_op jit(solution)/shard_map/ppermute | solution.py:28
  28.2 0.0 collective-permute-done.8
  28.2 0.1 collective-permute-start.9
  28.3 2.1 %collective-permute-done.6 = bf16[32,512]{1,0:T(8,128)(2,1)S(1)} collective-permute-done((bf16[32,512]{1,0:T(8,128)(2,1)S(1)}, bf16[32,512]{1,0:T(8,128)(2,1)S(1)}, u32[]{:S(2)}, u32[]{:S(2)}) %collective-permute-start.6) | collective-permute-done | bytes 32800 | tf_op jit(solution)/shard_map/ppermute | solution.py:28
  30.4 0.6 %slice_add_fusion.2 = f32[32,512]{1,0:T(8,128)} fusion(f32[64,512]{1,0:T(8,128)S(1)} %convert_add_fusion.1, bf16[32,512]{1,0:T(8,128)(2,1)S(1)} %collective-permute-done.6), kind=kLoop, calls=%fused_computation.10 | loop fusion | flops 32768 | bytes 163840 | tf_op jit(solution)/shard_map/add | solution.py:346
  31.1 0.6 %collective-permute-done.9 = bf16[32,512]{1,0:T(8,128)(2,1)S(1)} collective-permute-done((bf16[32,512]{1,0:T(8,128)(2,1)S(1)}, bf16[32,512]{1,0:T(8,128)(2,1)S(1)}, u32[]{:S(2)}, u32[]{:S(2)}) %collective-permute-start.9) | collective-permute-done | bytes 32800 | tf_op jit(solution)/shard_map/ppermute | solution.py:28
  31.7 0.6 %slice_add_fusion.1 = f32[32,512]{1,0:T(8,128)} fusion(f32[64,512]{1,0:T(8,128)S(1)} %slice_add_fusion, bf16[32,512]{1,0:T(8,128)(2,1)S(1)} %collective-permute-done.9), kind=kLoop, calls=%fused_computation.8 | loop fusion | flops 32768 | bytes 163840 | tf_op jit(solution)/shard_map/add | solution.py:346
  (12 shorter events, 0.1 us)
Async XLA Ops:
  0.6 1.2 %copy-start = (bf16[1024,512]{1,0:T(8,128)(2,1)S(1)}, bf16[1024,512]{1,0:T(8,128)(2,1)}, u32[]{:S(2)}) copy-start(bf16[1024,512]{1,0:T(8,128)(2,1)} %proj_ref.1) | copy-start | bytes 3145732
  0.6 1.2 %copy-start.1 = (bf16[32,1024]{1,0:T(8,128)(2,1)S(1)}, bf16[32,1024]{1,0:T(8,128)(2,1)}, u32[]{:S(2)}) copy-start(bf16[32,1024]{1,0:T(8,128)(2,1)} %text_ref.1) | copy-start | bytes 196612
  1.9 3.0 %copy-start.8 = (bf16[32,512]{1,0:T(8,128)(2,1)S(1)}, bf16[32,512]{1,0:T(8,128)(2,1)}, u32[]{:S(2)}) copy-start(bf16[32,512]{1,0:T(8,128)(2,1)} %param.10) | copy-start | bytes 98308
  1.9 10.0 %copy-start.9 = (f32[128,64]{0,1:T(8,128)S(1)}, f32[128,64]{0,1:T(8,128)}, u32[]{:S(2)}) copy-start(f32[128,64]{0,1:T(8,128)} %param.15) | copy-start | bytes 98308
  1.9 12.2 %copy-start.2 = (f32[64,128]{1,0:T(8,128)S(1)}, f32[64,128]{1,0:T(8,128)}, u32[]{:S(2)}) copy-start(f32[64,128]{1,0:T(8,128)} %w_in_ref.1) | copy-start | bytes 98308
  1.9 12.2 %copy-start.3 = (s32[1024]{0:T(1024)S(1)}, s32[1024]{0:T(1024)}, u32[]{:S(2)}) copy-start(s32[1024]{0:T(1024)} %param.17) | copy-start | bytes 12292
  1.9 12.2 %copy-start.4 = (s32[1024]{0:T(1024)S(1)}, s32[1024]{0:T(1024)}, u32[]{:S(2)}) copy-start(s32[1024]{0:T(1024)} %param.18) | copy-start | bytes 12292
  1.9 12.2 %copy-start.5 = (f32[1024]{0:T(1024)S(1)}, f32[1024]{0:T(1024)}, u32[]{:S(2)}) copy-start(f32[1024]{0:T(1024)} %param.19) | copy-start | bytes 12292
  1.9 12.2 %copy-start.6 = (f32[128]{0:T(128)S(1)}, f32[128]{0:T(128)}, u32[]{:S(2)}) copy-start(f32[128]{0:T(128)} %param.14) | copy-start | bytes 1540
  1.9 12.2 %copy-start.7 = (f32[64]{0:T(128)S(1)}, f32[64]{0:T(128)}, u32[]{:S(2)}) copy-start(f32[64]{0:T(128)} %param.16) | copy-start | bytes 772
  2.4 5.1 %collective-permute-start = (bf16[32,512]{1,0:T(8,128)(2,1)S(1)}, bf16[32,512]{1,0:T(8,128)(2,1)S(1)}, u32[]{:S(2)}, u32[]{:S(2)}) collective-permute-start(bf16[32,512]{1,0:T(8,128)(2,1)S(1)} %shard_map.114), channel_id=1, source_target_pairs={{0,12},{4,8},{8,4},{12,0},{16,28},{20,24},{24,20},{28,16},{1,13},{... | collective-permute-start | bytes 98312 | tf_op jit(solution)/shard_map/ppermute | solution.py:28
  4.9 4.9 %collective-permute-start.3 = (bf16[32,512]{1,0:T(8,128)(2,1)S(1)}, bf16[32,512]{1,0:T(8,128)(2,1)S(1)}, u32[]{:S(2)}, u32[]{:S(2)}) collective-permute-start(bf16[32,512]{1,0:T(8,128)(2,1)S(1)} %copy-done.8), channel_id=1, source_target_pairs={{0,2},{1,3},{2,0},{3,1},{4,6},{5,7},{6,4},{7,5},{8,10},{9,11},{10,... | collective-permute-start | bytes 98312 | tf_op jit(solution)/shard_map/ppermute | solution.py:28
  7.5 3.9 %collective-permute-start.1 = (bf16[64,512]{1,0:T(8,128)(2,1)S(1)}, bf16[64,512]{1,0:T(8,128)(2,1)S(1)}, u32[]{:S(2)}, u32[]{:S(2)}) collective-permute-start(bf16[64,512]{1,0:T(8,128)(2,1)S(1)} %pad_maximum_fusion.3), channel_id=1, source_target_pairs={{0,20},{4,16},{8,28},{12,24},{16,4},{20,0},{24,12},{28,8},{1,21},{... | collective-permute-start | bytes 196616 | tf_op jit(solution)/shard_map/ppermute | solution.py:28
  9.8 4.3 %collective-permute-start.4 = (bf16[64,512]{1,0:T(8,128)(2,1)S(1)}, bf16[64,512]{1,0:T(8,128)(2,1)S(1)}, u32[]{:S(2)}, u32[]{:S(2)}) collective-permute-start(bf16[64,512]{1,0:T(8,128)(2,1)S(1)} %pad_maximum_fusion.4), channel_id=1, source_target_pairs={{0,1},{1,0},{2,3},{3,2},{4,5},{5,4},{6,7},{7,6},{8,9},{9,8},{10,11... | collective-permute-start | bytes 196616 | tf_op jit(solution)/shard_map/ppermute | solution.py:28
  11.4 2.7 %collective-permute-start.2 = (bf16[128,512]{1,0:T(8,128)(2,1)S(1)}, bf16[128,512]{1,0:T(8,128)(2,1)S(1)}, u32[]{:S(2)}, u32[]{:S(2)}) collective-permute-start(bf16[128,512]{1,0:T(8,128)(2,1)S(1)} %pad_maximum_fusion.1), channel_id=1, source_target_pairs={{0,4},{4,0},{8,12},{12,8},{16,20},{20,16},{24,28},{28,24},{1,5},{5... | collective-permute-start | bytes 393224 | tf_op jit(solution)/shard_map/ppermute | solution.py:28
  18.8 3.4 %collective-permute-start.7 = (bf16[128,512]{1,0:T(8,128)(2,1)S(1)}, bf16[128,512]{1,0:T(8,128)(2,1)S(1)}, u32[]{:S(2)}, u32[]{:S(2)}) collective-permute-start(bf16[128,512]{1,0:T(8,128)(2,1)S(1)} %get-tuple-element.27), channel_id=1, source_target_pairs={{0,4},{4,0},{8,12},{12,8},{16,20},{20,16},{24,28},{28,24},{1,5},{5... | collective-permute-start | bytes 393224 | tf_op jit(solution)/shard_map/ppermute | solution.py:28
  20.5 4.6 %collective-permute-start.5 = (bf16[64,512]{1,0:T(8,128)(2,1)S(1)}, bf16[64,512]{1,0:T(8,128)(2,1)S(1)}, u32[]{:S(2)}, u32[]{:S(2)}) collective-permute-start(bf16[64,512]{1,0:T(8,128)(2,1)S(1)} %get-tuple-element.25), channel_id=1, source_target_pairs={{0,1},{1,0},{2,3},{3,2},{4,5},{5,4},{6,7},{7,6},{8,9},{9,8},{10,11... | collective-permute-start | bytes 196616 | tf_op jit(solution)/shard_map/ppermute | solution.py:28
  22.2 6.0 %collective-permute-start.8 = (bf16[64,512]{1,0:T(8,128)(2,1)S(1)}, bf16[64,512]{1,0:T(8,128)(2,1)S(1)}, u32[]{:S(2)}, u32[]{:S(2)}) collective-permute-start(bf16[64,512]{1,0:T(8,128)(2,1)S(1)} %slice.39), channel_id=1, source_target_pairs={{0,20},{4,16},{8,28},{12,24},{16,4},{20,0},{24,12},{28,8},{1,21},{... | collective-permute-start | bytes 196616 | tf_op jit(solution)/shard_map/ppermute | solution.py:28
  25.1 5.3 %collective-permute-start.6 = (bf16[32,512]{1,0:T(8,128)(2,1)S(1)}, bf16[32,512]{1,0:T(8,128)(2,1)S(1)}, u32[]{:S(2)}, u32[]{:S(2)}) collective-permute-start(bf16[32,512]{1,0:T(8,128)(2,1)S(1)} %slice.41), channel_id=1, source_target_pairs={{0,2},{1,3},{2,0},{3,1},{4,6},{5,7},{6,4},{7,5},{8,10},{9,11},{10,... | collective-permute-start | bytes 98312 | tf_op jit(solution)/shard_map/ppermute | solution.py:28
  28.2 3.5 %collective-permute-start.9 = (bf16[32,512]{1,0:T(8,128)(2,1)S(1)}, bf16[32,512]{1,0:T(8,128)(2,1)S(1)}, u32[]{:S(2)}, u32[]{:S(2)}) collective-permute-start(bf16[32,512]{1,0:T(8,128)(2,1)S(1)} %slice.40), channel_id=1, source_target_pairs={{0,12},{4,8},{8,4},{12,0},{16,28},{20,24},{24,20},{28,16},{1,13},{... | collective-permute-start | bytes 98312 | tf_op jit(solution)/shard_map/ppermute | solution.py:28

commit v5 on v4

--- a/solution.py
+++ b/solution.py
@@ -127,6 +127,7 @@
     pair_item_ref,
     teacher_ref,
     item_pairs,
+    item_short,
     user_hot,
     item_hot,
     w_in_fwd,
@@ -149,7 +150,10 @@
         lanes = slice(block * WIDE, (block + 1) * WIDE)
         hot = hot_rows(pair_item_ref[:, lanes], item_rows, n_user, me_user, 1)
         item_hot[:, lanes] = hot
-        item_pairs[:, lanes] = dot(items_t, hot)
+        rows = dot(items_t, hot)
+        item_pairs[:, lanes] = rows
+        for at in range(WIDE // TILE):
+            item_short[block * (WIDE // TILE) + at] = rows[:, at * TILE : (at + 1) * TILE].astype(BF16)
         user_hot[:, lanes] = hot_rows(pair_user_ref[:, lanes], user_rows, n_item, me_item, 0)
 
 
@@ -166,6 +170,29 @@
                 total = term if total is None else total + term
             at = one * CDIM + j * 16
             terms[at : at + 16, span] = total.astype(BF16)
+
+
+def short_gradients(grad_ref, pairs_ref, terms, tile, row):
+    span = slice(tile * TILE, (tile + 1) * TILE)
+    for first in range(0, COMPS, 1):
+        spread = [
+            [
+                jnp.broadcast_to(grad_ref[row(one, two) : row(one, two) + 1, span], (16, TILE)).astype(BF16)
+                for two in range(COMPS)
+            ]
+            for one in range(first, first + 1)
+        ]
+        for j in range(CDIM // 16):
+            values = []
+            for two in range(COMPS):
+                at = two * CDIM + j * 16
+                values.append(pairs_ref[tile, at : at + 16, :])
+            for one in range(1):
+                parts = [spread[one][two] * values[two] for two in range(COMPS)]
+                while len(parts) > 1:
+                    parts = [parts[i] + parts[i + 1] for i in range(0, len(parts), 2)]
+                at = (first + one) * CDIM + j * 16
+                terms[at : at + 16, span] = parts[0]
 
 
 def collect(hot, terms, keep_ref, send_ref):
@@ -255,9 +282,9 @@
     collect(item_hot, item_terms, item_keep_ref, item_send_ref)
 
 
-def user_kernel(item_pairs, user_hot, grad_ref, user_keep_ref, user_send_ref, user_terms):
-    for at in range(0, user_hot.shape[1], TILE):
-        pair_gradients(grad_ref, item_pairs, user_terms, slice(at, at + TILE), lambda c, k: c * COMPS + k)
+def user_kernel(item_short, user_hot, grad_ref, user_keep_ref, user_send_ref, user_terms):
+    for tile in range(user_hot.shape[1] // TILE):
+        short_gradients(grad_ref, item_short, user_terms, tile, lambda c, k: c * COMPS + k)
     collect(user_hot, user_terms, user_keep_ref, user_send_ref)
 
 
@@ -296,10 +323,11 @@
     for step in round_steps(n_user, 1):
         items = gather_round(items, "user", step)
 
-    item_pairs, user_hot, item_hot, w_in_fwd, w_out_fwd, w_in_bwd, w_out_bwd, target = call(
+    item_pairs, item_short, user_hot, item_hot, w_in_fwd, w_out_fwd, w_in_bwd, w_out_bwd, target = call(
         functools.partial(item_kernel, (n_user, n_item)),
         [
             shape(width, pairs, F32),
+            jax.ShapeDtypeStruct((pairs // TILE, width, TILE), BF16),
             shape(user_rows, pairs, BF16),
             shape(item_rows, pairs, BF16),
             shape(hidden, 3 * gates + 16, BF16),
@@ -334,7 +362,7 @@
         user_kernel,
         [shape(user_rows // 2, width, F32), shape(user_rows // 2, width, BF16)],
         [shape(width, pairs, BF16)],
-        [item_pairs, user_hot, grads],
+        [item_short, user_hot, grads],
         12,
         2.0,
     )

time: 32.5 us -> 32 us (0.985)
  Pallas kernels: 6.76 us -> 6.26 us
    pallas_call x5, Pallas kernels: 6.76 us -> 6.26 us  [call(): pl.pallas_call(kernel, out_shape=outputs, in_specs=[VMEM] * len(arguments...]
  transfers between devices with their start and end apart: 10 -> 10, of which waited for: 5 -> 5; matrix products, arithmetic and copies ran while one was open for 3% -> 3% of each run, Pallas kernels for 5% -> 4%
where the time goes in v5:
time: 32 us; the launch traced here: 31.8 us
  starting transfers between devices  14.9 us (47%)
  waiting for transfers between devices  7.02 us (22%)
  Pallas kernels  6.26 us (20%)
  other arithmetic  1.39 us (4%)
  local copies, waits for them, and re-layouts  1.36 us (4%)
  between operations  0.86 us (3%)
    ppermute x10, starting transfers between devices, exchange(): return lax.ppermute(value, axis, [(i, i ^ step) for i in range(size)])  14.9 us
    ppermute x10, waiting for transfers between devices, exchange(): return lax.ppermute(value, axis, [(i, i ^ step) for i in range(size)])  7.02 us
    pallas_call x5, Pallas kernels, call(): pl.pallas_call(kernel, out_shape=outputs, in_specs=[VMEM] * len(arguments...  6.26 us
    add x5, other arithmetic, scatter(): total = keep + got.astype(F32)  1.34 us
    unnamed x21, local copies, waits for them, and re-layouts  1.33 us
  transfers between devices with their start and end apart: 10, of which 5 were waited for; matrix products, arithmetic and copies ran while one was open for 3% of the time, Pallas kernels for 4%

profile of v5, /device:TPU:0, one launch (start us, length us, event | category | flops | bytes accessed | tf_op | source)
XLA Modules:
  0.0 31.8 jit_solution(3661985556425821021)
XLA Ops:
  0.6 0.0 copy-start
  0.6 0.0 copy-start.1
  0.7 1.2 %copy-done = bf16[1024,512]{1,0:T(8,128)(2,1)S(1)} copy-done((bf16[1024,512]{1,0:T(8,128)(2,1)S(1)}, bf16[1024,512]{1,0:T(8,128)(2,1)}, u32[]{:S(2)}) %copy-start) | copy-done | bytes 1048600
  1.9 0.0 copy-done.1
  1.9 0.0 copy-start.8
  1.9 0.0 copy-start.9
  1.9 0.0 copy-start.2
  1.9 0.0 copy-start.3
  1.9 0.0 copy-start.4
  1.9 0.0 copy-start.5
  1.9 0.0 copy-start.6
  1.9 0.0 copy-start.7
  1.9 0.5 %shard_map.114 = bf16[32,512]{1,0:T(8,128)(2,1)S(1)} custom-call(bf16[32,1024]{1,0:T(8,128)(2,1)S(1)} %copy-done.1, bf16[1024,512]{1,0:T(8,128)(2,1)S(1)} %copy-done, f32[8,128]{1,0:T(8,128)S(1)} %shard_map.113.ready_ref), custom_call_target="tpu_custom_call" | custom-call | flops 1000000000 | bytes 6000000 | tf_op jit(solution)/shard_map/pallas_call | solution.py:296
  2.4 2.5 %collective-permute-start = (bf16[32,512]{1,0:T(8,128)(2,1)S(1)}, bf16[32,512]{1,0:T(8,128)(2,1)S(1)}, u32[]{:S(2)}, u32[]{:S(2)}) collective-permute-start(bf16[32,512]{1,0:T(8,128)(2,1)S(1)} %shard_map.114), channel_id=1, source_target_pairs={{0,12},{4,8},{8,4},{12,0},{16,28},{20,24},{24,20},{28,16},{1,13},{... | collective-permute-start | bytes 98312 | tf_op jit(solution)/shard_map/ppermute | solution.py:28
  4.9 0.0 copy-done.8
  4.9 2.6 %collective-permute-start.3 = (bf16[32,512]{1,0:T(8,128)(2,1)S(1)}, bf16[32,512]{1,0:T(8,128)(2,1)S(1)}, u32[]{:S(2)}, u32[]{:S(2)}) collective-permute-start(bf16[32,512]{1,0:T(8,128)(2,1)S(1)} %copy-done.8), channel_id=1, source_target_pairs={{0,2},{1,3},{2,0},{3,1},{4,6},{5,7},{6,4},{7,5},{8,10},{9,11},{10,... | collective-permute-start | bytes 98312 | tf_op jit(solution)/shard_map/ppermute | solution.py:28
  7.5 0.0 collective-permute-done
  7.5 1.6 %collective-permute-start.1 = (bf16[64,512]{1,0:T(8,128)(2,1)S(1)}, bf16[64,512]{1,0:T(8,128)(2,1)S(1)}, u32[]{:S(2)}, u32[]{:S(2)}) collective-permute-start(bf16[64,512]{1,0:T(8,128)(2,1)S(1)} %pad_maximum_fusion.3), channel_id=1, source_target_pairs={{0,20},{4,16},{8,28},{12,24},{16,4},{20,0},{24,12},{28,8},{1,21},{... | collective-permute-start | bytes 196616 | tf_op jit(solution)/shard_map/ppermute | solution.py:28
  9.1 0.7 %collective-permute-done.3 = bf16[32,512]{1,0:T(8,128)(2,1)S(1)} collective-permute-done((bf16[32,512]{1,0:T(8,128)(2,1)S(1)}, bf16[32,512]{1,0:T(8,128)(2,1)S(1)}, u32[]{:S(2)}, u32[]{:S(2)}) %collective-permute-start.3) | collective-permute-done | bytes 32800 | tf_op jit(solution)/shard_map/ppermute | solution.py:28
  9.8 1.6 %collective-permute-start.4 = (bf16[64,512]{1,0:T(8,128)(2,1)S(1)}, bf16[64,512]{1,0:T(8,128)(2,1)S(1)}, u32[]{:S(2)}, u32[]{:S(2)}) collective-permute-start(bf16[64,512]{1,0:T(8,128)(2,1)S(1)} %pad_maximum_fusion.4), channel_id=1, source_target_pairs={{0,1},{1,0},{2,3},{3,2},{4,5},{5,4},{6,7},{7,6},{8,9},{9,8},{10,11... | collective-permute-start | bytes 196616 | tf_op jit(solution)/shard_map/ppermute | solution.py:28
  11.4 0.0 collective-permute-done.1
  11.4 0.5 %collective-permute-start.2 = (bf16[128,512]{1,0:T(8,128)(2,1)S(1)}, bf16[128,512]{1,0:T(8,128)(2,1)S(1)}, u32[]{:S(2)}, u32[]{:S(2)}) collective-permute-start(bf16[128,512]{1,0:T(8,128)(2,1)S(1)} %pad_maximum_fusion.1), channel_id=1, source_target_pairs={{0,4},{4,0},{8,12},{12,8},{16,20},{20,16},{24,28},{28,24},{1,5},{5... | collective-permute-start | bytes 393224 | tf_op jit(solution)/shard_map/ppermute | solution.py:28
  11.9 0.0 copy-done.9
  11.9 0.1 copy.12.w_out_ref
  12.0 2.1 %collective-permute-done.4 = bf16[64,512]{1,0:T(8,128)(2,1)S(1)} collective-permute-done((bf16[64,512]{1,0:T(8,128)(2,1)S(1)}, bf16[64,512]{1,0:T(8,128)(2,1)S(1)}, u32[]{:S(2)}, u32[]{:S(2)}) %collective-permute-start.4) | collective-permute-done | bytes 65568 | tf_op jit(solution)/shard_map/ppermute | solution.py:28
  14.1 0.0 collective-permute-done.2
  14.1 0.0 copy-done.2
  14.1 0.0 copy-done.3
  14.1 0.0 copy-done.4
  14.1 0.0 copy-done.5
  14.1 0.0 copy-done.6
  14.2 0.0 copy-done.7
  14.2 0.6 %shard_map.115 = (f32[512,1024]{1,0:T(8,128)S(1)}, bf16[8,512,128]{2,1,0:T(8,128)(2,1)S(1)}, bf16[128,1024]{1,0:T(8,128)(2,1)S(1)}, bf16[256,1024]{1,0:T(8,128)(...) custom-call(bf16[256,512]{1,0:T(8,128)(2,1)S(1)} %pad_maximum_fusion, ...), custom_call_target="tpu_custom_call" | custom-call | flops 750000000 | bytes 4500000 | tf_op jit(solution)/shard_map/pallas_call | solution.py:296
  14.7 4.1 %shard_map.116 = (f32[128,512]{1,0:T(8,128)S(1)}, bf16[128,512]{1,0:T(8,128)(2,1)S(1)}, f32[64,1024]{1,0:T(8,128)S(1)}) custom-call(bf16[128,512]{1,0:T(8,128)(2,1)S(1)} %pad_maximum_fusion.2.users_ref, f32[512,1024]{1,0:T(8,128)S(1)} %get-tuple-element.18.item_pairs, bf16[128,1024]{1,0:T(8,128)(2,1)S(1)} %get-tuple-element.17.user_hot, ...), custom_call_target="tpu_custom_call" | custom-call | flops 2249999872 | bytes 13500000 | tf_op jit(solution)/shard_map/pallas_call | solution.py:296
  18.8 0.1 collective-permute-start.7
  18.9 1.1 %shard_map.117 = (f32[64,512]{1,0:T(8,128)S(1)}, bf16[64,512]{1,0:T(8,128)(2,1)S(1)}) custom-call(bf16[8,512,128]{2,1,0:T(8,128)(2,1)S(1)} %get-tuple-element.16.item_short, bf16[128,1024]{1,0:T(8,128)(2,1)S(1)} %get-tuple-element.17.user_hot, f32[64,1024]{1,0:T(8,128)S(1)} %get-tuple-element.25.grad_ref), custom_call_target="tpu_custom_call" | custom-call | flops 1000000000 | bytes 6000000 | tf_op jit(solution)/shard_map/pallas_call | solution.py:296
  20.0 1.6 %collective-permute-start.5 = (bf16[64,512]{1,0:T(8,128)(2,1)S(1)}, bf16[64,512]{1,0:T(8,128)(2,1)S(1)}, u32[]{:S(2)}, u32[]{:S(2)}) collective-permute-start(bf16[64,512]{1,0:T(8,128)(2,1)S(1)} %get-tuple-element.27), channel_id=1, source_target_pairs={{0,1},{1,0},{2,3},{3,2},{4,5},{5,4},{6,7},{7,6},{8,9},{9,8},{10,11... | collective-permute-start | bytes 196616 | tf_op jit(solution)/shard_map/ppermute | solution.py:28
  21.7 0.0 collective-permute-done.7
  21.7 1.4 %collective-permute-start.8 = (bf16[64,512]{1,0:T(8,128)(2,1)S(1)}, bf16[64,512]{1,0:T(8,128)(2,1)S(1)}, u32[]{:S(2)}, u32[]{:S(2)}) collective-permute-start(bf16[64,512]{1,0:T(8,128)(2,1)S(1)} %slice.39), channel_id=1, source_target_pairs={{0,20},{4,16},{8,28},{12,24},{16,4},{20,0},{24,12},{28,8},{1,21},{... | collective-permute-start | bytes 196616 | tf_op jit(solution)/shard_map/ppermute | solution.py:28
  23.1 1.4 %collective-permute-done.5 = bf16[64,512]{1,0:T(8,128)(2,1)S(1)} collective-permute-done((bf16[64,512]{1,0:T(8,128)(2,1)S(1)}, bf16[64,512]{1,0:T(8,128)(2,1)S(1)}, u32[]{:S(2)}, u32[]{:S(2)}) %collective-permute-start.5) | collective-permute-done | bytes 65568 | tf_op jit(solution)/shard_map/ppermute | solution.py:28
  24.6 3.1 %collective-permute-start.6 = (bf16[32,512]{1,0:T(8,128)(2,1)S(1)}, bf16[32,512]{1,0:T(8,128)(2,1)S(1)}, u32[]{:S(2)}, u32[]{:S(2)}) collective-permute-start(bf16[32,512]{1,0:T(8,128)(2,1)S(1)} %slice.41), channel_id=1, source_target_pairs={{0,2},{1,3},{2,0},{3,1},{4,6},{5,7},{6,4},{7,5},{8,10},{9,11},{10,... | collective-permute-start | bytes 98312 | tf_op jit(solution)/shard_map/ppermute | solution.py:28
  27.7 0.0 collective-permute-done.8
  27.7 0.1 collective-permute-start.9
  27.8 2.1 %collective-permute-done.6 = bf16[32,512]{1,0:T(8,128)(2,1)S(1)} collective-permute-done((bf16[32,512]{1,0:T(8,128)(2,1)S(1)}, bf16[32,512]{1,0:T(8,128)(2,1)S(1)}, u32[]{:S(2)}, u32[]{:S(2)}) %collective-permute-start.6) | collective-permute-done | bytes 32800 | tf_op jit(solution)/shard_map/ppermute | solution.py:28
  29.9 0.6 %slice_add_fusion.2 = f32[32,512]{1,0:T(8,128)} fusion(f32[64,512]{1,0:T(8,128)S(1)} %convert_add_fusion.1, bf16[32,512]{1,0:T(8,128)(2,1)S(1)} %collective-permute-done.6), kind=kLoop, calls=%fused_computation.10 | loop fusion | flops 32768 | bytes 163840 | tf_op jit(solution)/shard_map/add | solution.py:374
  30.6 0.6 %collective-permute-done.9 = bf16[32,512]{1,0:T(8,128)(2,1)S(1)} collective-permute-done((bf16[32,512]{1,0:T(8,128)(2,1)S(1)}, bf16[32,512]{1,0:T(8,128)(2,1)S(1)}, u32[]{:S(2)}, u32[]{:S(2)}) %collective-permute-start.9) | collective-permute-done | bytes 32800 | tf_op jit(solution)/shard_map/ppermute | solution.py:28
  31.2 0.6 %slice_add_fusion.1 = f32[32,512]{1,0:T(8,128)} fusion(f32[64,512]{1,0:T(8,128)S(1)} %slice_add_fusion, bf16[32,512]{1,0:T(8,128)(2,1)S(1)} %collective-permute-done.9), kind=kLoop, calls=%fused_computation.8 | loop fusion | flops 32768 | bytes 163840 | tf_op jit(solution)/shard_map/add | solution.py:374
  (12 shorter events, 0.1 us)
Async XLA Ops:
  0.6 1.2 %copy-start = (bf16[1024,512]{1,0:T(8,128)(2,1)S(1)}, bf16[1024,512]{1,0:T(8,128)(2,1)}, u32[]{:S(2)}) copy-start(bf16[1024,512]{1,0:T(8,128)(2,1)} %proj_ref.1) | copy-start | bytes 3145732
  0.6 1.2 %copy-start.1 = (bf16[32,1024]{1,0:T(8,128)(2,1)S(1)}, bf16[32,1024]{1,0:T(8,128)(2,1)}, u32[]{:S(2)}) copy-start(bf16[32,1024]{1,0:T(8,128)(2,1)} %text_ref.1) | copy-start | bytes 196612
  1.9 3.0 %copy-start.8 = (bf16[32,512]{1,0:T(8,128)(2,1)S(1)}, bf16[32,512]{1,0:T(8,128)(2,1)}, u32[]{:S(2)}) copy-start(bf16[32,512]{1,0:T(8,128)(2,1)} %param.10) | copy-start | bytes 98308
  1.9 10.0 %copy-start.9 = (f32[128,64]{0,1:T(8,128)S(1)}, f32[128,64]{0,1:T(8,128)}, u32[]{:S(2)}) copy-start(f32[128,64]{0,1:T(8,128)} %param.15) | copy-start | bytes 98308
  1.9 12.2 %copy-start.2 = (f32[64,128]{1,0:T(8,128)S(1)}, f32[64,128]{1,0:T(8,128)}, u32[]{:S(2)}) copy-start(f32[64,128]{1,0:T(8,128)} %w_in_ref.1) | copy-start | bytes 98308
  1.9 12.2 %copy-start.3 = (s32[1024]{0:T(1024)S(1)}, s32[1024]{0:T(1024)}, u32[]{:S(2)}) copy-start(s32[1024]{0:T(1024)} %param.17) | copy-start | bytes 12292
  1.9 12.2 %copy-start.4 = (s32[1024]{0:T(1024)S(1)}, s32[1024]{0:T(1024)}, u32[]{:S(2)}) copy-start(s32[1024]{0:T(1024)} %param.18) | copy-start | bytes 12292
  1.9 12.2 %copy-start.5 = (f32[1024]{0:T(1024)S(1)}, f32[1024]{0:T(1024)}, u32[]{:S(2)}) copy-start(f32[1024]{0:T(1024)} %param.19) | copy-start | bytes 12292
  1.9 12.2 %copy-start.6 = (f32[128]{0:T(128)S(1)}, f32[128]{0:T(128)}, u32[]{:S(2)}) copy-start(f32[128]{0:T(128)} %param.14) | copy-start | bytes 1540
  1.9 12.2 %copy-start.7 = (f32[64]{0:T(128)S(1)}, f32[64]{0:T(128)}, u32[]{:S(2)}) copy-start(f32[64]{0:T(128)} %param.16) | copy-start | bytes 772
  2.4 5.1 %collective-permute-start = (bf16[32,512]{1,0:T(8,128)(2,1)S(1)}, bf16[32,512]{1,0:T(8,128)(2,1)S(1)}, u32[]{:S(2)}, u32[]{:S(2)}) collective-permute-start(bf16[32,512]{1,0:T(8,128)(2,1)S(1)} %shard_map.114), channel_id=1, source_target_pairs={{0,12},{4,8},{8,4},{12,0},{16,28},{20,24},{24,20},{28,16},{1,13},{... | collective-permute-start | bytes 98312 | tf_op jit(solution)/shard_map/ppermute | solution.py:28
  4.9 4.9 %collective-permute-start.3 = (bf16[32,512]{1,0:T(8,128)(2,1)S(1)}, bf16[32,512]{1,0:T(8,128)(2,1)S(1)}, u32[]{:S(2)}, u32[]{:S(2)}) collective-permute-start(bf16[32,512]{1,0:T(8,128)(2,1)S(1)} %copy-done.8), channel_id=1, source_target_pairs={{0,2},{1,3},{2,0},{3,1},{4,6},{5,7},{6,4},{7,5},{8,10},{9,11},{10,... | collective-permute-start | bytes 98312 | tf_op jit(solution)/shard_map/ppermute | solution.py:28
  7.5 3.9 %collective-permute-start.1 = (bf16[64,512]{1,0:T(8,128)(2,1)S(1)}, bf16[64,512]{1,0:T(8,128)(2,1)S(1)}, u32[]{:S(2)}, u32[]{:S(2)}) collective-permute-start(bf16[64,512]{1,0:T(8,128)(2,1)S(1)} %pad_maximum_fusion.3), channel_id=1, source_target_pairs={{0,20},{4,16},{8,28},{12,24},{16,4},{20,0},{24,12},{28,8},{1,21},{... | collective-permute-start | bytes 196616 | tf_op jit(solution)/shard_map/ppermute | solution.py:28
  9.8 4.3 %collective-permute-start.4 = (bf16[64,512]{1,0:T(8,128)(2,1)S(1)}, bf16[64,512]{1,0:T(8,128)(2,1)S(1)}, u32[]{:S(2)}, u32[]{:S(2)}) collective-permute-start(bf16[64,512]{1,0:T(8,128)(2,1)S(1)} %pad_maximum_fusion.4), channel_id=1, source_target_pairs={{0,1},{1,0},{2,3},{3,2},{4,5},{5,4},{6,7},{7,6},{8,9},{9,8},{10,11... | collective-permute-start | bytes 196616 | tf_op jit(solution)/shard_map/ppermute | solution.py:28
  11.4 2.7 %collective-permute-start.2 = (bf16[128,512]{1,0:T(8,128)(2,1)S(1)}, bf16[128,512]{1,0:T(8,128)(2,1)S(1)}, u32[]{:S(2)}, u32[]{:S(2)}) collective-permute-start(bf16[128,512]{1,0:T(8,128)(2,1)S(1)} %pad_maximum_fusion.1), channel_id=1, source_target_pairs={{0,4},{4,0},{8,12},{12,8},{16,20},{20,16},{24,28},{28,24},{1,5},{5... | collective-permute-start | bytes 393224 | tf_op jit(solution)/shard_map/ppermute | solution.py:28
  18.8 2.9 %collective-permute-start.7 = (bf16[128,512]{1,0:T(8,128)(2,1)S(1)}, bf16[128,512]{1,0:T(8,128)(2,1)S(1)}, u32[]{:S(2)}, u32[]{:S(2)}) collective-permute-start(bf16[128,512]{1,0:T(8,128)(2,1)S(1)} %get-tuple-element.29), channel_id=1, source_target_pairs={{0,4},{4,0},{8,12},{12,8},{16,20},{20,16},{24,28},{28,24},{1,5},{5... | collective-permute-start | bytes 393224 | tf_op jit(solution)/shard_map/ppermute | solution.py:28
  20.0 4.6 %collective-permute-start.5 = (bf16[64,512]{1,0:T(8,128)(2,1)S(1)}, bf16[64,512]{1,0:T(8,128)(2,1)S(1)}, u32[]{:S(2)}, u32[]{:S(2)}) collective-permute-start(bf16[64,512]{1,0:T(8,128)(2,1)S(1)} %get-tuple-element.27), channel_id=1, source_target_pairs={{0,1},{1,0},{2,3},{3,2},{4,5},{5,4},{6,7},{7,6},{8,9},{9,8},{10,11... | collective-permute-start | bytes 196616 | tf_op jit(solution)/shard_map/ppermute | solution.py:28
  21.7 6.0 %collective-permute-start.8 = (bf16[64,512]{1,0:T(8,128)(2,1)S(1)}, bf16[64,512]{1,0:T(8,128)(2,1)S(1)}, u32[]{:S(2)}, u32[]{:S(2)}) collective-permute-start(bf16[64,512]{1,0:T(8,128)(2,1)S(1)} %slice.39), channel_id=1, source_target_pairs={{0,20},{4,16},{8,28},{12,24},{16,4},{20,0},{24,12},{28,8},{1,21},{... | collective-permute-start | bytes 196616 | tf_op jit(solution)/shard_map/ppermute | solution.py:28
  24.6 5.3 %collective-permute-start.6 = (bf16[32,512]{1,0:T(8,128)(2,1)S(1)}, bf16[32,512]{1,0:T(8,128)(2,1)S(1)}, u32[]{:S(2)}, u32[]{:S(2)}) collective-permute-start(bf16[32,512]{1,0:T(8,128)(2,1)S(1)} %slice.41), channel_id=1, source_target_pairs={{0,2},{1,3},{2,0},{3,1},{4,6},{5,7},{6,4},{7,5},{8,10},{9,11},{10,... | collective-permute-start | bytes 98312 | tf_op jit(solution)/shard_map/ppermute | solution.py:28
  27.7 3.5 %collective-permute-start.9 = (bf16[32,512]{1,0:T(8,128)(2,1)S(1)}, bf16[32,512]{1,0:T(8,128)(2,1)S(1)}, u32[]{:S(2)}, u32[]{:S(2)}) collective-permute-start(bf16[32,512]{1,0:T(8,128)(2,1)S(1)} %slice.40), channel_id=1, source_target_pairs={{0,12},{4,8},{8,4},{12,0},{16,28},{20,24},{24,20},{28,16},{1,13},{... | collective-permute-start | bytes 98312 | tf_op jit(solution)/shard_map/ppermute | solution.py:28

commit v6 on v5

--- a/solution.py
+++ b/solution.py
@@ -195,11 +195,8 @@
                 terms[at : at + 16, span] = parts[0]
 
 
-def collect(hot, terms, keep_ref, send_ref):
-    total = lax.dot_general(hot[...], terms[...], (((1,), (1,)), ((), ())), preferred_element_type=F32)
-    half = total.shape[0] // 2
-    keep_ref[...] = total[:half]
-    send_ref[...] = total[half:].astype(BF16)
+def collect(hot, terms):
+    return lax.dot_general(hot, terms, (((1,), (1,)), ((), ())), preferred_element_type=F32)
 
 
 def pair_kernel(
@@ -213,12 +210,11 @@
     w_in_bwd,
     w_out_bwd,
     target,
-    item_keep_ref,
     item_send_ref,
     grad_ref,
+    item_terms,
     user_pairs,
     logits_ref,
-    item_terms,
 ):
     pairs = user_hot.shape[1]
     blocks = pairs // WIDE
@@ -279,13 +275,21 @@
         for at, stage in enumerate(stages):
             if 0 <= step - at < blocks:
                 stage(step - at)
-    collect(item_hot, item_terms, item_keep_ref, item_send_ref)
-
-
-def user_kernel(item_short, user_hot, grad_ref, user_keep_ref, user_send_ref, user_terms):
+    half = item_hot.shape[0] // 2
+    item_send_ref[...] = collect(item_hot[half:, :], item_terms[...]).astype(BF16)
+
+
+def user_kernel(
+    item_short, user_hot, grad_ref, item_hot, item_terms, user_keep_ref, user_send_ref, item_keep_ref, user_terms
+):
+    half = item_hot.shape[0] // 2
+    item_keep_ref[...] = collect(item_hot[:half, :], item_terms[...])
     for tile in range(user_hot.shape[1] // TILE):
         short_gradients(grad_ref, item_short, user_terms, tile, lambda c, k: c * COMPS + k)
-    collect(user_hot, user_terms, user_keep_ref, user_send_ref)
+    total = collect(user_hot[...], user_terms[...])
+    half = total.shape[0] // 2
+    user_keep_ref[...] = total[:half]
+    user_send_ref[...] = total[half:].astype(BF16)
 
 
 def shape(rows, columns, kind):
@@ -350,19 +354,23 @@
         12,
         1.5,
     )
-    item_keep, item_send, grads = call(
+    item_send, grads, item_terms = call(
         functools.partial(pair_kernel, loss_scale),
-        [shape(item_rows // 2, width, F32), shape(item_rows // 2, width, BF16), shape(gates, pairs, F32)],
-        [shape(width, pairs, F32), shape(gates, pairs, F32), shape(width, pairs, BF16)],
+        [shape(item_rows // 2, width, BF16), shape(gates, pairs, F32), shape(width, pairs, BF16)],
+        [shape(width, pairs, F32), shape(gates, pairs, F32)],
         [users, item_pairs, user_hot, item_hot, w_in_fwd, w_out_fwd, w_in_bwd, w_out_bwd, target],
         20,
         4.5,
     )
-    user_keep, user_send = call(
+    user_keep, user_send, item_keep = call(
         user_kernel,
-        [shape(user_rows // 2, width, F32), shape(user_rows // 2, width, BF16)],
+        [
+            shape(user_rows // 2, width, F32),
+            shape(user_rows // 2, width, BF16),
+            shape(item_rows // 2, width, F32),
+        ],
         [shape(width, pairs, BF16)],
-        [item_short, user_hot, grads],
+        [item_short, user_hot, grads, item_hot, item_terms],
         12,
         2.0,
     )

time: 32 us -> 32.3 us (level)
  no operation moved by 1% of the time
where the time goes in v6:
time: 32.3 us; the launch traced here: 32.1 us
  starting transfers between devices  14.9 us (46%)
  waiting for transfers between devices  7.02 us (22%)
  Pallas kernels  6.56 us (20%)
  other arithmetic  1.38 us (4%)
  local copies, waits for them, and re-layouts  1.36 us (4%)
  between operations  0.86 us (3%)
    ppermute x10, starting transfers between devices, exchange(): return lax.ppermute(value, axis, [(i, i ^ step) for i in range(size)])  14.9 us
    ppermute x10, waiting for transfers between devices, exchange(): return lax.ppermute(value, axis, [(i, i ^ step) for i in range(size)])  7.02 us
    pallas_call x5, Pallas kernels, call(): pl.pallas_call(kernel, out_shape=outputs, in_specs=[VMEM] * len(arguments...  6.56 us
    unnamed x21, local copies, waits for them, and re-layouts  1.33 us
    add x5, other arithmetic, scatter(): total = keep + got.astype(F32)  1.33 us
  transfers between devices with their start and end apart: 10, of which 5 were waited for; matrix products, arithmetic and copies ran while one was open for 3% of the time, Pallas kernels for 4%

profile of v6, /device:TPU:0, one launch (start us, length us, event | category | flops | bytes accessed | tf_op | source)
XLA Modules:
  0.0 32.1 jit_solution(14431955379367196499)
XLA Ops:
  0.6 0.0 copy-start
  0.6 0.0 copy-start.1
  0.7 1.2 %copy-done = bf16[1024,512]{1,0:T(8,128)(2,1)S(1)} copy-done((bf16[1024,512]{1,0:T(8,128)(2,1)S(1)}, bf16[1024,512]{1,0:T(8,128)(2,1)}, u32[]{:S(2)}) %copy-start) | copy-done | bytes 1048600
  1.9 0.0 copy-done.1
  1.9 0.0 copy-start.8
  1.9 0.0 copy-start.9
  1.9 0.0 copy-start.2
  1.9 0.0 copy-start.3
  1.9 0.0 copy-start.4
  1.9 0.0 copy-start.5
  1.9 0.0 copy-start.6
  1.9 0.0 copy-start.7
  1.9 0.5 %shard_map.114 = bf16[32,512]{1,0:T(8,128)(2,1)S(1)} custom-call(bf16[32,1024]{1,0:T(8,128)(2,1)S(1)} %copy-done.1, bf16[1024,512]{1,0:T(8,128)(2,1)S(1)} %copy-done, f32[8,128]{1,0:T(8,128)S(1)} %shard_map.113.ready_ref), custom_call_target="tpu_custom_call" | custom-call | flops 1000000000 | bytes 6000000 | tf_op jit(solution)/shard_map/pallas_call | solution.py:300
  2.4 2.5 %collective-permute-start = (bf16[32,512]{1,0:T(8,128)(2,1)S(1)}, bf16[32,512]{1,0:T(8,128)(2,1)S(1)}, u32[]{:S(2)}, u32[]{:S(2)}) collective-permute-start(bf16[32,512]{1,0:T(8,128)(2,1)S(1)} %shard_map.114), channel_id=1, source_target_pairs={{0,12},{4,8},{8,4},{12,0},{16,28},{20,24},{24,20},{28,16},{1,13},{... | collective-permute-start | bytes 98312 | tf_op jit(solution)/shard_map/ppermute | solution.py:28
  4.9 0.0 copy-done.8
  4.9 2.6 %collective-permute-start.3 = (bf16[32,512]{1,0:T(8,128)(2,1)S(1)}, bf16[32,512]{1,0:T(8,128)(2,1)S(1)}, u32[]{:S(2)}, u32[]{:S(2)}) collective-permute-start(bf16[32,512]{1,0:T(8,128)(2,1)S(1)} %copy-done.8), channel_id=1, source_target_pairs={{0,2},{1,3},{2,0},{3,1},{4,6},{5,7},{6,4},{7,5},{8,10},{9,11},{10,... | collective-permute-start | bytes 98312 | tf_op jit(solution)/shard_map/ppermute | solution.py:28
  7.5 0.0 collective-permute-done
  7.5 1.6 %collective-permute-start.1 = (bf16[64,512]{1,0:T(8,128)(2,1)S(1)}, bf16[64,512]{1,0:T(8,128)(2,1)S(1)}, u32[]{:S(2)}, u32[]{:S(2)}) collective-permute-start(bf16[64,512]{1,0:T(8,128)(2,1)S(1)} %pad_maximum_fusion.3), channel_id=1, source_target_pairs={{0,20},{4,16},{8,28},{12,24},{16,4},{20,0},{24,12},{28,8},{1,21},{... | collective-permute-start | bytes 196616 | tf_op jit(solution)/shard_map/ppermute | solution.py:28
  9.1 0.7 %collective-permute-done.3 = bf16[32,512]{1,0:T(8,128)(2,1)S(1)} collective-permute-done((bf16[32,512]{1,0:T(8,128)(2,1)S(1)}, bf16[32,512]{1,0:T(8,128)(2,1)S(1)}, u32[]{:S(2)}, u32[]{:S(2)}) %collective-permute-start.3) | collective-permute-done | bytes 32800 | tf_op jit(solution)/shard_map/ppermute | solution.py:28
  9.8 1.6 %collective-permute-start.4 = (bf16[64,512]{1,0:T(8,128)(2,1)S(1)}, bf16[64,512]{1,0:T(8,128)(2,1)S(1)}, u32[]{:S(2)}, u32[]{:S(2)}) collective-permute-start(bf16[64,512]{1,0:T(8,128)(2,1)S(1)} %pad_maximum_fusion.4), channel_id=1, source_target_pairs={{0,1},{1,0},{2,3},{3,2},{4,5},{5,4},{6,7},{7,6},{8,9},{9,8},{10,11... | collective-permute-start | bytes 196616 | tf_op jit(solution)/shard_map/ppermute | solution.py:28
  11.4 0.0 collective-permute-done.1
  11.4 0.5 %collective-permute-start.2 = (bf16[128,512]{1,0:T(8,128)(2,1)S(1)}, bf16[128,512]{1,0:T(8,128)(2,1)S(1)}, u32[]{:S(2)}, u32[]{:S(2)}) collective-permute-start(bf16[128,512]{1,0:T(8,128)(2,1)S(1)} %pad_maximum_fusion.1), channel_id=1, source_target_pairs={{0,4},{4,0},{8,12},{12,8},{16,20},{20,16},{24,28},{28,24},{1,5},{5... | collective-permute-start | bytes 393224 | tf_op jit(solution)/shard_map/ppermute | solution.py:28
  11.9 0.0 copy-done.9
  11.9 0.1 copy.12.w_out_ref
  12.0 2.1 %collective-permute-done.4 = bf16[64,512]{1,0:T(8,128)(2,1)S(1)} collective-permute-done((bf16[64,512]{1,0:T(8,128)(2,1)S(1)}, bf16[64,512]{1,0:T(8,128)(2,1)S(1)}, u32[]{:S(2)}, u32[]{:S(2)}) %collective-permute-start.4) | collective-permute-done | bytes 65568 | tf_op jit(solution)/shard_map/ppermute | solution.py:28
  14.1 0.0 collective-permute-done.2
  14.1 0.0 copy-done.2
  14.1 0.0 copy-done.3
  14.1 0.0 copy-done.4
  14.1 0.0 copy-done.5
  14.1 0.0 copy-done.6
  14.2 0.0 copy-done.7
  14.2 0.6 %shard_map.115 = (f32[512,1024]{1,0:T(8,128)S(1)}, bf16[8,512,128]{2,1,0:T(8,128)(2,1)S(1)}, bf16[128,1024]{1,0:T(8,128)(2,1)S(1)}, bf16[256,1024]{1,0:T(8,128)(...) custom-call(bf16[256,512]{1,0:T(8,128)(2,1)S(1)} %pad_maximum_fusion, ...), custom_call_target="tpu_custom_call" | custom-call | flops 750000000 | bytes 4500000 | tf_op jit(solution)/shard_map/pallas_call | solution.py:300
  14.7 4.1 %shard_map.116 = (bf16[128,512]{1,0:T(8,128)(2,1)S(1)}, f32[64,1024]{1,0:T(8,128)S(1)}, bf16[512,1024]{1,0:T(8,128)(2,1)S(1)}) custom-call(bf16[128,512]{1,0:T(8,128)(2,1)S(1)} %pad_maximum_fusion.2.users_ref, f32[512,1024]{1,0:T(8,128)S(1)} %get-tuple-element.19.item_pairs, bf16[128,1024]{1,0:T(8,128)(2,1)S(1)} %get-tuple-element.18.user_hot, ...), custom_call_target="tpu_custom_call" | custom-call | flops 2249999872 | bytes 13500000 | tf_op jit(solution)/shard_map/pallas_call | solution.py:300
  18.8 0.1 collective-permute-start.7
  18.9 1.4 %shard_map.117 = (f32[64,512]{1,0:T(8,128)S(1)}, bf16[64,512]{1,0:T(8,128)(2,1)S(1)}, f32[128,512]{1,0:T(8,128)S(1)}) custom-call(bf16[8,512,128]{2,1,0:T(8,128)(2,1)S(1)} %get-tuple-element.17.item_short, bf16[128,1024]{1,0:T(8,128)(2,1)S(1)} %get-tuple-element.18.user_hot, f32[64,1024]{1,0:T(8,128)S(1)} %get-tuple-element.26.grad_ref, ...), custom_call_target="tpu_custom_call" | custom-call | flops 1000000000 | bytes 6000000 | tf_op jit(solution)/shard_map/pallas_call | solution.py:300
  20.3 1.6 %collective-permute-start.5 = (bf16[64,512]{1,0:T(8,128)(2,1)S(1)}, bf16[64,512]{1,0:T(8,128)(2,1)S(1)}, u32[]{:S(2)}, u32[]{:S(2)}) collective-permute-start(bf16[64,512]{1,0:T(8,128)(2,1)S(1)} %get-tuple-element.29), channel_id=1, source_target_pairs={{0,1},{1,0},{2,3},{3,2},{4,5},{5,4},{6,7},{7,6},{8,9},{9,8},{10,11... | collective-permute-start | bytes 196616 | tf_op jit(solution)/shard_map/ppermute | solution.py:28
  22.0 0.0 collective-permute-done.7
  22.0 1.4 %collective-permute-start.8 = (bf16[64,512]{1,0:T(8,128)(2,1)S(1)}, bf16[64,512]{1,0:T(8,128)(2,1)S(1)}, u32[]{:S(2)}, u32[]{:S(2)}) collective-permute-start(bf16[64,512]{1,0:T(8,128)(2,1)S(1)} %slice.39), channel_id=1, source_target_pairs={{0,20},{4,16},{8,28},{12,24},{16,4},{20,0},{24,12},{28,8},{1,21},{... | collective-permute-start | bytes 196616 | tf_op jit(solution)/shard_map/ppermute | solution.py:28
  23.4 1.5 %collective-permute-done.5 = bf16[64,512]{1,0:T(8,128)(2,1)S(1)} collective-permute-done((bf16[64,512]{1,0:T(8,128)(2,1)S(1)}, bf16[64,512]{1,0:T(8,128)(2,1)S(1)}, u32[]{:S(2)}, u32[]{:S(2)}) %collective-permute-start.5) | collective-permute-done | bytes 65568 | tf_op jit(solution)/shard_map/ppermute | solution.py:28
  24.9 3.1 %collective-permute-start.6 = (bf16[32,512]{1,0:T(8,128)(2,1)S(1)}, bf16[32,512]{1,0:T(8,128)(2,1)S(1)}, u32[]{:S(2)}, u32[]{:S(2)}) collective-permute-start(bf16[32,512]{1,0:T(8,128)(2,1)S(1)} %slice.41), channel_id=1, source_target_pairs={{0,2},{1,3},{2,0},{3,1},{4,6},{5,7},{6,4},{7,5},{8,10},{9,11},{10,... | collective-permute-start | bytes 98312 | tf_op jit(solution)/shard_map/ppermute | solution.py:28
  28.0 0.0 collective-permute-done.8
  28.0 0.1 collective-permute-start.9
  28.1 2.1 %collective-permute-done.6 = bf16[32,512]{1,0:T(8,128)(2,1)S(1)} collective-permute-done((bf16[32,512]{1,0:T(8,128)(2,1)S(1)}, bf16[32,512]{1,0:T(8,128)(2,1)S(1)}, u32[]{:S(2)}, u32[]{:S(2)}) %collective-permute-start.6) | collective-permute-done | bytes 32800 | tf_op jit(solution)/shard_map/ppermute | solution.py:28
  30.2 0.6 %slice_add_fusion.2 = f32[32,512]{1,0:T(8,128)} fusion(f32[64,512]{1,0:T(8,128)S(1)} %convert_add_fusion.1, bf16[32,512]{1,0:T(8,128)(2,1)S(1)} %collective-permute-done.6), kind=kLoop, calls=%fused_computation.10 | loop fusion | flops 32768 | bytes 163840 | tf_op jit(solution)/shard_map/add | solution.py:382
  30.9 0.6 %collective-permute-done.9 = bf16[32,512]{1,0:T(8,128)(2,1)S(1)} collective-permute-done((bf16[32,512]{1,0:T(8,128)(2,1)S(1)}, bf16[32,512]{1,0:T(8,128)(2,1)S(1)}, u32[]{:S(2)}, u32[]{:S(2)}) %collective-permute-start.9) | collective-permute-done | bytes 32800 | tf_op jit(solution)/shard_map/ppermute | solution.py:28
  31.5 0.6 %slice_add_fusion.1 = f32[32,512]{1,0:T(8,128)} fusion(f32[64,512]{1,0:T(8,128)S(1)} %slice_add_fusion, bf16[32,512]{1,0:T(8,128)(2,1)S(1)} %collective-permute-done.9), kind=kLoop, calls=%fused_computation.8 | loop fusion | flops 32768 | bytes 163840 | tf_op jit(solution)/shard_map/add | solution.py:382
  (12 shorter events, 0.1 us)
Async XLA Ops:
  0.6 1.2 %copy-start = (bf16[1024,512]{1,0:T(8,128)(2,1)S(1)}, bf16[1024,512]{1,0:T(8,128)(2,1)}, u32[]{:S(2)}) copy-start(bf16[1024,512]{1,0:T(8,128)(2,1)} %proj_ref.1) | copy-start | bytes 3145732
  0.6 1.2 %copy-start.1 = (bf16[32,1024]{1,0:T(8,128)(2,1)S(1)}, bf16[32,1024]{1,0:T(8,128)(2,1)}, u32[]{:S(2)}) copy-start(bf16[32,1024]{1,0:T(8,128)(2,1)} %text_ref.1) | copy-start | bytes 196612
  1.9 3.0 %copy-start.8 = (bf16[32,512]{1,0:T(8,128)(2,1)S(1)}, bf16[32,512]{1,0:T(8,128)(2,1)}, u32[]{:S(2)}) copy-start(bf16[32,512]{1,0:T(8,128)(2,1)} %param.10) | copy-start | bytes 98308
  1.9 10.0 %copy-start.9 = (f32[128,64]{0,1:T(8,128)S(1)}, f32[128,64]{0,1:T(8,128)}, u32[]{:S(2)}) copy-start(f32[128,64]{0,1:T(8,128)} %param.15) | copy-start | bytes 98308
  1.9 12.2 %copy-start.2 = (f32[64,128]{1,0:T(8,128)S(1)}, f32[64,128]{1,0:T(8,128)}, u32[]{:S(2)}) copy-start(f32[64,128]{1,0:T(8,128)} %w_in_ref.1) | copy-start | bytes 98308
  1.9 12.2 %copy-start.3 = (s32[1024]{0:T(1024)S(1)}, s32[1024]{0:T(1024)}, u32[]{:S(2)}) copy-start(s32[1024]{0:T(1024)} %param.17) | copy-start | bytes 12292
  1.9 12.2 %copy-start.4 = (s32[1024]{0:T(1024)S(1)}, s32[1024]{0:T(1024)}, u32[]{:S(2)}) copy-start(s32[1024]{0:T(1024)} %param.18) | copy-start | bytes 12292
  1.9 12.2 %copy-start.5 = (f32[1024]{0:T(1024)S(1)}, f32[1024]{0:T(1024)}, u32[]{:S(2)}) copy-start(f32[1024]{0:T(1024)} %param.19) | copy-start | bytes 12292
  1.9 12.2 %copy-start.6 = (f32[128]{0:T(128)S(1)}, f32[128]{0:T(128)}, u32[]{:S(2)}) copy-start(f32[128]{0:T(128)} %param.14) | copy-start | bytes 1540
  1.9 12.2 %copy-start.7 = (f32[64]{0:T(128)S(1)}, f32[64]{0:T(128)}, u32[]{:S(2)}) copy-start(f32[64]{0:T(128)} %param.16) | copy-start | bytes 772
  2.4 5.1 %collective-permute-start = (bf16[32,512]{1,0:T(8,128)(2,1)S(1)}, bf16[32,512]{1,0:T(8,128)(2,1)S(1)}, u32[]{:S(2)}, u32[]{:S(2)}) collective-permute-start(bf16[32,512]{1,0:T(8,128)(2,1)S(1)} %shard_map.114), channel_id=1, source_target_pairs={{0,12},{4,8},{8,4},{12,0},{16,28},{20,24},{24,20},{28,16},{1,13},{... | collective-permute-start | bytes 98312 | tf_op jit(solution)/shard_map/ppermute | solution.py:28
  4.9 4.9 %collective-permute-start.3 = (bf16[32,512]{1,0:T(8,128)(2,1)S(1)}, bf16[32,512]{1,0:T(8,128)(2,1)S(1)}, u32[]{:S(2)}, u32[]{:S(2)}) collective-permute-start(bf16[32,512]{1,0:T(8,128)(2,1)S(1)} %copy-done.8), channel_id=1, source_target_pairs={{0,2},{1,3},{2,0},{3,1},{4,6},{5,7},{6,4},{7,5},{8,10},{9,11},{10,... | collective-permute-start | bytes 98312 | tf_op jit(solution)/shard_map/ppermute | solution.py:28
  7.5 3.9 %collective-permute-start.1 = (bf16[64,512]{1,0:T(8,128)(2,1)S(1)}, bf16[64,512]{1,0:T(8,128)(2,1)S(1)}, u32[]{:S(2)}, u32[]{:S(2)}) collective-permute-start(bf16[64,512]{1,0:T(8,128)(2,1)S(1)} %pad_maximum_fusion.3), channel_id=1, source_target_pairs={{0,20},{4,16},{8,28},{12,24},{16,4},{20,0},{24,12},{28,8},{1,21},{... | collective-permute-start | bytes 196616 | tf_op jit(solution)/shard_map/ppermute | solution.py:28
  9.8 4.3 %collective-permute-start.4 = (bf16[64,512]{1,0:T(8,128)(2,1)S(1)}, bf16[64,512]{1,0:T(8,128)(2,1)S(1)}, u32[]{:S(2)}, u32[]{:S(2)}) collective-permute-start(bf16[64,512]{1,0:T(8,128)(2,1)S(1)} %pad_maximum_fusion.4), channel_id=1, source_target_pairs={{0,1},{1,0},{2,3},{3,2},{4,5},{5,4},{6,7},{7,6},{8,9},{9,8},{10,11... | collective-permute-start | bytes 196616 | tf_op jit(solution)/shard_map/ppermute | solution.py:28
  11.4 2.7 %collective-permute-start.2 = (bf16[128,512]{1,0:T(8,128)(2,1)S(1)}, bf16[128,512]{1,0:T(8,128)(2,1)S(1)}, u32[]{:S(2)}, u32[]{:S(2)}) collective-permute-start(bf16[128,512]{1,0:T(8,128)(2,1)S(1)} %pad_maximum_fusion.1), channel_id=1, source_target_pairs={{0,4},{4,0},{8,12},{12,8},{16,20},{20,16},{24,28},{28,24},{1,5},{5... | collective-permute-start | bytes 393224 | tf_op jit(solution)/shard_map/ppermute | solution.py:28
  18.8 3.2 %collective-permute-start.7 = (bf16[128,512]{1,0:T(8,128)(2,1)S(1)}, bf16[128,512]{1,0:T(8,128)(2,1)S(1)}, u32[]{:S(2)}, u32[]{:S(2)}) collective-permute-start(bf16[128,512]{1,0:T(8,128)(2,1)S(1)} %get-tuple-element.31), channel_id=1, source_target_pairs={{0,4},{4,0},{8,12},{12,8},{16,20},{20,16},{24,28},{28,24},{1,5},{5... | collective-permute-start | bytes 393224 | tf_op jit(solution)/shard_map/ppermute | solution.py:28
  20.3 4.6 %collective-permute-start.5 = (bf16[64,512]{1,0:T(8,128)(2,1)S(1)}, bf16[64,512]{1,0:T(8,128)(2,1)S(1)}, u32[]{:S(2)}, u32[]{:S(2)}) collective-permute-start(bf16[64,512]{1,0:T(8,128)(2,1)S(1)} %get-tuple-element.29), channel_id=1, source_target_pairs={{0,1},{1,0},{2,3},{3,2},{4,5},{5,4},{6,7},{7,6},{8,9},{9,8},{10,11... | collective-permute-start | bytes 196616 | tf_op jit(solution)/shard_map/ppermute | solution.py:28
  22.0 6.0 %collective-permute-start.8 = (bf16[64,512]{1,0:T(8,128)(2,1)S(1)}, bf16[64,512]{1,0:T(8,128)(2,1)S(1)}, u32[]{:S(2)}, u32[]{:S(2)}) collective-permute-start(bf16[64,512]{1,0:T(8,128)(2,1)S(1)} %slice.39), channel_id=1, source_target_pairs={{0,20},{4,16},{8,28},{12,24},{16,4},{20,0},{24,12},{28,8},{1,21},{... | collective-permute-start | bytes 196616 | tf_op jit(solution)/shard_map/ppermute | solution.py:28
  24.9 5.3 %collective-permute-start.6 = (bf16[32,512]{1,0:T(8,128)(2,1)S(1)}, bf16[32,512]{1,0:T(8,128)(2,1)S(1)}, u32[]{:S(2)}, u32[]{:S(2)}) collective-permute-start(bf16[32,512]{1,0:T(8,128)(2,1)S(1)} %slice.41), channel_id=1, source_target_pairs={{0,2},{1,3},{2,0},{3,1},{4,6},{5,7},{6,4},{7,5},{8,10},{9,11},{10,... | collective-permute-start | bytes 98312 | tf_op jit(solution)/shard_map/ppermute | solution.py:28
  28.0 3.5 %collective-permute-start.9 = (bf16[32,512]{1,0:T(8,128)(2,1)S(1)}, bf16[32,512]{1,0:T(8,128)(2,1)S(1)}, u32[]{:S(2)}, u32[]{:S(2)}) collective-permute-start(bf16[32,512]{1,0:T(8,128)(2,1)S(1)} %slice.40), channel_id=1, source_target_pairs={{0,12},{4,8},{8,4},{12,0},{16,28},{20,24},{24,20},{28,16},{1,13},{... | collective-permute-start | bytes 98312 | tf_op jit(solution)/shard_map/ppermute | solution.py:28
